TPU v7x, 1024 devices: a whole 8x8x8 slice. The times are simulated.
1024 devices in a mesh: gx: 128 (over y, x, z_lo), sa: 8 (over z_hi, core).
Axes of the slice: x: 8, y: 8, z: 8 (z_hi: 4, z_lo: 2; z = z_hi * 2 + z_lo), core: 2. Of those that a mesh axis runs over, the one named last changes fastest.
Arguments:
- field_in: bfloat16 [8, 128, 256, 1024], P('sa', 'gx'), may hold values from -6 to 6
- cotangent: bfloat16 [8, 128, 256, 1024], P('sa', 'gx'), may hold values from -6 to 6
- mode_weights: bfloat16 [32, 512, 64, 128], P(None, 'gx'), may hold values from -4 to 4
- point_weights: bfloat16 [64, 64], replicated, may hold values from -0.75 to 0.75
Outputs:
- field_out: bfloat16 [8, 128, 256, 1024], P('sa', 'gx')
- field_grad: bfloat16 [8, 128, 256, 1024], P('sa', 'gx')
- weight_grad: float32 [32, 512, 64, 128], P('sa', 'gx')
All inputs are finite; a program needn't handle non-finite values.
Results may differ from a plain program's by a relative error of at most 0.018.
Values may be sent and summed in bfloat16 or wider, within the bound.
No kernel may reach another device: no remote copies, remote signals or barrier semaphores. Data moves between devices by JAX's collectives and lax.ppermute only.
A program may use at most 32 MiB of HBM per device.

v0:
```python
import math

import jax
import jax.numpy as jnp
from jax import lax
from jax.sharding import PartitionSpec as P

KY = 32
KZ = 16


HIGHEST_PREC = lax.Precision.HIGHEST
GELU_COEF = 0.044715


def partner(block, axis, distance):
    count = lax.axis_size(axis)
    route = []
    for low in range(count):
        high = low | 1 << distance
        if high != low and high < count:
            route += [(low, high), (high, low)]
    return lax.ppermute(block, axis, route)


def angles(freq_count, grid_count):
    frequency = jnp.arange(freq_count, dtype=jnp.int32) - freq_count // 2
    places = jnp.arange(grid_count, dtype=jnp.int32)
    turn_index = jnp.mod(frequency[:, None] * places[None, :], grid_count)
    return turn_index.astype(jnp.float32) * (2.0 * math.pi / grid_count)


def gelu_parts(pre_act):
    root_const = math.sqrt(2.0 / math.pi)
    inner_arg = root_const * (pre_act + GELU_COEF * pre_act * pre_act * pre_act)
    tangent = jnp.tanh(inner_arg)
    activated = 0.5 * pre_act * (1.0 + tangent)
    gelu_slope = 0.5 * (1.0 + tangent) + 0.5 * pre_act * (1.0 - tangent * tangent) * root_const * (
        1.0 + 3.0 * GELU_COEF * pre_act * pre_act
    )
    return (activated, gelu_slope)


def along_z_forward(data_in, table_z):
    return jnp.einsum("pyzc,kz->pykc", data_in, table_z, precision=HIGHEST_PREC)


def along_z_inverse(data_in, table_z):
    return jnp.einsum("pykc,kz->pyzc", data_in, table_z, precision=HIGHEST_PREC)


def forward_yz(local_field, channels):
    planes, y_count, last_width = local_field.shape
    z_count = last_width // channels
    theta_y = angles(KY, y_count)
    table_y = jnp.concatenate([jnp.cos(theta_y), -jnp.sin(theta_y)], 0).astype(jnp.bfloat16)
    first_pass = jnp.einsum("fy,pyq->pfq", table_y, local_field, preferred_element_type=jnp.float32)
    first_pass = first_pass.reshape(planes, 2, KY, z_count, channels)
    theta_z = angles(KZ, z_count)
    cos_z = jnp.cos(theta_z)
    sin_z = jnp.sin(theta_z)
    real_in = first_pass[:, 0]
    imag_in = first_pass[:, 1]
    real_out = along_z_forward(real_in, cos_z) + along_z_forward(imag_in, sin_z)
    imag_out = along_z_forward(imag_in, cos_z) - along_z_forward(real_in, sin_z)
    mode_data = jnp.concatenate([real_out, imag_out], -1)
    return mode_data.reshape(planes, KY * KZ, 2 * channels).astype(jnp.bfloat16)


def forward_x(mode_data, kx_count, norm_scale):
    x_length, mode_block, pair_width = mode_data.shape
    channels = pair_width // 2
    theta_x = angles(kx_count, x_length)
    flat_data = mode_data.reshape(x_length, mode_block * pair_width)
    cos_part = jnp.dot(
        jnp.cos(theta_x).astype(jnp.bfloat16), flat_data, preferred_element_type=jnp.float32
    ).reshape(kx_count, mode_block, pair_width)
    sin_part = jnp.dot(
        jnp.sin(theta_x).astype(jnp.bfloat16), flat_data, preferred_element_type=jnp.float32
    ).reshape(kx_count, mode_block, pair_width)
    real_out = cos_part[..., :channels] + sin_part[..., channels:]
    imag_out = cos_part[..., channels:] - sin_part[..., :channels]
    return (jnp.concatenate([real_out, imag_out], -1) * norm_scale).astype(jnp.bfloat16)


def inverse_x(mixed_modes, x_length):
    kx_count, mode_block, pair_width = mixed_modes.shape
    channels = pair_width // 2
    theta_x = angles(kx_count, x_length).T
    flat_data = mixed_modes.reshape(kx_count, mode_block * pair_width)
    cos_part = jnp.dot(
        jnp.cos(theta_x).astype(jnp.bfloat16), flat_data, preferred_element_type=jnp.float32
    ).reshape(x_length, mode_block, pair_width)
    sin_part = jnp.dot(
        jnp.sin(theta_x).astype(jnp.bfloat16), flat_data, preferred_element_type=jnp.float32
    ).reshape(x_length, mode_block, pair_width)
    real_out = cos_part[..., :channels] - sin_part[..., channels:]
    imag_out = cos_part[..., channels:] + sin_part[..., :channels]
    return jnp.concatenate([real_out, imag_out], -1).astype(jnp.bfloat16)


def inverse_yz(planes_data, y_count, z_count, norm_scale):
    planes, mode_total, pair_width = planes_data.shape
    channels = pair_width // 2
    wide_data = planes_data.astype(jnp.float32).reshape(planes, KY, KZ, pair_width)
    real_in = wide_data[..., :channels]
    imag_in = wide_data[..., channels:]
    theta_z = angles(KZ, z_count)
    cos_z = jnp.cos(theta_z)
    sin_z = jnp.sin(theta_z)
    real_mid = along_z_inverse(real_in, cos_z) - along_z_inverse(imag_in, sin_z)
    imag_mid = along_z_inverse(imag_in, cos_z) + along_z_inverse(real_in, sin_z)
    stacked = jnp.concatenate([real_mid, imag_mid], 1).reshape(planes, 2 * KY, z_count * channels)
    theta_y = angles(KY, y_count)
    table_y = jnp.concatenate([jnp.cos(theta_y), -jnp.sin(theta_y)], 0)
    return jnp.einsum("pfq,fy->pyq", stacked, table_y, precision=HIGHEST_PREC) * norm_scale


def mix_forward(coeffs, weights_local):
    channels = weights_local.shape[2]
    real_part = jnp.einsum(
        "kmc,kmcp->kmp", coeffs[..., :channels], weights_local, preferred_element_type=jnp.float32
    )
    imag_part = jnp.einsum(
        "kmc,kmcp->kmp", coeffs[..., channels:], weights_local, preferred_element_type=jnp.float32
    )
    out_real = real_part[..., :channels] - imag_part[..., channels:]
    out_imag = real_part[..., channels:] + imag_part[..., :channels]
    return jnp.concatenate([out_real, out_imag], -1).astype(jnp.bfloat16)


def mix_backward(coeffs, weights_local):
    channels = weights_local.shape[2]
    swapped = jnp.concatenate([coeffs[..., channels:], -coeffs[..., :channels]], -1)
    first_half = jnp.einsum(
        "kmp,kmcp->kmc", coeffs, weights_local, preferred_element_type=jnp.float32
    )
    second_half = jnp.einsum(
        "kmp,kmcp->kmc", swapped, weights_local, preferred_element_type=jnp.float32
    )
    return jnp.concatenate([first_half, second_half], -1).astype(jnp.bfloat16)


def pointwise(local_field, weights_small):
    planes, y_count, last_width = local_field.shape
    channels = weights_small.shape[0]
    paired = jnp.kron(jnp.eye(2, dtype=weights_small.dtype), weights_small)
    cell_pairs = local_field.reshape(planes * y_count * last_width // (2 * channels), 2 * channels)
    return jnp.dot(cell_pairs, paired, preferred_element_type=jnp.float32).reshape(
        planes, y_count, last_width
    )


def sample_sum(left_side, right_side):
    channels = left_side.shape[-1] // 2
    left_real = left_side[..., :channels]
    left_imag = left_side[..., channels:]
    right_real = right_side[..., :channels]
    right_imag = right_side[..., channels:]

    def outer_sum(left_op, right_op):
        return jnp.einsum("skmc,skmo->kmco", left_op, right_op, preferred_element_type=jnp.float32)

    real_sum = outer_sum(left_real, right_real) + outer_sum(left_imag, right_imag)
    imag_sum = outer_sum(left_real, right_imag) - outer_sum(left_imag, right_real)
    return jnp.concatenate([real_sum, imag_sum], -1)


def partner_rounds(slot_buffer):
    slot_count = slot_buffer.shape[0]
    my_index = lax.axis_index("gx")
    for bit_pos in range(slot_count.bit_length() - 1):
        shaped = slot_buffer.reshape(
            (slot_count >> bit_pos + 1, 2, 1 << bit_pos) + slot_buffer.shape[1:]
        )
        lower_half = shaped[:, 0]
        upper_half = shaped[:, 1]
        own_bit = jnp.bitwise_and(jnp.right_shift(my_index, bit_pos), 1) == 1
        outgoing = jnp.where(own_bit, lower_half, upper_half)
        incoming = partner(outgoing, "gx", bit_pos)
        new_lower = jnp.where(own_bit, incoming, lower_half)
        new_upper = jnp.where(own_bit, upper_half, incoming)
        slot_buffer = jnp.stack([new_lower, new_upper], 1).reshape(slot_buffer.shape)
    return slot_buffer


def toward_modes(mode_data):
    planes, mode_total, pair_width = mode_data.shape
    group_size = lax.axis_size("gx")
    slot_buffer = mode_data.reshape(
        planes, group_size, mode_total // group_size, pair_width
    ).transpose(1, 0, 2, 3)
    return partner_rounds(slot_buffer).reshape(
        planes * group_size, mode_total // group_size, pair_width
    )


def toward_planes(back_planes):
    x_length, mode_block, pair_width = back_planes.shape
    group_size = lax.axis_size("gx")
    slot_buffer = back_planes.reshape(group_size, x_length // group_size, mode_block, pair_width)
    arrived = partner_rounds(slot_buffer)
    return arrived.transpose(1, 0, 2, 3).reshape(
        x_length // group_size, group_size * mode_block, pair_width
    )


def on_device(field_in, cotangent, mode_weights, point_weights):
    local_field = field_in[0]
    planes, y_count, last_width = local_field.shape
    channels = point_weights.shape[0]
    z_count = last_width // channels
    kx_count = mode_weights.shape[0]
    x_length = planes * lax.axis_size("gx")
    norm_scale = 1.0 / math.sqrt(x_length * y_count * z_count)
    coeffs_in = forward_x(toward_modes(forward_yz(local_field, channels)), kx_count, norm_scale)
    mixed_modes = mix_forward(coeffs_in, mode_weights)
    spec_out = inverse_yz(
        toward_planes(inverse_x(mixed_modes, x_length)), y_count, z_count, norm_scale
    )
    pre_act = spec_out + pointwise(local_field, point_weights)
    activated, gelu_slope = gelu_parts(pre_act)
    out_grad = (cotangent[0].astype(jnp.float32) * gelu_slope).astype(jnp.bfloat16)
    coeffs_grad = forward_x(toward_modes(forward_yz(out_grad, channels)), kx_count, norm_scale)
    back_modes = mix_backward(coeffs_grad, mode_weights)
    spec_grad = inverse_yz(
        toward_planes(inverse_x(back_modes, x_length)), y_count, z_count, norm_scale
    )
    field_grad = (spec_grad + pointwise(out_grad, point_weights.T)).astype(jnp.bfloat16)
    shared_in, shared_grad = (
        lax.all_to_all(coeffs_in[None], "sa", split_axis=1, concat_axis=0, tiled=True),
        lax.all_to_all(coeffs_grad[None], "sa", split_axis=1, concat_axis=0, tiled=True),
    )
    weight_grad = sample_sum(shared_in, shared_grad)
    return (activated.astype(jnp.bfloat16)[None], field_grad[None], weight_grad)


def solution(mesh):
    in_specs = (
        P("sa", "gx", None, None),
        P("sa", "gx", None, None),
        P(None, "gx", None, None),
        P(),
    )
    out_specs = (P("sa", "gx", None, None), P("sa", "gx", None, None), P("sa", "gx", None, None))
    return jax.shard_map(
        on_device, mesh=mesh, in_specs=in_specs, out_specs=out_specs, check_vma=False
    )
```

profile of v0, /device:TPU:8, one launch (start us, length us, event | category | flops | bytes accessed | tf_op | source)
XLA Modules:
  0.0 280.4 jit_solution(13363651498479496618)
XLA Ops:
  5.0 5.2 %collective-permute-start = (bf16[64,1,1,4,128]{4,0,3,2,1:T(8,128)(2,1)S(1)}, bf16[64,1,1,4,128]{4,0,3,2,1:T(8,128)(2,1)S(1)}, u32[]{:S(2)}, u32[]{:S(2)}) collective-permute-start(bf16[64,1,1,4,128]{4,0,3,2,1:T(8,128)(2,1)S(1)} %broadcast_select_fusion.8), channel_id=1, source_target_pairs={{0,8},{8,0},{16,24},{24,16},{32,40},{40,32},{48,56},{56,48},{64,72... | collective-permute-start | bytes 196616 | tf_op jit(solution)/shard_map/ppermute | solution.py:23
  15.1 3.6 %collective-permute-done.1 = bf16[32,2,1,4,128]{4,0,3,1,2:T(8,128)(2,1)S(1)} collective-permute-done((bf16[32,2,1,4,128]{4,0,3,1,2:T(8,128)(2,1)S(1)}, bf16[32,2,1,4,128]{4,0,3,1,2:T(8,128)(2,1)S(1)}, u32[]{:S(2)}, u32[]{:S(2)}) %collective-permute-start.1) | collective-permute-done | bytes 65568 | tf_op jit(solution)/shard_map/ppermute | solution.py:23
  21.5 5.2 %collective-permute-done.2 = bf16[16,4,1,4,128]{4,0,3,1,2:T(8,128)(2,1)S(1)} collective-permute-done((bf16[16,4,1,4,128]{4,0,3,1,2:T(8,128)(2,1)S(1)}, bf16[16,4,1,4,128]{4,0,3,1,2:T(8,128)(2,1)S(1)}, u32[]{:S(2)}, u32[]{:S(2)}) %collective-permute-start.2) | collective-permute-done | bytes 65568 | tf_op jit(solution)/shard_map/ppermute | solution.py:23
  26.9 13.2 %collective-permute-start.3 = (bf16[8,8,1,4,128]{4,1,3,0,2:T(8,128)(2,1)S(1)}, bf16[8,8,1,4,128]{4,1,3,0,2:T(8,128)(2,1)S(1)}, u32[]{:S(2)}, u32[]{:S(2)}) collective-permute-start(bf16[8,8,1,4,128]{4,1,3,0,2:T(8,128)(2,1)S(1)} %broadcast_select_fusion.18), channel_id=1, source_target_pairs={{0,64},{64,0},{8,72},{72,8},{16,80},{80,16},{24,88},{88,24},{32,96... | collective-permute-start | bytes 196616 | tf_op jit(solution)/shard_map/ppermute | solution.py:23
  44.4 4.2 %collective-permute-done.4 = bf16[4,16,1,4,128]{4,1,3,0,2:T(8,128)(2,1)S(1)} collective-permute-done((bf16[4,16,1,4,128]{4,1,3,0,2:T(8,128)(2,1)S(1)}, bf16[4,16,1,4,128]{4,1,3,0,2:T(8,128)(2,1)S(1)}, u32[]{:S(2)}, u32[]{:S(2)}) %collective-permute-start.4) | collective-permute-done | bytes 65568 | tf_op jit(solution)/shard_map/ppermute | solution.py:23
  50.6 6.0 %collective-permute-done.5 = bf16[2,32,1,4,128]{4,1,3,0,2:T(8,128)(2,1)S(1)} collective-permute-done((bf16[2,32,1,4,128]{4,1,3,0,2:T(8,128)(2,1)S(1)}, bf16[2,32,1,4,128]{4,1,3,0,2:T(8,128)(2,1)S(1)}, u32[]{:S(2)}, u32[]{:S(2)}) %collective-permute-start.5) | collective-permute-done | bytes 65568 | tf_op jit(solution)/shard_map/ppermute | solution.py:23
  56.7 4.1 %collective-permute-start.6 = (bf16[1,64,1,4,128]{4,1,3,2,0:T(8,128)(2,1)S(1)}, bf16[1,64,1,4,128]{4,1,3,2,0:T(8,128)(2,1)S(1)}, u32[]{:S(2)}, u32[]{:S(2)}) collective-permute-start(bf16[1,64,1,4,128]{4,1,3,2,0:T(8,128)(2,1)S(1)} %broadcast_select_fusion.30), channel_id=1, source_target_pairs={{0,512},{512,0},{8,520},{520,8},{16,528},{528,16},{24,536},{536,24... | collective-permute-start | bytes 196616 | tf_op jit(solution)/shard_map/ppermute | solution.py:23
  60.8 6.0 %collective-permute-done.6 = bf16[1,64,1,4,128]{4,1,3,2,0:T(8,128)(2,1)S(1)} collective-permute-done((bf16[1,64,1,4,128]{4,1,3,2,0:T(8,128)(2,1)S(1)}, bf16[1,64,1,4,128]{4,1,3,2,0:T(8,128)(2,1)S(1)}, u32[]{:S(2)}, u32[]{:S(2)}) %collective-permute-start.6) | collective-permute-done | bytes 65568 | tf_op jit(solution)/shard_map/ppermute | solution.py:23
  71.1 3.4 %collective-permute-start.7 = (bf16[64,1,1,4,128]{4,0,3,2,1:T(8,128)(2,1)S(1)}, bf16[64,1,1,4,128]{4,0,3,2,1:T(8,128)(2,1)S(1)}, u32[]{:S(2)}, u32[]{:S(2)}) collective-permute-start(bf16[64,1,1,4,128]{4,0,3,2,1:T(8,128)(2,1)S(1)} %bitcast_select_fusion.3), channel_id=1, source_target_pairs={{0,8},{8,0},{16,24},{24,16},{32,40},{40,32},{48,56},{56,48},{64,72... | collective-permute-start | bytes 196616 | tf_op jit(solution)/shard_map/ppermute | solution.py:23
  79.8 3.7 %collective-permute-done.8 = bf16[32,2,1,4,128]{4,0,3,1,2:T(8,128)(2,1)S(1)} collective-permute-done((bf16[32,2,1,4,128]{4,0,3,1,2:T(8,128)(2,1)S(1)}, bf16[32,2,1,4,128]{4,0,3,1,2:T(8,128)(2,1)S(1)}, u32[]{:S(2)}, u32[]{:S(2)}) %collective-permute-start.8) | collective-permute-done | bytes 65568 | tf_op jit(solution)/shard_map/ppermute | solution.py:23
  86.0 5.6 %collective-permute-done.9 = bf16[16,4,1,4,128]{4,0,3,1,2:T(8,128)(2,1)S(1)} collective-permute-done((bf16[16,4,1,4,128]{4,0,3,1,2:T(8,128)(2,1)S(1)}, bf16[16,4,1,4,128]{4,0,3,1,2:T(8,128)(2,1)S(1)}, u32[]{:S(2)}, u32[]{:S(2)}) %collective-permute-start.9) | collective-permute-done | bytes 65568 | tf_op jit(solution)/shard_map/ppermute | solution.py:23
  91.8 7.6 %collective-permute-start.10 = (bf16[8,8,1,4,128]{4,1,3,0,2:T(8,128)(2,1)S(1)}, bf16[8,8,1,4,128]{4,1,3,0,2:T(8,128)(2,1)S(1)}, u32[]{:S(2)}, u32[]{:S(2)}) collective-permute-start(bf16[8,8,1,4,128]{4,1,3,0,2:T(8,128)(2,1)S(1)} %broadcast_select_fusion.17), channel_id=1, source_target_pairs={{0,64},{64,0},{8,72},{72,8},{16,80},{80,16},{24,88},{88,24},{32,96... | collective-permute-start | bytes 196616 | tf_op jit(solution)/shard_map/ppermute | solution.py:23
  104.4 4.4 %collective-permute-done.11 = bf16[4,16,1,4,128]{4,1,3,0,2:T(8,128)(2,1)S(1)} collective-permute-done((bf16[4,16,1,4,128]{4,1,3,0,2:T(8,128)(2,1)S(1)}, bf16[4,16,1,4,128]{4,1,3,0,2:T(8,128)(2,1)S(1)}, u32[]{:S(2)}, u32[]{:S(2)}) %collective-permute-start.11) | collective-permute-done | bytes 65568 | tf_op jit(solution)/shard_map/ppermute | solution.py:23
  116.0 4.6 %collective-permute-start.13 = (bf16[1,64,1,4,128]{4,1,3,2,0:T(8,128)(2,1)S(1)}, bf16[1,64,1,4,128]{4,1,3,2,0:T(8,128)(2,1)S(1)}, u32[]{:S(2)}, u32[]{:S(2)}) collective-permute-start(bf16[1,64,1,4,128]{4,1,3,2,0:T(8,128)(2,1)S(1)} %broadcast_select_fusion.29), channel_id=1, source_target_pairs={{0,512},{512,0},{8,520},{520,8},{16,528},{528,16},{24,536},{536,24... | collective-permute-start | bytes 196616 | tf_op jit(solution)/shard_map/ppermute | solution.py:23
  127.7 4.0 %fusion.22 = (bf16[256,1024]{1,0:T(8,128)(2,1)S(1)}, bf16[1,1,256,1024]{3,2,1,0:T(8,128)(2,1)}) fusion(bf16[1,1,256,1024]{3,2,1,0:T(8,128)(2,1)} %param.5, f32[256,1024]{1,0:T(8,128)} %reshape.968, f32[64,1024]{1,0:T(8,128)S(1)} %reshape.967, f32[32,256]{1,0:T(8,128)S(1)} %copy-done.6, f32[32,256]{1,0:T(8,128)S(1)} %copy-done.3), kind=kOutput, calls=%fused_computation.39 | convolution fusion | flops 207634432 | bytes 2949120 | tf_op jit(solution)/shard_map/pfq,fy->pyq/dot_general | solution.py:116
  134.2 3.3 %collective-permute-start.14 = (bf16[64,1,1,4,128]{4,0,3,2,1:T(8,128)(2,1)S(1)}, bf16[64,1,1,4,128]{4,0,3,2,1:T(8,128)(2,1)S(1)}, u32[]{:S(2)}, u32[]{:S(2)}) collective-permute-start(bf16[64,1,1,4,128]{4,0,3,2,1:T(8,128)(2,1)S(1)} %broadcast_select_fusion.5), channel_id=1, source_target_pairs={{0,8},{8,0},{16,24},{24,16},{32,40},{40,32},{48,56},{56,48},{64,72... | collective-permute-start | bytes 196616 | tf_op jit(solution)/shard_map/ppermute | solution.py:23
  143.1 3.5 %collective-permute-done.15 = bf16[32,2,1,4,128]{4,0,3,1,2:T(8,128)(2,1)S(1)} collective-permute-done((bf16[32,2,1,4,128]{4,0,3,1,2:T(8,128)(2,1)S(1)}, bf16[32,2,1,4,128]{4,0,3,1,2:T(8,128)(2,1)S(1)}, u32[]{:S(2)}, u32[]{:S(2)}) %collective-permute-start.15) | collective-permute-done | bytes 65568 | tf_op jit(solution)/shard_map/ppermute | solution.py:23
  148.8 5.8 %collective-permute-done.16 = bf16[16,4,1,4,128]{4,0,3,1,2:T(8,128)(2,1)S(1)} collective-permute-done((bf16[16,4,1,4,128]{4,0,3,1,2:T(8,128)(2,1)S(1)}, bf16[16,4,1,4,128]{4,0,3,1,2:T(8,128)(2,1)S(1)}, u32[]{:S(2)}, u32[]{:S(2)}) %collective-permute-start.16) | collective-permute-done | bytes 65568 | tf_op jit(solution)/shard_map/ppermute | solution.py:23
  154.8 6.7 %collective-permute-start.17 = (bf16[8,8,1,4,128]{4,1,3,0,2:T(8,128)(2,1)S(1)}, bf16[8,8,1,4,128]{4,1,3,0,2:T(8,128)(2,1)S(1)}, u32[]{:S(2)}, u32[]{:S(2)}) collective-permute-start(bf16[8,8,1,4,128]{4,1,3,0,2:T(8,128)(2,1)S(1)} %broadcast_select_fusion.16), channel_id=1, source_target_pairs={{0,64},{64,0},{8,72},{72,8},{16,80},{80,16},{24,88},{88,24},{32,96... | collective-permute-start | bytes 196616 | tf_op jit(solution)/shard_map/ppermute | solution.py:23
  161.6 3.3 %collective-permute-done.17 = bf16[8,8,1,4,128]{4,1,3,0,2:T(8,128)(2,1)S(1)} collective-permute-done((bf16[8,8,1,4,128]{4,1,3,0,2:T(8,128)(2,1)S(1)}, bf16[8,8,1,4,128]{4,1,3,0,2:T(8,128)(2,1)S(1)}, u32[]{:S(2)}, u32[]{:S(2)}) %collective-permute-start.17) | collective-permute-done | bytes 65568 | tf_op jit(solution)/shard_map/ppermute | solution.py:23
  167.4 3.8 %collective-permute-done.18 = bf16[4,16,1,4,128]{4,1,3,0,2:T(8,128)(2,1)S(1)} collective-permute-done((bf16[4,16,1,4,128]{4,1,3,0,2:T(8,128)(2,1)S(1)}, bf16[4,16,1,4,128]{4,1,3,0,2:T(8,128)(2,1)S(1)}, u32[]{:S(2)}, u32[]{:S(2)}) %collective-permute-start.18) | collective-permute-done | bytes 65568 | tf_op jit(solution)/shard_map/ppermute | solution.py:23
  173.2 5.8 %collective-permute-done.19 = bf16[2,32,1,4,128]{4,1,3,0,2:T(8,128)(2,1)S(1)} collective-permute-done((bf16[2,32,1,4,128]{4,1,3,0,2:T(8,128)(2,1)S(1)}, bf16[2,32,1,4,128]{4,1,3,0,2:T(8,128)(2,1)S(1)}, u32[]{:S(2)}, u32[]{:S(2)}) %collective-permute-start.19) | collective-permute-done | bytes 65568 | tf_op jit(solution)/shard_map/ppermute | solution.py:23
  179.0 4.5 %collective-permute-start.20 = (bf16[1,64,1,4,128]{4,1,3,2,0:T(8,128)(2,1)S(1)}, bf16[1,64,1,4,128]{4,1,3,2,0:T(8,128)(2,1)}, u32[]{:S(2)}, u32[]{:S(2)}) collective-permute-start(bf16[1,64,1,4,128]{4,1,3,2,0:T(8,128)(2,1)S(1)} %broadcast_select_fusion.28), channel_id=1, source_target_pairs={{0,512},{512,0},{8,520},{520,8},{16,528},{528,16},{24,536},{536,24... | collective-permute-start | bytes 196616 | tf_op jit(solution)/shard_map/ppermute | solution.py:23
  184.3 13.7 %all-to-all-start = ((bf16[1,32,4,128]{3,2,0,1:T(4,128)(2,1)}), bf16[1,32,4,128]{3,2,0,1:T(4,128)(2,1)S(1)}, u32[]{:S(2)}, u32[]{:S(2)}) async-start(bf16[1,32,4,128]{3,2,0,1:T(4,128)(2,1)} %copy.513), calls=%async_computation | async-start | bytes 65536 | tf_op jit(solution)/shard_map/all_to_all | solution.py:231
  198.1 7.8 %all-to-all-done = bf16[1,32,4,128]{3,2,0,1:T(4,128)(2,1)S(1)} async-done(((bf16[1,32,4,128]{3,2,0,1:T(4,128)(2,1)}), bf16[1,32,4,128]{3,2,0,1:T(4,128)(2,1)S(1)}, u32[]{:S(2)}, u32[]{:S(2)}) %all-to-all-start) | async-done | bytes 32800 | tf_op jit(solution)/shard_map/all_to_all | solution.py:231
  212.2 4.0 %all-to-all-start.1 = ((bf16[1,32,4,128]{3,2,0,1:T(4,128)(2,1)}), bf16[1,32,4,128]{3,2,0,1:T(4,128)(2,1)}, u32[]{:S(2)}, u32[]{:S(2)}) async-start(bf16[1,32,4,128]{3,2,0,1:T(4,128)(2,1)} %copy.516), calls=%async_computation.1 | async-start | bytes 65536 | tf_op jit(solution)/shard_map/all_to_all | solution.py:232
  217.3 3.7 %collective-permute-start.21 = (bf16[64,1,1,4,128]{4,0,3,2,1:T(8,128)(2,1)}, bf16[64,1,1,4,128]{4,0,3,2,1:T(8,128)(2,1)}, u32[]{:S(2)}, u32[]{:S(2)}) collective-permute-start(bf16[64,1,1,4,128]{4,0,3,2,1:T(8,128)(2,1)} %get-tuple-element.3), channel_id=1, source_target_pairs={{0,8},{8,0},{16,24},{24,16},{32,40},{40,32},{48,56},{56,48},{64,72... | collective-permute-start | bytes 196616 | tf_op jit(solution)/shard_map/ppermute | solution.py:23
  235.1 5.0 %collective-permute-done.23 = bf16[16,4,1,4,128]{4,0,3,1,2:T(8,128)(2,1)S(1)} collective-permute-done((bf16[16,4,1,4,128]{4,0,3,1,2:T(8,128)(2,1)S(1)}, bf16[16,4,1,4,128]{4,0,3,1,2:T(8,128)(2,1)S(1)}, u32[]{:S(2)}, u32[]{:S(2)}) %collective-permute-start.23) | collective-permute-done | bytes 65568 | tf_op jit(solution)/shard_map/ppermute | solution.py:23
  243.7 7.2 %collective-permute-done.24 = bf16[8,8,1,4,128]{4,1,3,0,2:T(8,128)(2,1)S(1)} collective-permute-done((bf16[8,8,1,4,128]{4,1,3,0,2:T(8,128)(2,1)S(1)}, bf16[8,8,1,4,128]{4,1,3,0,2:T(8,128)(2,1)S(1)}, u32[]{:S(2)}, u32[]{:S(2)}) %collective-permute-start.24) | collective-permute-done | bytes 65568 | tf_op jit(solution)/shard_map/ppermute | solution.py:23
  259.4 4.9 %collective-permute-done.26 = bf16[2,32,1,4,128]{4,1,3,0,2:T(8,128)(2,1)S(1)} collective-permute-done((bf16[2,32,1,4,128]{4,1,3,0,2:T(8,128)(2,1)S(1)}, bf16[2,32,1,4,128]{4,1,3,0,2:T(8,128)(2,1)S(1)}, u32[]{:S(2)}, u32[]{:S(2)}) %collective-permute-start.26) | collective-permute-done | bytes 65568 | tf_op jit(solution)/shard_map/ppermute | solution.py:23
  264.3 5.1 %collective-permute-start.27 = (bf16[1,64,1,4,128]{4,1,3,2,0:T(8,128)(2,1)S(1)}, bf16[1,64,1,4,128]{4,1,3,2,0:T(8,128)(2,1)S(1)}, u32[]{:S(2)}, u32[]{:S(2)}) collective-permute-start(bf16[1,64,1,4,128]{4,1,3,2,0:T(8,128)(2,1)S(1)} %broadcast_select_fusion.27), channel_id=1, source_target_pairs={{0,512},{512,0},{8,520},{520,8},{16,528},{528,16},{24,536},{536,24... | collective-permute-start | bytes 196616 | tf_op jit(solution)/shard_map/ppermute | solution.py:23
  270.4 4.7 %collective-permute-done.27 = bf16[1,64,1,4,128]{4,1,3,2,0:T(8,128)(2,1)S(1)} collective-permute-done((bf16[1,64,1,4,128]{4,1,3,2,0:T(8,128)(2,1)S(1)}, bf16[1,64,1,4,128]{4,1,3,2,0:T(8,128)(2,1)S(1)}, u32[]{:S(2)}, u32[]{:S(2)}) %collective-permute-start.27) | collective-permute-done | bytes 65568 | tf_op jit(solution)/shard_map/ppermute | solution.py:23
  (257 shorter events, 104.5 us)
Async XLA Ops:
  0.6 67.3 %copy-start = (bf16[32,4,64,128]{3,2,1,0:T(8,128)(2,1)S(1)}, bf16[32,4,64,128]{3,2,1,0:T(8,128)(2,1)}, u32[]{:S(2)}) copy-start(bf16[32,4,64,128]{3,2,1,0:T(8,128)(2,1)} %param.6) | copy-start | bytes 6291460
  5.0 7.4 %collective-permute-start = (bf16[64,1,1,4,128]{4,0,3,2,1:T(8,128)(2,1)S(1)}, bf16[64,1,1,4,128]{4,0,3,2,1:T(8,128)(2,1)S(1)}, u32[]{:S(2)}, u32[]{:S(2)}) collective-permute-start(bf16[64,1,1,4,128]{4,0,3,2,1:T(8,128)(2,1)S(1)} %broadcast_select_fusion.8), channel_id=1, source_target_pairs={{0,8},{8,0},{16,24},{24,16},{32,40},{40,32},{48,56},{56,48},{64,72... | collective-permute-start | bytes 196616 | tf_op jit(solution)/shard_map/ppermute | solution.py:23
  12.5 6.2 %collective-permute-start.1 = (bf16[32,2,1,4,128]{4,0,3,1,2:T(8,128)(2,1)S(1)}, bf16[32,2,1,4,128]{4,0,3,1,2:T(8,128)(2,1)S(1)}, u32[]{:S(2)}, u32[]{:S(2)}) collective-permute-start(bf16[32,2,1,4,128]{4,0,3,1,2:T(8,128)(2,1)S(1)} %broadcast_select_fusion.11), channel_id=1, source_target_pairs={{0,16},{16,0},{8,24},{24,8},{32,48},{48,32},{40,56},{56,40},{64,80... | collective-permute-start | bytes 196616 | tf_op jit(solution)/shard_map/ppermute | solution.py:23
  19.0 7.8 %collective-permute-start.2 = (bf16[16,4,1,4,128]{4,0,3,1,2:T(8,128)(2,1)S(1)}, bf16[16,4,1,4,128]{4,0,3,1,2:T(8,128)(2,1)S(1)}, u32[]{:S(2)}, u32[]{:S(2)}) collective-permute-start(bf16[16,4,1,4,128]{4,0,3,1,2:T(8,128)(2,1)S(1)} %broadcast_select_fusion.14), channel_id=1, source_target_pairs={{0,32},{32,0},{8,40},{40,8},{16,48},{48,16},{24,56},{56,24},{64,96... | collective-permute-start | bytes 196616 | tf_op jit(solution)/shard_map/ppermute | solution.py:23
  26.9 15.4 %collective-permute-start.3 = (bf16[8,8,1,4,128]{4,1,3,0,2:T(8,128)(2,1)S(1)}, bf16[8,8,1,4,128]{4,1,3,0,2:T(8,128)(2,1)S(1)}, u32[]{:S(2)}, u32[]{:S(2)}) collective-permute-start(bf16[8,8,1,4,128]{4,1,3,0,2:T(8,128)(2,1)S(1)} %broadcast_select_fusion.18), channel_id=1, source_target_pairs={{0,64},{64,0},{8,72},{72,8},{16,80},{80,16},{24,88},{88,24},{32,96... | collective-permute-start | bytes 196616 | tf_op jit(solution)/shard_map/ppermute | solution.py:23
  42.4 6.2 %collective-permute-start.4 = (bf16[4,16,1,4,128]{4,1,3,0,2:T(8,128)(2,1)S(1)}, bf16[4,16,1,4,128]{4,1,3,0,2:T(8,128)(2,1)S(1)}, u32[]{:S(2)}, u32[]{:S(2)}) collective-permute-start(bf16[4,16,1,4,128]{4,1,3,0,2:T(8,128)(2,1)S(1)} %broadcast_select_fusion.22), channel_id=1, source_target_pairs={{0,128},{128,0},{8,136},{136,8},{16,144},{144,16},{24,152},{152,24... | collective-permute-start | bytes 196616 | tf_op jit(solution)/shard_map/ppermute | solution.py:23
  48.7 7.9 %collective-permute-start.5 = (bf16[2,32,1,4,128]{4,1,3,0,2:T(8,128)(2,1)S(1)}, bf16[2,32,1,4,128]{4,1,3,0,2:T(8,128)(2,1)S(1)}, u32[]{:S(2)}, u32[]{:S(2)}) collective-permute-start(bf16[2,32,1,4,128]{4,1,3,0,2:T(8,128)(2,1)S(1)} %broadcast_select_fusion.26), channel_id=1, source_target_pairs={{0,256},{256,0},{8,264},{264,8},{16,272},{272,16},{24,280},{280,24... | collective-permute-start | bytes 196616 | tf_op jit(solution)/shard_map/ppermute | solution.py:23
  56.7 10.1 %collective-permute-start.6 = (bf16[1,64,1,4,128]{4,1,3,2,0:T(8,128)(2,1)S(1)}, bf16[1,64,1,4,128]{4,1,3,2,0:T(8,128)(2,1)S(1)}, u32[]{:S(2)}, u32[]{:S(2)}) collective-permute-start(bf16[1,64,1,4,128]{4,1,3,2,0:T(8,128)(2,1)S(1)} %broadcast_select_fusion.30), channel_id=1, source_target_pairs={{0,512},{512,0},{8,520},{520,8},{16,528},{528,16},{24,536},{536,24... | collective-permute-start | bytes 196616 | tf_op jit(solution)/shard_map/ppermute | solution.py:23
  71.1 6.2 %collective-permute-start.7 = (bf16[64,1,1,4,128]{4,0,3,2,1:T(8,128)(2,1)S(1)}, bf16[64,1,1,4,128]{4,0,3,2,1:T(8,128)(2,1)S(1)}, u32[]{:S(2)}, u32[]{:S(2)}) collective-permute-start(bf16[64,1,1,4,128]{4,0,3,2,1:T(8,128)(2,1)S(1)} %bitcast_select_fusion.3), channel_id=1, source_target_pairs={{0,8},{8,0},{16,24},{24,16},{32,40},{40,32},{48,56},{56,48},{64,72... | collective-permute-start | bytes 196616 | tf_op jit(solution)/shard_map/ppermute | solution.py:23
  77.3 6.2 %collective-permute-start.8 = (bf16[32,2,1,4,128]{4,0,3,1,2:T(8,128)(2,1)S(1)}, bf16[32,2,1,4,128]{4,0,3,1,2:T(8,128)(2,1)S(1)}, u32[]{:S(2)}, u32[]{:S(2)}) collective-permute-start(bf16[32,2,1,4,128]{4,0,3,1,2:T(8,128)(2,1)S(1)} %bitcast_select_fusion.6), channel_id=1, source_target_pairs={{0,16},{16,0},{8,24},{24,8},{32,48},{48,32},{40,56},{56,40},{64,80... | collective-permute-start | bytes 196616 | tf_op jit(solution)/shard_map/ppermute | solution.py:23
  83.8 7.8 %collective-permute-start.9 = (bf16[16,4,1,4,128]{4,0,3,1,2:T(8,128)(2,1)S(1)}, bf16[16,4,1,4,128]{4,0,3,1,2:T(8,128)(2,1)S(1)}, u32[]{:S(2)}, u32[]{:S(2)}) collective-permute-start(bf16[16,4,1,4,128]{4,0,3,1,2:T(8,128)(2,1)S(1)} %bitcast_select_fusion.5), channel_id=1, source_target_pairs={{0,32},{32,0},{8,40},{40,8},{16,48},{48,16},{24,56},{56,24},{64,96... | collective-permute-start | bytes 196616 | tf_op jit(solution)/shard_map/ppermute | solution.py:23
  91.8 10.1 %collective-permute-start.10 = (bf16[8,8,1,4,128]{4,1,3,0,2:T(8,128)(2,1)S(1)}, bf16[8,8,1,4,128]{4,1,3,0,2:T(8,128)(2,1)S(1)}, u32[]{:S(2)}, u32[]{:S(2)}) collective-permute-start(bf16[8,8,1,4,128]{4,1,3,0,2:T(8,128)(2,1)S(1)} %broadcast_select_fusion.17), channel_id=1, source_target_pairs={{0,64},{64,0},{8,72},{72,8},{16,80},{80,16},{24,88},{88,24},{32,96... | collective-permute-start | bytes 196616 | tf_op jit(solution)/shard_map/ppermute | solution.py:23
  101.9 6.8 %collective-permute-start.11 = (bf16[4,16,1,4,128]{4,1,3,0,2:T(8,128)(2,1)S(1)}, bf16[4,16,1,4,128]{4,1,3,0,2:T(8,128)(2,1)S(1)}, u32[]{:S(2)}, u32[]{:S(2)}) collective-permute-start(bf16[4,16,1,4,128]{4,1,3,0,2:T(8,128)(2,1)S(1)} %broadcast_select_fusion.21), channel_id=1, source_target_pairs={{0,128},{128,0},{8,136},{136,8},{16,144},{144,16},{24,152},{152,24... | collective-permute-start | bytes 196616 | tf_op jit(solution)/shard_map/ppermute | solution.py:23
  108.8 7.1 %collective-permute-start.12 = (bf16[2,32,1,4,128]{4,1,3,0,2:T(8,128)(2,1)S(1)}, bf16[2,32,1,4,128]{4,1,3,0,2:T(8,128)(2,1)S(1)}, u32[]{:S(2)}, u32[]{:S(2)}) collective-permute-start(bf16[2,32,1,4,128]{4,1,3,0,2:T(8,128)(2,1)S(1)} %broadcast_select_fusion.25), channel_id=1, source_target_pairs={{0,256},{256,0},{8,264},{264,8},{16,272},{272,16},{24,280},{280,24... | collective-permute-start | bytes 196616 | tf_op jit(solution)/shard_map/ppermute | solution.py:23
  116.0 10.1 %collective-permute-start.13 = (bf16[1,64,1,4,128]{4,1,3,2,0:T(8,128)(2,1)S(1)}, bf16[1,64,1,4,128]{4,1,3,2,0:T(8,128)(2,1)S(1)}, u32[]{:S(2)}, u32[]{:S(2)}) collective-permute-start(bf16[1,64,1,4,128]{4,1,3,2,0:T(8,128)(2,1)S(1)} %broadcast_select_fusion.29), channel_id=1, source_target_pairs={{0,512},{512,0},{8,520},{520,8},{16,528},{528,16},{24,536},{536,24... | collective-permute-start | bytes 196616 | tf_op jit(solution)/shard_map/ppermute | solution.py:23
  134.2 6.2 %collective-permute-start.14 = (bf16[64,1,1,4,128]{4,0,3,2,1:T(8,128)(2,1)S(1)}, bf16[64,1,1,4,128]{4,0,3,2,1:T(8,128)(2,1)S(1)}, u32[]{:S(2)}, u32[]{:S(2)}) collective-permute-start(bf16[64,1,1,4,128]{4,0,3,2,1:T(8,128)(2,1)S(1)} %broadcast_select_fusion.5), channel_id=1, source_target_pairs={{0,8},{8,0},{16,24},{24,16},{32,40},{40,32},{48,56},{56,48},{64,72... | collective-permute-start | bytes 196616 | tf_op jit(solution)/shard_map/ppermute | solution.py:23
  140.5 6.2 %collective-permute-start.15 = (bf16[32,2,1,4,128]{4,0,3,1,2:T(8,128)(2,1)S(1)}, bf16[32,2,1,4,128]{4,0,3,1,2:T(8,128)(2,1)S(1)}, u32[]{:S(2)}, u32[]{:S(2)}) collective-permute-start(bf16[32,2,1,4,128]{4,0,3,1,2:T(8,128)(2,1)S(1)} %broadcast_select_fusion.10), channel_id=1, source_target_pairs={{0,16},{16,0},{8,24},{24,8},{32,48},{48,32},{40,56},{56,40},{64,80... | collective-permute-start | bytes 196616 | tf_op jit(solution)/shard_map/ppermute | solution.py:23
  146.9 7.8 %collective-permute-start.16 = (bf16[16,4,1,4,128]{4,0,3,1,2:T(8,128)(2,1)S(1)}, bf16[16,4,1,4,128]{4,0,3,1,2:T(8,128)(2,1)S(1)}, u32[]{:S(2)}, u32[]{:S(2)}) collective-permute-start(bf16[16,4,1,4,128]{4,0,3,1,2:T(8,128)(2,1)S(1)} %broadcast_select_fusion.13), channel_id=1, source_target_pairs={{0,32},{32,0},{8,40},{40,8},{16,48},{48,16},{24,56},{56,24},{64,96... | collective-permute-start | bytes 196616 | tf_op jit(solution)/shard_map/ppermute | solution.py:23
  154.7 43.4 %copy-start.8 = (bf16[2,64,2,64]{3,2,1,0:T(2,128)(2,1)S(1)}, bf16[2,64,2,64]{3,2,1,0:T(2,128)(2,1)}, u32[]{:S(2)}) copy-start(bf16[2,64,2,64]{3,2,1,0:T(2,128)(2,1)} %get-tuple-element.91) | copy-start | bytes 98308
  154.8 10.1 %collective-permute-start.17 = (bf16[8,8,1,4,128]{4,1,3,0,2:T(8,128)(2,1)S(1)}, bf16[8,8,1,4,128]{4,1,3,0,2:T(8,128)(2,1)S(1)}, u32[]{:S(2)}, u32[]{:S(2)}) collective-permute-start(bf16[8,8,1,4,128]{4,1,3,0,2:T(8,128)(2,1)S(1)} %broadcast_select_fusion.16), channel_id=1, source_target_pairs={{0,64},{64,0},{8,72},{72,8},{16,80},{80,16},{24,88},{88,24},{32,96... | collective-permute-start | bytes 196616 | tf_op jit(solution)/shard_map/ppermute | solution.py:23
  165.0 6.2 %collective-permute-start.18 = (bf16[4,16,1,4,128]{4,1,3,0,2:T(8,128)(2,1)S(1)}, bf16[4,16,1,4,128]{4,1,3,0,2:T(8,128)(2,1)S(1)}, u32[]{:S(2)}, u32[]{:S(2)}) collective-permute-start(bf16[4,16,1,4,128]{4,1,3,0,2:T(8,128)(2,1)S(1)} %broadcast_select_fusion.20), channel_id=1, source_target_pairs={{0,128},{128,0},{8,136},{136,8},{16,144},{144,16},{24,152},{152,24... | collective-permute-start | bytes 196616 | tf_op jit(solution)/shard_map/ppermute | solution.py:23
  171.2 7.7 %collective-permute-start.19 = (bf16[2,32,1,4,128]{4,1,3,0,2:T(8,128)(2,1)S(1)}, bf16[2,32,1,4,128]{4,1,3,0,2:T(8,128)(2,1)S(1)}, u32[]{:S(2)}, u32[]{:S(2)}) collective-permute-start(bf16[2,32,1,4,128]{4,1,3,0,2:T(8,128)(2,1)S(1)} %broadcast_select_fusion.24), channel_id=1, source_target_pairs={{0,256},{256,0},{8,264},{264,8},{16,272},{272,16},{24,280},{280,24... | collective-permute-start | bytes 196616 | tf_op jit(solution)/shard_map/ppermute | solution.py:23
  179.0 27.2 %collective-permute-start.20 = (bf16[1,64,1,4,128]{4,1,3,2,0:T(8,128)(2,1)S(1)}, bf16[1,64,1,4,128]{4,1,3,2,0:T(8,128)(2,1)}, u32[]{:S(2)}, u32[]{:S(2)}) collective-permute-start(bf16[1,64,1,4,128]{4,1,3,2,0:T(8,128)(2,1)S(1)} %broadcast_select_fusion.28), channel_id=1, source_target_pairs={{0,512},{512,0},{8,520},{520,8},{16,528},{528,16},{24,536},{536,24... | collective-permute-start | bytes 196616 | tf_op jit(solution)/shard_map/ppermute | solution.py:23
  184.3 21.7 %all-to-all-start = ((bf16[1,32,4,128]{3,2,0,1:T(4,128)(2,1)}), bf16[1,32,4,128]{3,2,0,1:T(4,128)(2,1)S(1)}, u32[]{:S(2)}, u32[]{:S(2)}) async-start(bf16[1,32,4,128]{3,2,0,1:T(4,128)(2,1)} %copy.513), calls=%async_computation | async-start | bytes 65536 | tf_op jit(solution)/shard_map/all_to_all | solution.py:231
  212.2 11.9 %all-to-all-start.1 = ((bf16[1,32,4,128]{3,2,0,1:T(4,128)(2,1)}), bf16[1,32,4,128]{3,2,0,1:T(4,128)(2,1)}, u32[]{:S(2)}, u32[]{:S(2)}) async-start(bf16[1,32,4,128]{3,2,0,1:T(4,128)(2,1)} %copy.516), calls=%async_computation.1 | async-start | bytes 65536 | tf_op jit(solution)/shard_map/all_to_all | solution.py:232
  217.3 7.6 %collective-permute-start.21 = (bf16[64,1,1,4,128]{4,0,3,2,1:T(8,128)(2,1)}, bf16[64,1,1,4,128]{4,0,3,2,1:T(8,128)(2,1)}, u32[]{:S(2)}, u32[]{:S(2)}) collective-permute-start(bf16[64,1,1,4,128]{4,0,3,2,1:T(8,128)(2,1)} %get-tuple-element.3), channel_id=1, source_target_pairs={{0,8},{8,0},{16,24},{24,16},{32,40},{40,32},{48,56},{56,48},{64,72... | collective-permute-start | bytes 196616 | tf_op jit(solution)/shard_map/ppermute | solution.py:23
  225.9 6.2 %collective-permute-start.22 = (bf16[32,2,1,4,128]{4,0,3,1,2:T(8,128)(2,1)S(1)}, bf16[32,2,1,4,128]{4,0,3,1,2:T(8,128)(2,1)S(1)}, u32[]{:S(2)}, u32[]{:S(2)}) collective-permute-start(bf16[32,2,1,4,128]{4,0,3,1,2:T(8,128)(2,1)S(1)} %broadcast_select_fusion.9), channel_id=1, source_target_pairs={{0,16},{16,0},{8,24},{24,8},{32,48},{48,32},{40,56},{56,40},{64,80... | collective-permute-start | bytes 196616 | tf_op jit(solution)/shard_map/ppermute | solution.py:23
  232.3 7.8 %collective-permute-start.23 = (bf16[16,4,1,4,128]{4,0,3,1,2:T(8,128)(2,1)S(1)}, bf16[16,4,1,4,128]{4,0,3,1,2:T(8,128)(2,1)S(1)}, u32[]{:S(2)}, u32[]{:S(2)}) collective-permute-start(bf16[16,4,1,4,128]{4,0,3,1,2:T(8,128)(2,1)S(1)} %broadcast_select_fusion.12), channel_id=1, source_target_pairs={{0,32},{32,0},{8,40},{40,8},{16,48},{48,16},{24,56},{56,24},{64,96... | collective-permute-start | bytes 196616 | tf_op jit(solution)/shard_map/ppermute | solution.py:23
  240.3 10.6 %collective-permute-start.24 = (bf16[8,8,1,4,128]{4,1,3,0,2:T(8,128)(2,1)S(1)}, bf16[8,8,1,4,128]{4,1,3,0,2:T(8,128)(2,1)S(1)}, u32[]{:S(2)}, u32[]{:S(2)}) collective-permute-start(bf16[8,8,1,4,128]{4,1,3,0,2:T(8,128)(2,1)S(1)} %broadcast_select_fusion.15), channel_id=1, source_target_pairs={{0,64},{64,0},{8,72},{72,8},{16,80},{80,16},{24,88},{88,24},{32,96... | collective-permute-start | bytes 196616 | tf_op jit(solution)/shard_map/ppermute | solution.py:23
  250.9 6.2 %collective-permute-start.25 = (bf16[4,16,1,4,128]{4,1,3,0,2:T(8,128)(2,1)S(1)}, bf16[4,16,1,4,128]{4,1,3,0,2:T(8,128)(2,1)S(1)}, u32[]{:S(2)}, u32[]{:S(2)}) collective-permute-start(bf16[4,16,1,4,128]{4,1,3,0,2:T(8,128)(2,1)S(1)} %broadcast_select_fusion.19), channel_id=1, source_target_pairs={{0,128},{128,0},{8,136},{136,8},{16,144},{144,16},{24,152},{152,24... | collective-permute-start | bytes 196616 | tf_op jit(solution)/shard_map/ppermute | solution.py:23
  257.2 7.1 %collective-permute-start.26 = (bf16[2,32,1,4,128]{4,1,3,0,2:T(8,128)(2,1)S(1)}, bf16[2,32,1,4,128]{4,1,3,0,2:T(8,128)(2,1)S(1)}, u32[]{:S(2)}, u32[]{:S(2)}) collective-permute-start(bf16[2,32,1,4,128]{4,1,3,0,2:T(8,128)(2,1)S(1)} %broadcast_select_fusion.23), channel_id=1, source_target_pairs={{0,256},{256,0},{8,264},{264,8},{16,272},{272,16},{24,280},{280,24... | collective-permute-start | bytes 196616 | tf_op jit(solution)/shard_map/ppermute | solution.py:23
  264.3 10.8 %collective-permute-start.27 = (bf16[1,64,1,4,128]{4,1,3,2,0:T(8,128)(2,1)S(1)}, bf16[1,64,1,4,128]{4,1,3,2,0:T(8,128)(2,1)S(1)}, u32[]{:S(2)}, u32[]{:S(2)}) collective-permute-start(bf16[1,64,1,4,128]{4,1,3,2,0:T(8,128)(2,1)S(1)} %broadcast_select_fusion.27), channel_id=1, source_target_pairs={{0,512},{512,0},{8,520},{520,8},{16,528},{528,16},{24,536},{536,24... | collective-permute-start | bytes 196616 | tf_op jit(solution)/shard_map/ppermute | solution.py:23
  (8 other events, 68.3 us)
where the time goes:
time: 282 us; the launch traced here: 280 us
  starting transfers between devices  119 us (42%)
  waiting for transfers between devices  112 us (40%)
  matrix products  23.2 us (8%)
  local copies, waits for them, and re-layouts  14.5 us (5%)
  other arithmetic  8.74 us (3%)
    ppermute x28, waiting for transfers between devices, partner(): return lax.ppermute(block, axis, route)  104 us
    ppermute x28, starting transfers between devices, partner(): return lax.ppermute(block, axis, route)  102 us
    all_to_all x1, starting transfers between devices, on_device(): lax.all_to_all(coeffs_in[None], 'sa', split_axis=1, concat_axis=0, tiled=...  13.7 us
    all_to_all x1, waiting for transfers between devices, on_device(): lax.all_to_all(coeffs_in[None], 'sa', split_axis=1, concat_axis=0, tiled=...  7.83 us
    dot_general x2, matrix products, inverse_yz(): jnp.einsum('pfq,fy->pyq', stacked, table_y, precision=HIGHEST_PREC)  5.82 us
  transfers between devices with their start and end apart: 30, of which 28 were waited for; matrix products, arithmetic and copies ran while one was open for 5% of the time, Pallas kernels for 0%

commit v1 on v0

--- a/solution.py
+++ b/solution.py
@@ -11,16 +11,6 @@
 
 HIGHEST_PREC = lax.Precision.HIGHEST
 GELU_COEF = 0.044715
-
-
-def partner(block, axis, distance):
-    count = lax.axis_size(axis)
-    route = []
-    for low in range(count):
-        high = low | 1 << distance
-        if high != low and high < count:
-            route += [(low, high), (high, low)]
-    return lax.ppermute(block, axis, route)
 
 
 def angles(freq_count, grid_count):
@@ -166,22 +156,8 @@
     return jnp.concatenate([real_sum, imag_sum], -1)
 
 
-def partner_rounds(slot_buffer):
-    slot_count = slot_buffer.shape[0]
-    my_index = lax.axis_index("gx")
-    for bit_pos in range(slot_count.bit_length() - 1):
-        shaped = slot_buffer.reshape(
-            (slot_count >> bit_pos + 1, 2, 1 << bit_pos) + slot_buffer.shape[1:]
-        )
-        lower_half = shaped[:, 0]
-        upper_half = shaped[:, 1]
-        own_bit = jnp.bitwise_and(jnp.right_shift(my_index, bit_pos), 1) == 1
-        outgoing = jnp.where(own_bit, lower_half, upper_half)
-        incoming = partner(outgoing, "gx", bit_pos)
-        new_lower = jnp.where(own_bit, incoming, lower_half)
-        new_upper = jnp.where(own_bit, upper_half, incoming)
-        slot_buffer = jnp.stack([new_lower, new_upper], 1).reshape(slot_buffer.shape)
-    return slot_buffer
+def exchange(slot_buffer):
+    return lax.all_to_all(slot_buffer, "gx", split_axis=0, concat_axis=0, tiled=True)
 
 
 def toward_modes(mode_data):
@@ -190,7 +166,7 @@
     slot_buffer = mode_data.reshape(
         planes, group_size, mode_total // group_size, pair_width
     ).transpose(1, 0, 2, 3)
-    return partner_rounds(slot_buffer).reshape(
+    return exchange(slot_buffer).reshape(
         planes * group_size, mode_total // group_size, pair_width
     )
 
@@ -199,7 +175,7 @@
     x_length, mode_block, pair_width = back_planes.shape
     group_size = lax.axis_size("gx")
     slot_buffer = back_planes.reshape(group_size, x_length // group_size, mode_block, pair_width)
-    arrived = partner_rounds(slot_buffer)
+    arrived = exchange(slot_buffer)
     return arrived.transpose(1, 0, 2, 3).reshape(
         x_length // group_size, group_size * mode_block, pair_width
     )

time: 282 us -> 149 us (0.53)
  the two profiles are of different devices: /device:TPU:8 before, /device:TPU:1 now
where the time goes in v1:
time: 149 us; the launch traced here: 148 us
  starting transfers between devices  61.6 us (41%)
  waiting for transfers between devices  44 us (30%)
  matrix products  24.1 us (16%)
  local copies, waits for them, and re-layouts  11.6 us (8%)
  other arithmetic  6.05 us (4%)
    all_to_all x4, starting transfers between devices, exchange(): lax.all_to_all(slot_buffer, 'gx', split_axis=0, concat_axis=0, tiled=True)  38.9 us
    all_to_all x4, waiting for transfers between devices, exchange(): lax.all_to_all(slot_buffer, 'gx', split_axis=0, concat_axis=0, tiled=True)  32.2 us
    all_to_all x1, starting transfers between devices, on_device(): lax.all_to_all(coeffs_in[None], 'sa', split_axis=1, concat_axis=0, tiled=...  17.1 us
    all_to_all x1, waiting for transfers between devices, on_device(): lax.all_to_all(coeffs_in[None], 'sa', split_axis=1, concat_axis=0, tiled=...  6.37 us
    dot_general x2, matrix products, inverse_yz(): jnp.einsum('pfq,fy->pyq', stacked, table_y, precision=HIGHEST_PREC)  5.83 us
    all_to_all x1, starting transfers between devices, on_device(): lax.all_to_all(coeffs_grad[None], 'sa', split_axis=1, concat_axis=0, tile...  5.63 us
    all_to_all x1, waiting for transfers between devices, on_device(): lax.all_to_all(coeffs_grad[None], 'sa', split_axis=1, concat_axis=0, tile...  5.42 us
    dot_general x8, matrix products, along_z_forward(): return jnp.einsum('pyzc,kz->pykc', data_in, table_z, precision=HIGHEST_PREC)  3.78 us
  transfers between devices with their start and end apart: 6, of which 6 were waited for; matrix products, arithmetic and copies ran while one was open for 9% of the time, Pallas kernels for 0%

profile of v1, /device:TPU:1, one launch (start us, length us, event | category | flops | bytes accessed | tf_op | source)
XLA Modules:
  0.0 148.3 jit_solution(1486465929367733724)
XLA Ops:
  0.9 1.4 convolution_bitcast_fusion.2
  4.3 0.8 pad_maximum_fusion.3
  5.1 18.0 %all-to-all-start = ((bf16[128,1,4,128]{3,2,1,0:T(4,128)(2,1)}), bf16[128,1,4,128]{3,2,1,0:T(4,128)(2,1)S(1)}, u32[]{:S(2)}, u32[]{:S(2)}) async-start(bf16[128,1,4,128]{3,2,1,0:T(4,128)(2,1)} %bitcast.18), calls=%async_computation | async-start | bytes 262144 | tf_op jit(solution)/shard_map/all_to_all | solution.py:160
  23.1 1.0 reshape_squeeze.3
  24.6 9.5 %all-to-all-done = bf16[128,1,4,128]{3,2,1,0:T(4,128)(2,1)S(1)} async-done(((bf16[128,1,4,128]{3,2,1,0:T(4,128)(2,1)}), bf16[128,1,4,128]{3,2,1,0:T(4,128)(2,1)S(1)}, u32[]{:S(2)}, u32[]{:S(2)}) %all-to-all-start) | async-done | bytes 131104 | tf_op jit(solution)/shard_map/all_to_all | solution.py:160
  38.0 17.1 %all-to-all-start.4 = ((bf16[1,32,4,128]{3,2,0,1:T(4,128)(2,1)}), bf16[1,32,4,128]{3,2,0,1:T(4,128)(2,1)S(1)}, u32[]{:S(2)}, u32[]{:S(2)}) async-start(bf16[1,32,4,128]{3,2,0,1:T(4,128)(2,1)} %copy.87), calls=%async_computation.4 | async-start | bytes 65536 | tf_op jit(solution)/shard_map/all_to_all | solution.py:207
  55.1 0.8 copy.75
  55.9 6.4 %all-to-all-done.4 = bf16[1,32,4,128]{3,2,0,1:T(4,128)(2,1)S(1)} async-done(((bf16[1,32,4,128]{3,2,0,1:T(4,128)(2,1)}), bf16[1,32,4,128]{3,2,0,1:T(4,128)(2,1)S(1)}, u32[]{:S(2)}, u32[]{:S(2)}) %all-to-all-start.4) | async-done | bytes 32800 | tf_op jit(solution)/shard_map/all_to_all | solution.py:207
  62.3 6.4 %all-to-all-start.1 = ((bf16[128,1,4,128]{3,2,1,0:T(4,128)(2,1)}), bf16[128,1,4,128]{3,2,1,0:T(4,128)(2,1)S(1)}, u32[]{:S(2)}, u32[]{:S(2)}) async-start(bf16[128,1,4,128]{3,2,1,0:T(4,128)(2,1)} %copy.75), calls=%async_computation.1 | async-start | bytes 262144 | tf_op jit(solution)/shard_map/all_to_all | solution.py:160
  68.6 1.4 convolution_bitcast_fusion
  70.0 1.3 copy.76
  71.3 2.3 %reshape.394 = f32[256,1024]{1,0:T(8,128)} reshape(f32[2048,128]{1,0:T(8,128)} %copy.76) | data formatting | bytes 2097152 | tf_op jit(solution)/shard_map/reshape | solution.py:139
  73.7 5.8 %all-to-all-done.1 = bf16[128,1,4,128]{3,2,1,0:T(4,128)(2,1)S(1)} async-done(((bf16[128,1,4,128]{3,2,1,0:T(4,128)(2,1)}), bf16[128,1,4,128]{3,2,1,0:T(4,128)(2,1)S(1)}, u32[]{:S(2)}, u32[]{:S(2)}) %all-to-all-start.1) | async-done | bytes 131104 | tf_op jit(solution)/shard_map/all_to_all | solution.py:160
  81.0 4.0 %fusion.22 = (bf16[256,1024]{1,0:T(8,128)(2,1)S(1)}, bf16[1,1,256,1024]{3,2,1,0:T(8,128)(2,1)}) fusion(bf16[1,1,256,1024]{3,2,1,0:T(8,128)(2,1)} %param.5, f32[256,1024]{1,0:T(8,128)} %reshape.394, f32[64,1024]{1,0:T(8,128)S(1)} %reshape.393, f32[32,256]{1,0:T(8,128)S(1)} %get-tuple-element.26, f32[32,256]{1,0:T(8,128)S(1)} %get-tuple-element.25), kind=kOutput, calls=%fused_computation.39 | convolution fusion | flops 207634432 | bytes 2949120 | tf_op jit(solution)/shard_map/pfq,fy->pyq/dot_general | solution.py:106
  87.4 0.8 pad_maximum_fusion.5
  88.2 8.1 %all-to-all-start.2 = ((bf16[128,1,4,128]{3,2,1,0:T(4,128)(2,1)}), bf16[128,1,4,128]{3,2,1,0:T(4,128)(2,1)S(1)}, u32[]{:S(2)}, u32[]{:S(2)}) async-start(bf16[128,1,4,128]{3,2,1,0:T(4,128)(2,1)} %bitcast.59), calls=%async_computation.2 | async-start | bytes 262144 | tf_op jit(solution)/shard_map/all_to_all | solution.py:160
  96.4 1.3 fusion.262
  97.6 1.4 reshape.403
  99.0 8.4 %all-to-all-done.2 = bf16[128,1,4,128]{3,2,1,0:T(4,128)(2,1)S(1)} async-done(((bf16[128,1,4,128]{3,2,1,0:T(4,128)(2,1)}), bf16[128,1,4,128]{3,2,1,0:T(4,128)(2,1)S(1)}, u32[]{:S(2)}, u32[]{:S(2)}) %all-to-all-start.2) | async-done | bytes 131104 | tf_op jit(solution)/shard_map/all_to_all | solution.py:160
  108.4 1.2 fusion.57
  109.8 1.2 fusion.55
  111.4 1.0 fusion.69
  113.1 5.6 %all-to-all-start.5 = ((bf16[1,32,4,128]{3,2,0,1:T(4,128)(2,1)}), bf16[1,32,4,128]{3,2,0,1:T(4,128)(2,1)S(1)}, u32[]{:S(2)}, u32[]{:S(2)}) async-start(bf16[1,32,4,128]{3,2,0,1:T(4,128)(2,1)} %copy.90), calls=%async_computation.5 | async-start | bytes 65536 | tf_op jit(solution)/shard_map/all_to_all | solution.py:208
  118.8 1.0 fusion.47
  119.8 0.8 copy.85
  120.6 5.4 %all-to-all-done.5 = bf16[1,32,4,128]{3,2,0,1:T(4,128)(2,1)S(1)} async-done(((bf16[1,32,4,128]{3,2,0,1:T(4,128)(2,1)}), bf16[1,32,4,128]{3,2,0,1:T(4,128)(2,1)S(1)}, u32[]{:S(2)}, u32[]{:S(2)}) %all-to-all-start.5) | async-done | bytes 32800 | tf_op jit(solution)/shard_map/all_to_all | solution.py:208
  126.0 6.4 %all-to-all-start.3 = ((bf16[128,1,4,128]{3,2,1,0:T(4,128)(2,1)}), bf16[128,1,4,128]{3,2,1,0:T(4,128)(2,1)S(1)}, u32[]{:S(2)}, u32[]{:S(2)}) async-start(bf16[128,1,4,128]{3,2,1,0:T(4,128)(2,1)} %copy.85), calls=%async_computation.3 | async-start | bytes 262144 | tf_op jit(solution)/shard_map/all_to_all | solution.py:160
  133.7 1.0 pad_maximum_fusion.2
  134.7 8.5 %all-to-all-done.3 = bf16[128,1,4,128]{3,2,1,0:T(4,128)(2,1)S(1)} async-done(((bf16[128,1,4,128]{3,2,1,0:T(4,128)(2,1)}), bf16[128,1,4,128]{3,2,1,0:T(4,128)(2,1)S(1)}, u32[]{:S(2)}, u32[]{:S(2)}) %all-to-all-start.3) | async-done | bytes 131104 | tf_op jit(solution)/shard_map/all_to_all | solution.py:160
  144.5 0.8 pad_maximum_fusion.1
  145.3 1.2 reshape.401
  146.5 1.8 %fusion.3 = bf16[1,1,256,1024]{3,2,1,0:T(8,128)(2,1)} fusion(f32[256,1024]{1,0:T(8,128)S(1)} %reshape.403, f32[64,1024]{1,0:T(8,128)S(1)} %reshape.401, f32[32,256]{1,0:T(8,128)S(1)} %get-tuple-element.26, f32[32,256]{1,0:T(8,128)S(1)} %get-tuple-element.25), kind=kOutput, calls=%fused_computation.8 | convolution fusion | flops 202129408 | bytes 1900544 | tf_op jit(solution)/shard_map/pfq,fy->pyq/dot_general | solution.py:106
  (74 shorter events, 15.2 us)
Async XLA Ops:
  0.6 34.4 %copy-start = (bf16[32,4,64,128]{3,2,1,0:T(8,128)(2,1)S(1)}, bf16[32,4,64,128]{3,2,1,0:T(8,128)(2,1)}, u32[]{:S(2)}) copy-start(bf16[32,4,64,128]{3,2,1,0:T(8,128)(2,1)} %param.6) | copy-start | bytes 6291460
  2.3 20.8 %copy-start.1 = (bf16[1,1,256,1024]{3,2,1,0:T(8,128)(2,1)S(1)}, bf16[1,1,256,1024]{3,2,1,0:T(8,128)(2,1)}, u32[]{:S(2)}) copy-start(bf16[1,1,256,1024]{3,2,1,0:T(8,128)(2,1)} %param.4) | copy-start | bytes 1572868
  2.4 21.7 %copy-start.2 = (bf16[64,64]{1,0:T(8,128)(2,1)S(1)}, bf16[64,64]{1,0:T(8,128)(2,1)}, u32[]{:S(2)}) copy-start(bf16[64,64]{1,0:T(8,128)(2,1)} %param.7) | copy-start | bytes 24580
  5.1 29.0 %all-to-all-start = ((bf16[128,1,4,128]{3,2,1,0:T(4,128)(2,1)}), bf16[128,1,4,128]{3,2,1,0:T(4,128)(2,1)S(1)}, u32[]{:S(2)}, u32[]{:S(2)}) async-start(bf16[128,1,4,128]{3,2,1,0:T(4,128)(2,1)} %bitcast.18), calls=%async_computation | async-start | bytes 262144 | tf_op jit(solution)/shard_map/all_to_all | solution.py:160
  38.0 24.3 %all-to-all-start.4 = ((bf16[1,32,4,128]{3,2,0,1:T(4,128)(2,1)}), bf16[1,32,4,128]{3,2,0,1:T(4,128)(2,1)S(1)}, u32[]{:S(2)}, u32[]{:S(2)}) async-start(bf16[1,32,4,128]{3,2,0,1:T(4,128)(2,1)} %copy.87), calls=%async_computation.4 | async-start | bytes 65536 | tf_op jit(solution)/shard_map/all_to_all | solution.py:207
  62.3 17.2 %all-to-all-start.1 = ((bf16[128,1,4,128]{3,2,1,0:T(4,128)(2,1)}), bf16[128,1,4,128]{3,2,1,0:T(4,128)(2,1)S(1)}, u32[]{:S(2)}, u32[]{:S(2)}) async-start(bf16[128,1,4,128]{3,2,1,0:T(4,128)(2,1)} %copy.75), calls=%async_computation.1 | async-start | bytes 262144 | tf_op jit(solution)/shard_map/all_to_all | solution.py:160
  88.2 19.2 %all-to-all-start.2 = ((bf16[128,1,4,128]{3,2,1,0:T(4,128)(2,1)}), bf16[128,1,4,128]{3,2,1,0:T(4,128)(2,1)S(1)}, u32[]{:S(2)}, u32[]{:S(2)}) async-start(bf16[128,1,4,128]{3,2,1,0:T(4,128)(2,1)} %bitcast.59), calls=%async_computation.2 | async-start | bytes 262144 | tf_op jit(solution)/shard_map/all_to_all | solution.py:160
  113.1 12.9 %all-to-all-start.5 = ((bf16[1,32,4,128]{3,2,0,1:T(4,128)(2,1)}), bf16[1,32,4,128]{3,2,0,1:T(4,128)(2,1)S(1)}, u32[]{:S(2)}, u32[]{:S(2)}) async-start(bf16[1,32,4,128]{3,2,0,1:T(4,128)(2,1)} %copy.90), calls=%async_computation.5 | async-start | bytes 65536 | tf_op jit(solution)/shard_map/all_to_all | solution.py:208
  126.0 17.2 %all-to-all-start.3 = ((bf16[128,1,4,128]{3,2,1,0:T(4,128)(2,1)}), bf16[128,1,4,128]{3,2,1,0:T(4,128)(2,1)S(1)}, u32[]{:S(2)}, u32[]{:S(2)}) async-start(bf16[128,1,4,128]{3,2,1,0:T(4,128)(2,1)} %copy.85), calls=%async_computation.3 | async-start | bytes 262144 | tf_op jit(solution)/shard_map/all_to_all | solution.py:160

commit v2 on v1

v2 whole, which is shorter than its diff:
```python
import math

import jax
import jax.numpy as jnp
import numpy as np
from jax import lax
from jax.experimental import pallas as pl
from jax.experimental.pallas import tpu as pltpu
from jax.sharding import PartitionSpec as P

KY = 32
KZ = 16
GELU_COEF = 0.044715
VMEM_BYTES = 40 << 20


def angles(freq_count, grid_count):
    frequency = np.arange(freq_count) - freq_count // 2
    turn_index = np.mod(frequency[:, None] * np.arange(grid_count)[None, :], grid_count)
    return turn_index.astype(np.float32) * np.float32(2.0 * math.pi / grid_count)


def tables_y(y_count):
    theta = angles(KY, y_count)
    return np.concatenate([np.cos(theta), -np.sin(theta)], 0).astype(np.float32)


def forward_table_y(y_count):
    return tables_y(y_count).astype(jnp.bfloat16)


def inverse_table_y(y_count):
    table = tables_y(y_count).T
    high = table.astype(jnp.bfloat16)
    low = (table - high.astype(np.float32)).astype(jnp.bfloat16)
    return np.concatenate([high, high, low], 1)


def tables_x(kx_count, x_length, mode_block):
    theta = angles(kx_count, x_length)
    same = np.eye(mode_block, dtype=np.float32)
    cos_wide = np.kron(np.cos(theta), same)
    sin_wide = np.kron(np.sin(theta), same)
    forward = np.concatenate([cos_wide, sin_wide], 0).astype(jnp.bfloat16)
    inverse = np.concatenate([cos_wide.T, sin_wide.T], 1).astype(jnp.bfloat16)
    return forward, inverse


def dot(left, right):
    return jnp.dot(left, right, preferred_element_type=jnp.float32)


def lanes_of(shape):
    return lax.broadcasted_iota(jnp.int32, shape, 1)


def halves_swapped(pair):
    return pltpu.roll(pair, pair.shape[1] // 2, 1)


def quarter_turn(pair, sign):
    low = lanes_of(pair.shape) < pair.shape[1] // 2
    swapped = halves_swapped(pair)
    return jnp.where(low, -swapped, swapped) if sign > 0 else jnp.where(low, swapped, -swapped)


def fourier(parts, sign):
    count = len(parts)
    if count == 1:
        return parts
    even = fourier(parts[0::2], sign)
    odd = fourier(parts[1::2], sign)
    lower, upper = [], []
    for k in range(count // 2):
        turned = odd[k]
        if 4 * k == count:
            turned = quarter_turn(turned, sign)
        elif k:
            angle = 2.0 * math.pi * k / count
            turned = math.cos(angle) * turned + math.sin(angle) * quarter_turn(turned, sign)
        lower.append(even[k] + turned)
        upper.append(even[k] - turned)
    return lower + upper


def modes_from(first_pass, wide_modes, modes_out):
    width = modes_out.shape[1]
    low = lanes_of((8, width)) < width // 2
    for block in range(KY // 8):
        parts = []
        for column in range(KZ // 2):
            lanes = pl.ds(column * width, width)
            real = first_pass[pl.ds(block * 8, 8), lanes]
            imag = first_pass[pl.ds(KY + block * 8, 8), lanes]
            parts.append(jnp.where(low, real, halves_swapped(imag)))
            parts.append(jnp.where(low, halves_swapped(real), imag))
        spectrum = fourier(parts, -1)
        for kz in range(KZ):
            wide_modes[pl.ds(block * 8 * KZ + kz, 8, stride=KZ), :] = spectrum[(kz + KZ // 2) % KZ]
    modes_out[...] = wide_modes[...].astype(modes_out.dtype)


def stacked_from(planes, wide_modes, stacked, norm_scale):
    width = planes.shape[1]
    low = lanes_of((8, width)) < width // 2
    wide_modes[...] = planes[...].astype(jnp.float32)
    for block in range(KY // 8):
        parts = [
            wide_modes[pl.ds(block * 8 * KZ + (k + KZ // 2) % KZ, 8, stride=KZ), :] for k in range(KZ)
        ]
        grid = fourier(parts, 1)
        for column in range(KZ // 2):
            lanes = pl.ds(column * width, width)
            first = grid[2 * column] * norm_scale
            second = grid[2 * column + 1] * norm_scale
            stacked[pl.ds(block * 8, 8), lanes] = jnp.where(low, first, halves_swapped(second))
            stacked[pl.ds(KY + block * 8, 8), lanes] = jnp.where(low, halves_swapped(first), second)


def three_terms(stacked, lanes):
    value = stacked[:, lanes]
    high = value.astype(jnp.bfloat16)
    low = (value - high.astype(jnp.float32)).astype(jnp.bfloat16)
    return jnp.concatenate([high, low, high], 0)


def forward_yz_kernel(table_y, field, modes_out, first_pass, wide_modes):
    first_pass[...] = dot(table_y[...], field[...])
    modes_from(first_pass, wide_modes, modes_out)


def middle_kernel(
    norm_scale, planes, inverse_y, table_y, paired, field, cotangent,
    modes_out, field_out, out_grad, stacked, first_pass, wide_modes,
):
    stacked_from(planes, wide_modes, stacked, norm_scale)
    root_const = math.sqrt(2.0 / math.pi)
    width = paired.shape[0]
    rows_per = 64
    for column in range(field.shape[1] // width):
        lanes = pl.ds(column * width, width)
        terms = three_terms(stacked, lanes)
        for start in range(0, field.shape[0], rows_per):
            rows = pl.ds(start, rows_per)
            pre_act = dot(inverse_y[rows, :], terms) + dot(field[rows, lanes], paired[...])
            square = pre_act * pre_act
            tangent = jnp.tanh(pre_act * (root_const + root_const * GELU_COEF * square))
            half = 0.5 + 0.5 * tangent
            activated = pre_act * half
            slope = half + activated * (1.0 - tangent) * (root_const + 3.0 * root_const * GELU_COEF * square)
            field_out[rows, lanes] = activated.astype(field_out.dtype)
            out_grad[rows, lanes] = (cotangent[rows, lanes].astype(jnp.float32) * slope).astype(out_grad.dtype)
        first_pass[:, lanes] = dot(table_y[...], out_grad[:, lanes])
    modes_from(first_pass, wide_modes, modes_out)


def last_kernel(norm_scale, planes, inverse_y, paired, out_grad, field_grad, stacked, wide_modes):
    stacked_from(planes, wide_modes, stacked, norm_scale)
    width = paired.shape[0]
    rows_per = 128
    for column in range(out_grad.shape[1] // width):
        lanes = pl.ds(column * width, width)
        terms = three_terms(stacked, lanes)
        for start in range(0, out_grad.shape[0], rows_per):
            rows = pl.ds(start, rows_per)
            grad = dot(inverse_y[rows, :], terms) + dot(out_grad[rows, lanes], paired[...])
            field_grad[rows, lanes] = grad.astype(field_grad.dtype)


def coeffs_of(forward_x, mode_data, norm_scale):
    both = dot(forward_x[...], mode_data[...])
    count = both.shape[0] // 2
    return ((both[:count] + quarter_turn(both[count:], -1)) * norm_scale).astype(jnp.bfloat16)


def planes_of(inverse_x, mixed):
    turned = quarter_turn(mixed.astype(jnp.float32), 1).astype(jnp.bfloat16)
    return dot(inverse_x[...], jnp.concatenate([mixed, turned], 0)).astype(jnp.bfloat16)


def own_block(shape, channels):
    row = lax.broadcasted_iota(jnp.int32, shape, 0)
    return lanes_of(shape) // channels == row % 8


def mixed_forward(coeffs, weights, mixed):
    count, width = coeffs.shape
    channels = width // 2
    mine = own_block((8, 8 * channels), channels)
    low = lanes_of((8, width)) < channels
    for start in range(0, count, 8):
        pair = coeffs[start : start + 8].astype(jnp.float32)
        swapped = halves_swapped(pair)
        real = jnp.where(low, pair, swapped)
        imag = jnp.where(low, swapped, pair)
        spread = jnp.concatenate(
            [jnp.where(mine, jnp.concatenate([part] * 4, 1), 0.0) for part in (real, imag)], 0
        ).astype(jnp.bfloat16)
        both = dot(spread, weights[pl.ds(start * channels, 8 * channels), :])
        mixed[pl.ds(start, 8), :] = both[:8] + quarter_turn(both[8:], 1)


def mixed_backward(coeffs, weights, mixed):
    count, width = coeffs.shape
    channels = width // 2
    mine = own_block((8, 8 * channels), channels)
    low = lanes_of((8, width)) < channels
    for start in range(0, count, 8):
        pair = coeffs[start : start + 8].astype(jnp.float32)
        sides = jnp.concatenate([pair, quarter_turn(pair, -1)], 0).astype(jnp.bfloat16)
        every = lax.dot_general(
            sides,
            weights[pl.ds(start * channels, 8 * channels), :],
            (((1,), (1,)), ((), ())),
            preferred_element_type=jnp.float32,
        )
        folded = []
        for half in (every[:8], every[8:]):
            own = jnp.where(mine, half, 0.0)
            total = sum(own[:, at * width : (at + 1) * width] for at in range(4))
            folded.append(total + halves_swapped(total))
        mixed[pl.ds(start, 8), :] = jnp.where(low, folded[0], folded[1])


def mix_forward_kernel(norm_scale, mode_data, forward_x, inverse_x, weights, coeffs_out, planes_out, mixed):
    coeffs = coeffs_of(forward_x, mode_data, norm_scale)
    coeffs_out[...] = coeffs
    mixed_forward(coeffs, weights, mixed)
    planes_out[...] = planes_of(inverse_x, mixed[...].astype(jnp.bfloat16))


def forward_x_kernel(norm_scale, mode_data, forward_x, coeffs_out):
    coeffs_out[...] = coeffs_of(forward_x, mode_data, norm_scale)


def mix_backward_kernel(coeffs_in, inverse_x, weights, planes_out, mixed):
    mixed_backward(coeffs_in[...], weights, mixed)
    planes_out[...] = planes_of(inverse_x, mixed[...].astype(jnp.bfloat16))


def call(kernel, operands, outs, scratch, name):
    single = isinstance(outs, tuple)
    flat = [outs] if single else list(outs)
    whole = pl.BlockSpec(memory_space=pltpu.VMEM)
    result = pl.pallas_call(
        kernel,
        name=name,
        out_shape=[jax.ShapeDtypeStruct(shape, jnp.bfloat16) for shape in flat],
        in_specs=[whole] * len(operands),
        out_specs=[whole] * len(flat),
        scratch_shapes=[pltpu.VMEM(shape, jnp.float32) for shape in scratch],
        compiler_params=pltpu.CompilerParams(vmem_limit_bytes=VMEM_BYTES),
    )(*operands)
    return result[0] if single else result


def exchange(rows):
    count = lax.axis_size("gx")
    slots = rows.reshape(count, rows.shape[0] // count, rows.shape[1])
    return lax.all_to_all(slots, "gx", split_axis=0, concat_axis=0, tiled=True).reshape(rows.shape)


def sample_sum(left_side, right_side):
    samples, kx_count, mode_block, width = left_side.shape
    channels = width // 2
    left = left_side.reshape(samples, kx_count, mode_block, 2, channels)
    swapped = jnp.concatenate([right_side[..., channels:], -right_side[..., :channels]], -1)
    right = jnp.stack([right_side, swapped], 3)
    return jnp.einsum("skmtc,skmtp->kmcp", left, right, preferred_element_type=jnp.float32)


def on_device(field_in, cotangent, mode_weights, point_weights):
    field = field_in.reshape(field_in.shape[-2:])
    cotangent_rows = cotangent.reshape(field.shape)
    y_count, last_width = field.shape
    channels = point_weights.shape[0]
    kx_count, mode_block = mode_weights.shape[:2]
    x_length = lax.axis_size("gx")
    samples = lax.axis_size("sa")
    z_count = last_width // channels
    norm_scale = 1.0 / math.sqrt(x_length * y_count * z_count)
    width = 2 * channels
    mode_total = KY * KZ
    table_y = forward_table_y(y_count)
    inverse_y = inverse_table_y(y_count)
    forward_x, inverse_x = tables_x(kx_count, x_length, mode_block)
    table_y, inverse_y, forward_x, inverse_x = map(jnp.asarray, (table_y, inverse_y, forward_x, inverse_x))
    weights = mode_weights.reshape(-1, width)
    four = jnp.eye(4, dtype=point_weights.dtype)
    paired = jnp.kron(four, point_weights)
    paired_back = jnp.kron(four, point_weights.T)
    scaled = lambda kernel: lambda *refs: kernel(norm_scale, *refs)
    rows = kx_count * mode_block
    planar = (mode_total, width)
    stacked = (2 * KY, last_width)

    modes = call(forward_yz_kernel, (table_y, field), planar, [stacked, planar], "forward_yz")
    coeffs_in, planes = call(
        scaled(mix_forward_kernel),
        (exchange(modes), forward_x, inverse_x, weights),
        [(rows, width), planar],
        [(rows, width)],
        "mix_forward",
    )
    modes, field_out, out_grad = call(
        scaled(middle_kernel),
        (exchange(planes), inverse_y, table_y, paired, field, cotangent_rows),
        [planar, field.shape, field.shape],
        [stacked, stacked, planar],
        "middle",
    )
    coeffs_grad = call(
        scaled(forward_x_kernel), (exchange(modes), forward_x), (rows, width), [], "forward_x"
    )
    both = jnp.stack([coeffs_in, coeffs_grad], 0).reshape(2, samples, kx_count // samples, mode_block, width)
    shared = lax.all_to_all(both, "sa", split_axis=1, concat_axis=1, tiled=True)
    planes = call(
        mix_backward_kernel, (coeffs_grad, inverse_x, weights), planar, [(rows, width)], "mix_backward"
    )
    field_grad = call(
        scaled(last_kernel),
        (exchange(planes), inverse_y, paired_back, out_grad),
        field.shape,
        [stacked, planar],
        "last",
    )
    weight_grad = sample_sum(shared[0], shared[1])
    return (
        field_out.reshape(field_in.shape),
        field_grad.reshape(field_in.shape),
        weight_grad,
    )


def solution(mesh):
    in_specs = (
        P("sa", "gx", None, None),
        P("sa", "gx", None, None),
        P(None, "gx", None, None),
        P(),
    )
    out_specs = (P("sa", "gx", None, None), P("sa", "gx", None, None), P("sa", "gx", None, None))
    return jax.shard_map(
        on_device, mesh=mesh, in_specs=in_specs, out_specs=out_specs, check_vma=False
    )
```

time: 149 us -> 124 us (0.83)
  blocking collectives: 0 us -> 45.5 us
  starting transfers between devices: 61.6 us -> 31.8 us
  matrix products: 24.1 us -> 1.07 us
  waiting for transfers between devices: 44 us -> 22.8 us
  Pallas kernels: 0 us -> 8.76 us
  other arithmetic: 6.05 us -> 1.9 us
    all_to_all x0 -> x2, blocking collectives: none -> 45.5 us  [exchange(): lax.all_to_all(slots, 'gx', split_axis=0, concat_axis=0, tiled=True)]
    all_to_all x6 -> x3, starting transfers between devices: 61.6 us -> 31.8 us  [the longest x1 19.4 us: on_device(): shared = lax.all_to_all(both, 'sa', split_axis=1, concat_axis=1, tiled=True)]
    dot_general x38 -> x1, matrix products: 24.1 us -> 1.07 us  [sample_sum(): jnp.einsum('skmtc,skmtp->kmcp', left, right, preferred_element_type=jnp.f...]
    all_to_all x6 -> x3, waiting for transfers between devices: 44 us -> 22.8 us  [the longest x2 18.3 us: exchange(): lax.all_to_all(slots, 'gx', split_axis=0, concat_axis=0, tiled=True)]
    pallas_call x0 -> x6, Pallas kernels: none -> 8.76 us  [call(): pl.pallas_call(kernel, name=name, out_shape=[jax.ShapeDtypeStruct(shape,...]
    unnamed x6 -> x35, local copies, waits for them, and re-layouts: 0.02 us -> 7.73 us
    concatenate x12 -> x0, other arithmetic: 4.73 us -> none  [the longest x2 1.53 us: forward_yz(): mode_data = jnp.concatenate([real_out, imag_out], -1)]
    reshape x5 -> x0, local copies, waits for them, and re-layouts: 4.23 us -> none  [the longest x2 3.73 us: pointwise(): jnp.dot(cell_pairs, paired, preferred_element_type=jnp.float32)]
  transfers between devices with their start and end apart: 6 -> 3, of which waited for: 6 -> 3; matrix products, arithmetic and copies ran while one was open for 9% -> 4% of each run, Pallas kernels for 0% -> 1%
where the time goes in v2:
time: 124 us; the launch traced here: 123 us
  blocking collectives  45.5 us (37%)
  starting transfers between devices  31.8 us (26%)
  waiting for transfers between devices  22.8 us (18%)
  local copies, waits for them, and re-layouts  10.4 us (8%)
  Pallas kernels  8.76 us (7%)
  other arithmetic  1.9 us (2%)
    all_to_all x2, blocking collectives, exchange(): lax.all_to_all(slots, 'gx', split_axis=0, concat_axis=0, tiled=True)  45.5 us
    all_to_all x1, starting transfers between devices, on_device(): shared = lax.all_to_all(both, 'sa', split_axis=1, concat_axis=1, tiled=True)  19.4 us
    all_to_all x2, waiting for transfers between devices, exchange(): lax.all_to_all(slots, 'gx', split_axis=0, concat_axis=0, tiled=True)  18.3 us
    all_to_all x2, starting transfers between devices, exchange(): lax.all_to_all(slots, 'gx', split_axis=0, concat_axis=0, tiled=True)  12.5 us
    pallas_call x6, Pallas kernels, call(): pl.pallas_call(kernel, name=name, out_shape=[jax.ShapeDtypeStruct(shape,...  8.76 us
    unnamed x35, local copies, waits for them, and re-layouts  7.73 us
    all_to_all x1, waiting for transfers between devices, on_device(): shared = lax.all_to_all(both, 'sa', split_axis=1, concat_axis=1, tiled=True)  4.54 us
  transfers between devices with their start and end apart: 3, of which 3 were waited for; matrix products, arithmetic and copies ran while one was open for 4% of the time, Pallas kernels for 1%

profile of v2, /device:TPU:1, one launch (start us, length us, event | category | flops | bytes accessed | tf_op | source)
XLA Modules:
  0.0 123.0 jit_solution(133554903855383672)
XLA Ops:
  0.6 1.0 copy-done.2
  1.7 0.8 copy-done.12
  2.4 0.6 forward_yz.1
  3.0 0.0 copy-start.11
  3.0 29.0 %all_to_all.25 = bf16[128,4,128]{2,1,0:T(4,128)(2,1)S(1)} all-to-all(bf16[128,4,128]{2,1,0:T(4,128)(2,1)S(1)} %bitcast.41), channel_id=1, replica_groups=mesh['gx'=128,'sa'=8] {'gx'}, dimensions={0} | all-to-all | bytes 262144 | tf_op jit(solution)/shard_map/all_to_all | solution.py:260
  32.0 1.6 %copy-done = bf16[32,4,64,128]{3,2,1,0:T(8,128)(2,1)S(1)} copy-done((bf16[32,4,64,128]{3,2,1,0:T(8,128)(2,1)S(1)}, bf16[32,4,64,128]{3,2,1,0:T(8,128)(2,1)}, u32[]{:S(2)}) %copy-start) | copy-done | bytes 2097176
  33.6 0.9 copy-done.4
  34.5 0.9 copy-done.6
  35.5 1.9 %mix_forward.1 = (bf16[128,128]{1,0:T(8,128)(2,1)S(1)}, bf16[512,128]{1,0:T(8,128)(2,1)}) custom-call(bf16[512,128]{1,0:T(8,128)(2,1)S(1)} %bitcast.43, bf16[256,512]{1,0:T(8,128)(2,1)S(1)} %copy-done.6, bf16[512,256]{1,0:T(8,128)(2,1)S(1)} %copy-done.4, bf16[8192,128]{1,0:T(8,128)(2,1)S(1)} %bitcast.34), custom_call_target="tpu_custom_call" | custom-call | tf_op jit(solution)/shard_map/mix_forward/pallas_call | solution.py:245
  37.3 0.6 copy-done.14
  37.9 6.3 %all-to-all-start.1 = ((bf16[128,4,128]{2,1,0:T(4,128)(2,1)}), bf16[128,4,128]{2,1,0:T(4,128)(2,1)S(1)}, u32[]{:S(2)}, u32[]{:S(2)}) async-start(bf16[128,4,128]{2,1,0:T(4,128)(2,1)} %bitcast.4), calls=%async_computation.1 | async-start | bytes 262144 | tf_op jit(solution)/shard_map/all_to_all | solution.py:260
  44.3 0.1 copy.21
  44.4 1.1 broadcast_multiply_fusion
  45.4 1.2 mul.44.refs_3_
  46.6 8.7 %all-to-all-done.1 = bf16[128,4,128]{2,1,0:T(4,128)(2,1)S(1)} async-done(((bf16[128,4,128]{2,1,0:T(4,128)(2,1)}), bf16[128,4,128]{2,1,0:T(4,128)(2,1)S(1)}, u32[]{:S(2)}, u32[]{:S(2)}) %all-to-all-start.1) | async-done | bytes 131104 | tf_op jit(solution)/shard_map/all_to_all | solution.py:260
  55.3 1.0 copy-done.8
  56.3 0.8 copy-done.13
  57.1 2.7 %middle.1 = (bf16[512,128]{1,0:T(8,128)(2,1)S(1)}, bf16[256,1024]{1,0:T(8,128)(2,1)}, bf16[256,1024]{1,0:T(8,128)(2,1)S(1)}) custom-call(bf16[512,128]{1,0:T(8,128)(2,1)S(1)} %bitcast.39, bf16[256,192]{1,0:T(8,128)(2,1)S(1)} %copy-done.11, bf16[64,256]{1,0:T(8,128)(2,1)S(1)} %copy-done.13, bf16[256,256]{1,0:T(8,128)(2,1)S(1)} %mul.44.refs_3_, ...), custom_call_target="tpu_custom_call" | custom-call | tf_op jit(solution)/shard_map/middle/pallas_call | solution.py:245
  59.8 16.6 %all_to_all.26 = bf16[128,4,128]{2,1,0:T(4,128)(2,1)S(1)} all-to-all(bf16[128,4,128]{2,1,0:T(4,128)(2,1)S(1)} %bitcast.45), channel_id=1, replica_groups=mesh['gx'=128,'sa'=8] {'gx'}, dimensions={0} | all-to-all | bytes 262144 | tf_op jit(solution)/shard_map/all_to_all | solution.py:260
  76.4 0.3 forward_x.1.coeffs_in
  76.7 0.7 pad_maximum_fusion
  77.4 19.4 %all-to-all-start.4 = ((bf16[2,8,4,4,128]{4,3,2,0,1:T(4,128)(2,1)}), bf16[2,8,4,4,128]{4,3,2,0,1:T(4,128)(2,1)S(1)}, u32[]{:S(2)}, u32[]{:S(2)}) async-start(bf16[2,8,4,4,128]{4,3,2,0,1:T(4,128)(2,1)} %pad_maximum_fusion), calls=%async_computation.4 | async-start | bytes 131072 | tf_op jit(solution)/shard_map/all_to_all | solution.py:316
  96.7 1.2 %mul.47.refs_2_ = bf16[256,256]{1,0:T(8,128)(2,1)S(1)} reshape(bf16[4,64,4,64]{3,2,1,0:T(4,128)(2,1)} %get-tuple-element.19) | data formatting | bytes 262144 | tf_op jit(solution)/shard_map/jit(kron)/mul | solution.py:291
  98.0 1.7 %mix_backward.1 = bf16[512,128]{1,0:T(8,128)(2,1)} custom-call(bf16[128,128]{1,0:T(8,128)(2,1)S(1)} %forward_x.1.coeffs_in, bf16[512,256]{1,0:T(8,128)(2,1)S(1)} %copy-done.5, bf16[8192,128]{1,0:T(8,128)(2,1)S(1)} %bitcast.35), custom_call_target="tpu_custom_call" | custom-call | tf_op jit(solution)/shard_map/mix_backward/pallas_call | solution.py:245
  99.7 4.5 %all-to-all-done.4 = bf16[2,8,4,4,128]{4,3,2,0,1:T(4,128)(2,1)S(1)} async-done(((bf16[2,8,4,4,128]{4,3,2,0,1:T(4,128)(2,1)}), bf16[2,8,4,4,128]{4,3,2,0,1:T(4,128)(2,1)S(1)}, u32[]{:S(2)}, u32[]{:S(2)}) %all-to-all-start.4) | async-done | bytes 65568 | tf_op jit(solution)/shard_map/all_to_all | solution.py:316
  104.2 6.2 %all-to-all-start.3 = ((bf16[128,4,128]{2,1,0:T(4,128)(2,1)}), bf16[128,4,128]{2,1,0:T(4,128)(2,1)S(1)}, u32[]{:S(2)}, u32[]{:S(2)}) async-start(bf16[128,4,128]{2,1,0:T(4,128)(2,1)} %bitcast.10), calls=%async_computation.3 | async-start | bytes 262144 | tf_op jit(solution)/shard_map/all_to_all | solution.py:260
  110.5 0.1 fusion.7
  110.5 0.1 reshape.83
  110.6 0.1 maximum_bitcast_fusion
  110.7 1.1 convolution_bitcast_fusion
  111.8 9.6 %all-to-all-done.3 = bf16[128,4,128]{2,1,0:T(4,128)(2,1)S(1)} async-done(((bf16[128,4,128]{2,1,0:T(4,128)(2,1)}), bf16[128,4,128]{2,1,0:T(4,128)(2,1)S(1)}, u32[]{:S(2)}, u32[]{:S(2)}) %all-to-all-start.3) | async-done | bytes 131104 | tf_op jit(solution)/shard_map/all_to_all | solution.py:260
  121.4 1.6 %last.1 = bf16[256,1024]{1,0:T(8,128)(2,1)} custom-call(bf16[512,128]{1,0:T(8,128)(2,1)S(1)} %bitcast.42, bf16[256,192]{1,0:T(8,128)(2,1)S(1)} %copy-done.11, bf16[256,256]{1,0:T(8,128)(2,1)S(1)} %mul.47.refs_2_, bf16[256,1024]{1,0:T(8,128)(2,1)S(1)} %copy-done.10), custom_call_target="tpu_custom_call" | custom-call | tf_op jit(solution)/shard_map/last/pallas_call | solution.py:245
  (28 shorter events, 0.1 us)
Async XLA Ops:
  0.6 1.0 copy-start.2
  1.7 0.8 copy-start.12
  2.4 41.8 %copy-start.16 = (bf16[64,64]{1,0:T(8,128)(2,1)S(1)}, bf16[64,64]{1,0:T(8,128)(2,1)}, u32[]{:S(2)}) copy-start(bf16[64,64]{1,0:T(8,128)(2,1)} %param.11) | copy-start | bytes 24580
  2.4 52.8 %copy-start.3 = (bf16[1,1,256,1024]{3,2,1,0:T(8,128)(2,1)S(1)}, bf16[1,1,256,1024]{3,2,1,0:T(8,128)(2,1)}, u32[]{:S(2)}) copy-start(bf16[1,1,256,1024]{3,2,1,0:T(8,128)(2,1)} %param.8) | copy-start | bytes 1572868
  3.0 52.3 %copy-start.11 = (bf16[256,192]{1,0:T(8,128)(2,1)S(1)}, bf16[256,192]{1,0:T(8,128)(2,1)}, u32[]{:S(2)}) copy-start(bf16[256,192]{1,0:T(8,128)(2,1)} %constant.9.clone.refs_1_) | copy-start | bytes 294916
  32.0 1.6 %copy-start = (bf16[32,4,64,128]{3,2,1,0:T(8,128)(2,1)S(1)}, bf16[32,4,64,128]{3,2,1,0:T(8,128)(2,1)}, u32[]{:S(2)}) copy-start(bf16[32,4,64,128]{3,2,1,0:T(8,128)(2,1)} %param.10) | copy-start | bytes 6291460
  33.6 0.9 copy-start.4
  34.5 0.9 copy-start.6
  37.3 0.6 copy-start.14
  37.9 38.4 %copy-start.7 = (bf16[256,512]{1,0:T(8,128)(2,1)S(1)}, bf16[256,512]{1,0:T(8,128)(2,1)}, u32[]{:S(2)}) copy-start(bf16[256,512]{1,0:T(8,128)(2,1)} %constant.10.clone.refs_1_) | copy-start | bytes 786436
  37.9 60.1 %copy-start.1 = (bf16[32,4,64,128]{3,2,1,0:T(8,128)(2,1)S(1)}, bf16[32,4,64,128]{3,2,1,0:T(8,128)(2,1)}, u32[]{:S(2)}) copy-start(bf16[32,4,64,128]{3,2,1,0:T(8,128)(2,1)} %param.10) | copy-start | bytes 6291460
  37.9 60.1 %copy-start.5 = (bf16[512,256]{1,0:T(8,128)(2,1)S(1)}, bf16[512,256]{1,0:T(8,128)(2,1)}, u32[]{:S(2)}) copy-start(bf16[512,256]{1,0:T(8,128)(2,1)} %constant.11.clone.refs_2_.inverse_x) | copy-start | bytes 786436
  37.9 17.3 %all-to-all-start.1 = ((bf16[128,4,128]{2,1,0:T(4,128)(2,1)}), bf16[128,4,128]{2,1,0:T(4,128)(2,1)S(1)}, u32[]{:S(2)}, u32[]{:S(2)}) async-start(bf16[128,4,128]{2,1,0:T(4,128)(2,1)} %bitcast.4), calls=%async_computation.1 | async-start | bytes 262144 | tf_op jit(solution)/shard_map/all_to_all | solution.py:260
  55.3 1.0 copy-start.8
  56.3 0.8 copy-start.13
  57.1 19.6 %copy-start.15 = (bf16[128,128]{1,0:T(8,128)(2,1)S(1)}, bf16[128,128]{1,0:T(8,128)(2,1)}, u32[]{:S(2)}) copy-start(bf16[128,128]{1,0:T(8,128)(2,1)} %copy-done.14) | copy-start | bytes 98308
  59.8 16.9 %copy-start.9 = (bf16[256,1024]{1,0:T(8,128)(2,1)}, bf16[256,1024]{1,0:T(8,128)(2,1)S(1)}, u32[]{:S(2)}) copy-start(bf16[256,1024]{1,0:T(8,128)(2,1)S(1)} %get-tuple-element.11.refs_3_) | copy-start | bytes 1572868
  77.4 26.9 %all-to-all-start.4 = ((bf16[2,8,4,4,128]{4,3,2,0,1:T(4,128)(2,1)}), bf16[2,8,4,4,128]{4,3,2,0,1:T(4,128)(2,1)S(1)}, u32[]{:S(2)}, u32[]{:S(2)}) async-start(bf16[2,8,4,4,128]{4,3,2,0,1:T(4,128)(2,1)} %pad_maximum_fusion), calls=%async_computation.4 | async-start | bytes 131072 | tf_op jit(solution)/shard_map/all_to_all | solution.py:316
  96.7 24.7 %copy-start.10 = (bf16[256,1024]{1,0:T(8,128)(2,1)S(1)}, bf16[256,1024]{1,0:T(8,128)(2,1)}, u32[]{:S(2)}) copy-start(bf16[256,1024]{1,0:T(8,128)(2,1)} %copy-done.9) | copy-start | bytes 1572868
  104.2 17.2 %all-to-all-start.3 = ((bf16[128,4,128]{2,1,0:T(4,128)(2,1)}), bf16[128,4,128]{2,1,0:T(4,128)(2,1)S(1)}, u32[]{:S(2)}, u32[]{:S(2)}) async-start(bf16[128,4,128]{2,1,0:T(4,128)(2,1)} %bitcast.10), calls=%async_computation.3 | async-start | bytes 262144 | tf_op jit(solution)/shard_map/all_to_all | solution.py:260

commit v3 on v2

--- a/solution.py
+++ b/solution.py
@@ -36,14 +36,12 @@
     return np.concatenate([high, high, low], 1)
 
 
-def tables_x(kx_count, x_length, mode_block):
+def table_x(kx_count, x_length, mode_block):
     theta = angles(kx_count, x_length)
     same = np.eye(mode_block, dtype=np.float32)
     cos_wide = np.kron(np.cos(theta), same)
     sin_wide = np.kron(np.sin(theta), same)
-    forward = np.concatenate([cos_wide, sin_wide], 0).astype(jnp.bfloat16)
-    inverse = np.concatenate([cos_wide.T, sin_wide.T], 1).astype(jnp.bfloat16)
-    return forward, inverse
+    return np.concatenate([cos_wide, sin_wide], 0).astype(jnp.bfloat16)
 
 
 def dot(left, right):
@@ -167,15 +165,20 @@
             field_grad[rows, lanes] = grad.astype(field_grad.dtype)
 
 
-def coeffs_of(forward_x, mode_data, norm_scale):
-    both = dot(forward_x[...], mode_data[...])
+def coeffs_of(along_x, mode_data, norm_scale):
+    both = dot(along_x[...], mode_data[...])
     count = both.shape[0] // 2
     return ((both[:count] + quarter_turn(both[count:], -1)) * norm_scale).astype(jnp.bfloat16)
 
 
-def planes_of(inverse_x, mixed):
+def planes_of(along_x, mixed):
     turned = quarter_turn(mixed.astype(jnp.float32), 1).astype(jnp.bfloat16)
-    return dot(inverse_x[...], jnp.concatenate([mixed, turned], 0)).astype(jnp.bfloat16)
+    return lax.dot_general(
+        along_x[...],
+        jnp.concatenate([mixed, turned], 0),
+        (((0,), (0,)), ((), ())),
+        preferred_element_type=jnp.float32,
+    ).astype(jnp.bfloat16)
 
 
 def own_block(shape, channels):
@@ -222,20 +225,20 @@
         mixed[pl.ds(start, 8), :] = jnp.where(low, folded[0], folded[1])
 
 
-def mix_forward_kernel(norm_scale, mode_data, forward_x, inverse_x, weights, coeffs_out, planes_out, mixed):
-    coeffs = coeffs_of(forward_x, mode_data, norm_scale)
+def mix_forward_kernel(norm_scale, mode_data, along_x, weights, coeffs_out, planes_out, mixed):
+    coeffs = coeffs_of(along_x, mode_data, norm_scale)
     coeffs_out[...] = coeffs
     mixed_forward(coeffs, weights, mixed)
-    planes_out[...] = planes_of(inverse_x, mixed[...].astype(jnp.bfloat16))
-
-
-def forward_x_kernel(norm_scale, mode_data, forward_x, coeffs_out):
-    coeffs_out[...] = coeffs_of(forward_x, mode_data, norm_scale)
-
-
-def mix_backward_kernel(coeffs_in, inverse_x, weights, planes_out, mixed):
+    planes_out[...] = planes_of(along_x, mixed[...].astype(jnp.bfloat16))
+
+
+def forward_x_kernel(norm_scale, mode_data, along_x, coeffs_out):
+    coeffs_out[...] = coeffs_of(along_x, mode_data, norm_scale)
+
+
+def mix_backward_kernel(coeffs_in, along_x, weights, planes_out, mixed):
     mixed_backward(coeffs_in[...], weights, mixed)
-    planes_out[...] = planes_of(inverse_x, mixed[...].astype(jnp.bfloat16))
+    planes_out[...] = planes_of(along_x, mixed[...].astype(jnp.bfloat16))
 
 
 def call(kernel, operands, outs, scratch, name):
@@ -260,6 +263,23 @@
     return lax.all_to_all(slots, "gx", split_axis=0, concat_axis=0, tiled=True).reshape(rows.shape)
 
 
+def swap_samples(both):
+    count = lax.axis_size("sa")
+    mine = lax.axis_index("sa")
+    core = jnp.bitwise_and(mine, 1)
+    place = jnp.right_shift(mine, 1)
+    blocks = both.reshape((2, count // 2, 2, both.shape[1] // count) + both.shape[2:])
+    kept = lax.dynamic_index_in_dim(blocks, core, 2, keepdims=False)
+    given = lax.dynamic_index_in_dim(blocks, 1 - core, 2, keepdims=False)
+    taken = lax.ppermute(given, "sa", [(i, i ^ 1) for i in range(count)])
+    pair = jnp.stack([kept, taken], 0)
+    arrived = [lax.dynamic_index_in_dim(pair, place, 2, keepdims=False)]
+    for step in range(1, count // 2):
+        block = lax.dynamic_index_in_dim(pair, jnp.bitwise_xor(place, step), 2, keepdims=False)
+        arrived.append(lax.ppermute(block, "sa", [(i, i ^ 2 * step) for i in range(count)]))
+    return jnp.concatenate(arrived, 0)
+
+
 def sample_sum(left_side, right_side):
     samples, kx_count, mode_block, width = left_side.shape
     channels = width // 2
@@ -283,8 +303,8 @@
     mode_total = KY * KZ
     table_y = forward_table_y(y_count)
     inverse_y = inverse_table_y(y_count)
-    forward_x, inverse_x = tables_x(kx_count, x_length, mode_block)
-    table_y, inverse_y, forward_x, inverse_x = map(jnp.asarray, (table_y, inverse_y, forward_x, inverse_x))
+    along_x = table_x(kx_count, x_length, mode_block)
+    table_y, inverse_y, along_x = map(jnp.asarray, (table_y, inverse_y, along_x))
     weights = mode_weights.reshape(-1, width)
     four = jnp.eye(4, dtype=point_weights.dtype)
     paired = jnp.kron(four, point_weights)
@@ -297,7 +317,7 @@
     modes = call(forward_yz_kernel, (table_y, field), planar, [stacked, planar], "forward_yz")
     coeffs_in, planes = call(
         scaled(mix_forward_kernel),
-        (exchange(modes), forward_x, inverse_x, weights),
+        (exchange(modes), along_x, weights),
         [(rows, width), planar],
         [(rows, width)],
         "mix_forward",
@@ -310,13 +330,13 @@
         "middle",
     )
     coeffs_grad = call(
-        scaled(forward_x_kernel), (exchange(modes), forward_x), (rows, width), [], "forward_x"
-    )
-    both = jnp.stack([coeffs_in, coeffs_grad], 0).reshape(2, samples, kx_count // samples, mode_block, width)
-    shared = lax.all_to_all(both, "sa", split_axis=1, concat_axis=1, tiled=True)
+        scaled(forward_x_kernel), (exchange(modes), along_x), (rows, width), [], "forward_x"
+    )
     planes = call(
-        mix_backward_kernel, (coeffs_grad, inverse_x, weights), planar, [(rows, width)], "mix_backward"
-    )
+        mix_backward_kernel, (coeffs_grad, along_x, weights), planar, [(rows, width)], "mix_backward"
+    )
+    both = jnp.stack([coeffs_in, coeffs_grad], 0).reshape(2, kx_count, mode_block, width)
+    shared = swap_samples(both)
     field_grad = call(
         scaled(last_kernel),
         (exchange(planes), inverse_y, paired_back, out_grad),
@@ -324,7 +344,8 @@
         [stacked, planar],
         "last",
     )
-    weight_grad = sample_sum(shared[0], shared[1])
+    shared, field_grad = lax.optimization_barrier((shared, field_grad))
+    weight_grad = sample_sum(shared[:, 0], shared[:, 1])
     return (
         field_out.reshape(field_in.shape),
         field_grad.reshape(field_in.shape),

time: 124 us -> 122 us (0.984)
  blocking collectives: 45.5 us -> 28.8 us
  starting transfers between devices: 31.8 us -> 47.3 us
    ppermute x0 -> x4, starting transfers between devices: none -> 27.5 us  [the longest x3 20.2 us: swap_samples(): lax.ppermute(block, 'sa', [(i, i ^ 2 * step) for i in range(count)])]
    all_to_all x1 -> x0, starting transfers between devices: 19.4 us -> none  [on_device(): shared = lax.all_to_all(both, 'sa', split_axis=1, concat_axis=1, tiled=True)]
    all_to_all x2 -> x1, blocking collectives: 45.5 us -> 28.8 us  [exchange(): lax.all_to_all(slots, 'gx', split_axis=0, concat_axis=0, tiled=True)]
    all_to_all x2 -> x3, starting transfers between devices: 12.5 us -> 19.8 us  [exchange(): lax.all_to_all(slots, 'gx', split_axis=0, concat_axis=0, tiled=True)]
    all_to_all x1 -> x0, waiting for transfers between devices: 4.54 us -> none  [on_device(): shared = lax.all_to_all(both, 'sa', split_axis=1, concat_axis=1, tiled=True)]
    ppermute x0 -> x4, waiting for transfers between devices: none -> 2.3 us  [the longest x3 2.3 us: swap_samples(): lax.ppermute(block, 'sa', [(i, i ^ 2 * step) for i in range(count)])]
    all_to_all x2 -> x3, waiting for transfers between devices: 18.3 us -> 19.3 us  [exchange(): lax.all_to_all(slots, 'gx', split_axis=0, concat_axis=0, tiled=True)]
    unnamed x35 -> x36, local copies, waits for them, and re-layouts: 7.73 us -> 8.72 us
  transfers between devices with their start and end apart: 3 -> 7, of which waited for: 3 -> 3; matrix products, arithmetic and copies ran while one was open for 4% -> 2% of each run, Pallas kernels for 1% -> 1%
where the time goes in v3:
time: 122 us; the launch traced here: 121 us
  starting transfers between devices  47.3 us (39%)
  blocking collectives  28.8 us (24%)
  waiting for transfers between devices  21.6 us (18%)
  local copies, waits for them, and re-layouts  10.4 us (9%)
  Pallas kernels  8.99 us (7%)
  other arithmetic  2.17 us (2%)
    all_to_all x1, blocking collectives, exchange(): lax.all_to_all(slots, 'gx', split_axis=0, concat_axis=0, tiled=True)  28.8 us
    ppermute x3, starting transfers between devices, swap_samples(): lax.ppermute(block, 'sa', [(i, i ^ 2 * step) for i in range(count)])  20.2 us
    all_to_all x3, starting transfers between devices, exchange(): lax.all_to_all(slots, 'gx', split_axis=0, concat_axis=0, tiled=True)  19.8 us
    all_to_all x3, waiting for transfers between devices, exchange(): lax.all_to_all(slots, 'gx', split_axis=0, concat_axis=0, tiled=True)  19.3 us
    pallas_call x6, Pallas kernels, call(): pl.pallas_call(kernel, name=name, out_shape=[jax.ShapeDtypeStruct(shape,...  8.99 us
    unnamed x36, local copies, waits for them, and re-layouts  8.72 us
    ppermute x1, starting transfers between devices, swap_samples(): taken = lax.ppermute(given, 'sa', [(i, i ^ 1) for i in range(count)])  7.27 us
  transfers between devices with their start and end apart: 7, of which 3 were waited for; matrix products, arithmetic and copies ran while one was open for 2% of the time, Pallas kernels for 1%

profile of v3, /device:TPU:1, one launch (start us, length us, event | category | flops | bytes accessed | tf_op | source)
XLA Modules:
  0.0 121.2 jit_solution(9709673952302207492)
XLA Ops:
  0.6 1.0 copy-done.4
  1.7 0.8 copy-done.13
  2.4 0.6 forward_yz.1
  3.0 28.8 %all_to_all.20 = bf16[128,4,128]{2,1,0:T(4,128)(2,1)S(1)} all-to-all(bf16[128,4,128]{2,1,0:T(4,128)(2,1)S(1)} %bitcast.59), channel_id=1, replica_groups=mesh['gx'=128,'sa'=8] {'gx'}, dimensions={0} | all-to-all | bytes 262144 | tf_op jit(solution)/shard_map/all_to_all | solution.py:263
  31.8 1.6 %copy-done = bf16[32,4,64,128]{3,2,1,0:T(8,128)(2,1)S(1)} copy-done((bf16[32,4,64,128]{3,2,1,0:T(8,128)(2,1)S(1)}, bf16[32,4,64,128]{3,2,1,0:T(8,128)(2,1)}, u32[]{:S(2)}) %copy-start) | copy-done | bytes 2097176
  33.4 0.9 copy-done.2
  34.4 1.2 mix_forward.1
  35.6 0.6 copy-done.12
  36.2 0.6 copy-done.15
  36.9 7.4 %all-to-all-start.1 = ((bf16[128,4,128]{2,1,0:T(4,128)(2,1)}), bf16[128,4,128]{2,1,0:T(4,128)(2,1)}, u32[]{:S(2)}, u32[]{:S(2)}) async-start(bf16[128,4,128]{2,1,0:T(4,128)(2,1)} %bitcast.63), calls=%async_computation.1 | async-start | bytes 262144 | tf_op jit(solution)/shard_map/all_to_all | solution.py:263
  44.4 1.1 broadcast_multiply_fusion
  45.4 1.2 mul.44.refs_3_
  46.6 8.3 %all-to-all-done.1 = bf16[128,4,128]{2,1,0:T(4,128)(2,1)} async-done(((bf16[128,4,128]{2,1,0:T(4,128)(2,1)}), bf16[128,4,128]{2,1,0:T(4,128)(2,1)}, u32[]{:S(2)}, u32[]{:S(2)}) %all-to-all-start.1) | async-done | bytes 131104 | tf_op jit(solution)/shard_map/all_to_all | solution.py:263
  54.9 0.9 copy-done.9
  55.8 0.8 copy-done.14
  56.6 3.6 %middle.1 = (bf16[512,128]{1,0:T(8,128)(2,1)S(1)}, bf16[256,1024]{1,0:T(8,128)(2,1)}, bf16[256,1024]{1,0:T(8,128)(2,1)S(1)}) custom-call(bf16[512,128]{1,0:T(8,128)(2,1)} %bitcast.5.refs_0_, bf16[256,192]{1,0:T(8,128)(2,1)S(1)} %copy-done.9, bf16[64,256]{1,0:T(8,128)(2,1)S(1)} %copy-done.14, bf16[256,256]{1,0:T(8,128)(2,1)S(1)} %mul.44.refs_3_, ...), custom_call_target="tpu_custom_call" | custom-call | tf_op jit(solution)/shard_map/middle/pallas_call | solution.py:248
  60.2 0.8 copy-done.7
  61.0 0.6 copy-done.11
  61.7 6.3 %all-to-all-start.2 = ((bf16[128,4,128]{2,1,0:T(4,128)(2,1)}), bf16[128,4,128]{2,1,0:T(4,128)(2,1)S(1)}, u32[]{:S(2)}, u32[]{:S(2)}) async-start(bf16[128,4,128]{2,1,0:T(4,128)(2,1)} %bitcast.62), calls=%async_computation.2 | async-start | bytes 262144 | tf_op jit(solution)/shard_map/all_to_all | solution.py:263
  67.9 11.0 %all-to-all-done.2 = bf16[128,4,128]{2,1,0:T(4,128)(2,1)S(1)} async-done(((bf16[128,4,128]{2,1,0:T(4,128)(2,1)}), bf16[128,4,128]{2,1,0:T(4,128)(2,1)S(1)}, u32[]{:S(2)}, u32[]{:S(2)}) %all-to-all-start.2) | async-done | bytes 131104 | tf_op jit(solution)/shard_map/all_to_all | solution.py:263
  79.0 0.3 forward_x.1.coeffs_in
  79.2 0.8 fusion.5
  80.0 7.3 %collective-permute-start = (bf16[2,4,4,4,128]{4,3,2,1,0:T(4,128)(2,1)S(1)}, bf16[2,4,4,4,128]{4,3,2,1,0:T(4,128)(2,1)S(1)}, u32[]{:S(2)}, u32[]{:S(2)}) collective-permute-start(bf16[2,4,4,4,128]{4,3,2,1,0:T(4,128)(2,1)S(1)} %get-tuple-element.24), channel_id=1, source_target_pairs={{0,1},{1,0},{2,3},{3,2},{4,5},{5,4},{6,7},{7,6},{8,9},{9,8},{10,11... | collective-permute-start | bytes 98312 | tf_op jit(solution)/shard_map/ppermute | solution.py:274
  87.3 1.7 %mix_backward.1 = bf16[512,128]{1,0:T(8,128)(2,1)} custom-call(bf16[128,128]{1,0:T(8,128)(2,1)S(1)} %forward_x.1.coeffs_in, bf16[256,512]{1,0:T(8,128)(2,1)S(1)} %copy-done.3, bf16[8192,128]{1,0:T(8,128)(2,1)S(1)} %bitcast.53), custom_call_target="tpu_custom_call" | custom-call | tf_op jit(solution)/shard_map/mix_backward/pallas_call | solution.py:248
  89.0 6.1 %all-to-all-start.3 = ((bf16[128,4,128]{2,1,0:T(4,128)(2,1)}), bf16[128,4,128]{2,1,0:T(4,128)(2,1)S(1)}, u32[]{:S(2)}, u32[]{:S(2)}) async-start(bf16[128,4,128]{2,1,0:T(4,128)(2,1)} %bitcast.19), calls=%async_computation.3 | async-start | bytes 262144 | tf_op jit(solution)/shard_map/all_to_all | solution.py:263
  95.3 14.3 %collective-permute-start.3 = (bf16[2,2,4,4,128]{4,0,3,2,1:T(2,128)(2,1)S(1)}, bf16[2,2,4,4,128]{4,0,3,2,1:T(2,128)(2,1)S(1)}, u32[]{:S(2)}, u32[]{:S(2)}) collective-permute-start(bf16[2,2,4,4,128]{4,0,3,2,1:T(2,128)(2,1)S(1)} %bitcast.71), channel_id=1, source_target_pairs={{0,6},{1,7},{2,4},{3,5},{4,2},{5,3},{6,0},{7,1},{8,14},{9,15},{10,... | collective-permute-start | bytes 49160 | tf_op jit(solution)/shard_map/ppermute | solution.py:279
  109.7 1.9 %collective-permute-start.2 = (bf16[2,2,4,4,128]{4,0,3,2,1:T(2,128)(2,1)S(1)}, bf16[2,2,4,4,128]{4,0,3,2,1:T(2,128)(2,1)S(1)}, u32[]{:S(2)}, u32[]{:S(2)}) collective-permute-start(bf16[2,2,4,4,128]{4,0,3,2,1:T(2,128)(2,1)S(1)} %bitcast.70), channel_id=1, source_target_pairs={{0,4},{1,5},{2,6},{3,7},{4,0},{5,1},{6,2},{7,3},{8,12},{9,13},{10,... | collective-permute-start | bytes 49160 | tf_op jit(solution)/shard_map/ppermute | solution.py:279
  111.6 4.0 %collective-permute-start.1 = (bf16[2,2,4,4,128]{4,0,3,2,1:T(2,128)(2,1)S(1)}, bf16[2,2,4,4,128]{4,0,3,2,1:T(2,128)(2,1)S(1)}, u32[]{:S(2)}, u32[]{:S(2)}) collective-permute-start(bf16[2,2,4,4,128]{4,0,3,2,1:T(2,128)(2,1)S(1)} %bitcast.69), channel_id=1, source_target_pairs={{0,2},{1,3},{2,0},{3,1},{4,6},{5,7},{6,4},{7,5},{8,10},{9,11},{10,... | collective-permute-start | bytes 49160 | tf_op jit(solution)/shard_map/ppermute | solution.py:279
  115.6 0.2 mul.47.refs_2_
  115.8 2.3 %collective-permute-done.2 = bf16[2,2,4,4,128]{4,0,3,2,1:T(2,128)(2,1)S(1)} collective-permute-done((bf16[2,2,4,4,128]{4,0,3,2,1:T(2,128)(2,1)S(1)}, bf16[2,2,4,4,128]{4,0,3,2,1:T(2,128)(2,1)S(1)}, u32[]{:S(2)}, u32[]{:S(2)}) %collective-permute-start.2) | collective-permute-done | bytes 16416 | tf_op jit(solution)/shard_map/ppermute | solution.py:279
  118.3 1.6 %last.1 = bf16[256,1024]{1,0:T(8,128)(2,1)} custom-call(bf16[512,128]{1,0:T(8,128)(2,1)S(1)} %bitcast.60, bf16[256,192]{1,0:T(8,128)(2,1)S(1)} %copy-done.10, bf16[256,256]{1,0:T(8,128)(2,1)S(1)} %mul.47.refs_2_, bf16[256,1024]{1,0:T(8,128)(2,1)S(1)} %copy-done.8), custom_call_target="tpu_custom_call" | custom-call | tf_op jit(solution)/shard_map/last/pallas_call | solution.py:248
  120.2 1.1 convolution_bitcast_fusion
  (42 shorter events, 0.6 us)
Async XLA Ops:
  0.6 1.0 copy-start.4
  1.7 0.8 copy-start.13
  2.4 41.8 %copy-start.17 = (bf16[64,64]{1,0:T(8,128)(2,1)S(1)}, bf16[64,64]{1,0:T(8,128)(2,1)}, u32[]{:S(2)}) copy-start(bf16[64,64]{1,0:T(8,128)(2,1)} %param.10) | copy-start | bytes 24580
  2.4 52.5 %copy-start.5 = (bf16[1,1,256,1024]{3,2,1,0:T(8,128)(2,1)S(1)}, bf16[1,1,256,1024]{3,2,1,0:T(8,128)(2,1)}, u32[]{:S(2)}) copy-start(bf16[1,1,256,1024]{3,2,1,0:T(8,128)(2,1)} %param.7) | copy-start | bytes 1572868
  31.8 1.6 %copy-start = (bf16[32,4,64,128]{3,2,1,0:T(8,128)(2,1)S(1)}, bf16[32,4,64,128]{3,2,1,0:T(8,128)(2,1)}, u32[]{:S(2)}) copy-start(bf16[32,4,64,128]{3,2,1,0:T(8,128)(2,1)} %param.9) | copy-start | bytes 6291460
  33.4 0.9 copy-start.2
  34.4 20.6 %copy-start.6 = (bf16[1,1,256,1024]{3,2,1,0:T(8,128)(2,1)S(1)}, bf16[1,1,256,1024]{3,2,1,0:T(8,128)(2,1)}, u32[]{:S(2)}) copy-start(bf16[1,1,256,1024]{3,2,1,0:T(8,128)(2,1)} %param.8) | copy-start | bytes 1572868
  35.6 0.7 copy-start.12
  36.2 0.6 copy-start.15
  36.8 42.1 %copy-start.3 = (bf16[256,512]{1,0:T(8,128)(2,1)S(1)}, bf16[256,512]{1,0:T(8,128)(2,1)}, u32[]{:S(2)}) copy-start(bf16[256,512]{1,0:T(8,128)(2,1)} %constant.37.clone.refs_1_.along_x) | copy-start | bytes 786436
  36.8 50.5 %copy-start.1 = (bf16[32,4,64,128]{3,2,1,0:T(8,128)(2,1)S(1)}, bf16[32,4,64,128]{3,2,1,0:T(8,128)(2,1)}, u32[]{:S(2)}) copy-start(bf16[32,4,64,128]{3,2,1,0:T(8,128)(2,1)} %param.9) | copy-start | bytes 6291460
  36.9 18.1 %all-to-all-start.1 = ((bf16[128,4,128]{2,1,0:T(4,128)(2,1)}), bf16[128,4,128]{2,1,0:T(4,128)(2,1)}, u32[]{:S(2)}, u32[]{:S(2)}) async-start(bf16[128,4,128]{2,1,0:T(4,128)(2,1)} %bitcast.63), calls=%async_computation.1 | async-start | bytes 262144 | tf_op jit(solution)/shard_map/all_to_all | solution.py:263
  54.9 0.9 copy-start.9
  55.8 0.8 copy-start.14
  60.2 0.8 copy-start.7
  61.0 0.6 copy-start.11
  61.7 53.9 %copy-start.16 = (bf16[4,64,4,64]{3,2,1,0:T(4,128)(2,1)S(1)}, bf16[4,64,4,64]{3,2,1,0:T(4,128)(2,1)}, u32[]{:S(2)}) copy-start(bf16[4,64,4,64]{3,2,1,0:T(4,128)(2,1)} %get-tuple-element.28) | copy-start | bytes 393220
  61.7 17.3 %all-to-all-start.2 = ((bf16[128,4,128]{2,1,0:T(4,128)(2,1)}), bf16[128,4,128]{2,1,0:T(4,128)(2,1)S(1)}, u32[]{:S(2)}, u32[]{:S(2)}) async-start(bf16[128,4,128]{2,1,0:T(4,128)(2,1)} %bitcast.62), calls=%async_computation.2 | async-start | bytes 262144 | tf_op jit(solution)/shard_map/all_to_all | solution.py:263
  79.0 39.3 %copy-start.8 = (bf16[256,1024]{1,0:T(8,128)(2,1)S(1)}, bf16[256,1024]{1,0:T(8,128)(2,1)}, u32[]{:S(2)}) copy-start(bf16[256,1024]{1,0:T(8,128)(2,1)} %copy-done.7) | copy-start | bytes 1572868
  79.0 39.3 %copy-start.10 = (bf16[256,192]{1,0:T(8,128)(2,1)S(1)}, bf16[256,192]{1,0:T(8,128)(2,1)}, u32[]{:S(2)}) copy-start(bf16[256,192]{1,0:T(8,128)(2,1)} %constant.36.clone.refs_1_) | copy-start | bytes 294916
  80.0 15.1 %collective-permute-start = (bf16[2,4,4,4,128]{4,3,2,1,0:T(4,128)(2,1)S(1)}, bf16[2,4,4,4,128]{4,3,2,1,0:T(4,128)(2,1)S(1)}, u32[]{:S(2)}, u32[]{:S(2)}) collective-permute-start(bf16[2,4,4,4,128]{4,3,2,1,0:T(4,128)(2,1)S(1)} %get-tuple-element.24), channel_id=1, source_target_pairs={{0,1},{1,0},{2,3},{3,2},{4,5},{5,4},{6,7},{7,6},{8,9},{9,8},{10,11... | collective-permute-start | bytes 98312 | tf_op jit(solution)/shard_map/ppermute | solution.py:274
  89.0 29.2 %all-to-all-start.3 = ((bf16[128,4,128]{2,1,0:T(4,128)(2,1)}), bf16[128,4,128]{2,1,0:T(4,128)(2,1)S(1)}, u32[]{:S(2)}, u32[]{:S(2)}) async-start(bf16[128,4,128]{2,1,0:T(4,128)(2,1)} %bitcast.19), calls=%async_computation.3 | async-start | bytes 262144 | tf_op jit(solution)/shard_map/all_to_all | solution.py:263
  95.3 20.5 %collective-permute-start.3 = (bf16[2,2,4,4,128]{4,0,3,2,1:T(2,128)(2,1)S(1)}, bf16[2,2,4,4,128]{4,0,3,2,1:T(2,128)(2,1)S(1)}, u32[]{:S(2)}, u32[]{:S(2)}) collective-permute-start(bf16[2,2,4,4,128]{4,0,3,2,1:T(2,128)(2,1)S(1)} %bitcast.71), channel_id=1, source_target_pairs={{0,6},{1,7},{2,4},{3,5},{4,2},{5,3},{6,0},{7,1},{8,14},{9,15},{10,... | collective-permute-start | bytes 49160 | tf_op jit(solution)/shard_map/ppermute | solution.py:279
  109.7 8.5 %collective-permute-start.2 = (bf16[2,2,4,4,128]{4,0,3,2,1:T(2,128)(2,1)S(1)}, bf16[2,2,4,4,128]{4,0,3,2,1:T(2,128)(2,1)S(1)}, u32[]{:S(2)}, u32[]{:S(2)}) collective-permute-start(bf16[2,2,4,4,128]{4,0,3,2,1:T(2,128)(2,1)S(1)} %bitcast.70), channel_id=1, source_target_pairs={{0,4},{1,5},{2,6},{3,7},{4,0},{5,1},{6,2},{7,3},{8,12},{9,13},{10,... | collective-permute-start | bytes 49160 | tf_op jit(solution)/shard_map/ppermute | solution.py:279
  111.6 6.6 %collective-permute-start.1 = (bf16[2,2,4,4,128]{4,0,3,2,1:T(2,128)(2,1)S(1)}, bf16[2,2,4,4,128]{4,0,3,2,1:T(2,128)(2,1)S(1)}, u32[]{:S(2)}, u32[]{:S(2)}) collective-permute-start(bf16[2,2,4,4,128]{4,0,3,2,1:T(2,128)(2,1)S(1)} %bitcast.69), channel_id=1, source_target_pairs={{0,2},{1,3},{2,0},{3,1},{4,6},{5,7},{6,4},{7,5},{8,10},{9,11},{10,... | collective-permute-start | bytes 49160 | tf_op jit(solution)/shard_map/ppermute | solution.py:279

commit v4 on v3

--- a/solution.py
+++ b/solution.py
@@ -11,7 +11,9 @@
 KY = 32
 KZ = 16
 GELU_COEF = 0.044715
-VMEM_BYTES = 40 << 20
+LARGE_BYTES = 56 << 20
+SMALL_BYTES = 16 << 20
+PIECES = 4
 
 
 def angles(freq_count, grid_count):
@@ -81,7 +83,27 @@
     return lower + upper
 
 
-def modes_from(first_pass, wide_modes, modes_out):
+class Fetched:
+    def __init__(self, source, target, semaphores, first, pieces=1, axis=0):
+        size = source.shape[axis] // pieces
+        self.copies = []
+        for at in range(pieces):
+            part = pl.ds(at * size, size)
+            index = (part,) if axis == 0 else (slice(None), part)
+            self.copies.append(
+                pltpu.make_async_copy(source.at[index], target.at[index], semaphores.at[first + at])
+            )
+
+    def start(self, at=None):
+        for copy in self.copies if at is None else self.copies[at : at + 1]:
+            copy.start()
+
+    def wait(self, at=None):
+        for copy in self.copies if at is None else self.copies[at : at + 1]:
+            copy.wait()
+
+
+def modes_from(first_pass, wide_modes, modes_out, store):
     width = modes_out.shape[1]
     low = lanes_of((8, width)) < width // 2
     for block in range(KY // 8):
@@ -95,7 +117,9 @@
         spectrum = fourier(parts, -1)
         for kz in range(KZ):
             wide_modes[pl.ds(block * 8 * KZ + kz, 8, stride=KZ), :] = spectrum[(kz + KZ // 2) % KZ]
-    modes_out[...] = wide_modes[...].astype(modes_out.dtype)
+        rows = pl.ds(block * 8 * KZ, 8 * KZ)
+        modes_out[rows, :] = wide_modes[rows, :].astype(modes_out.dtype)
+        store.start(block)
 
 
 def stacked_from(planes, wide_modes, stacked, norm_scale):
@@ -122,25 +146,72 @@
     return jnp.concatenate([high, low, high], 0)
 
 
-def forward_yz_kernel(table_y, field, modes_out, first_pass, wide_modes):
-    first_pass[...] = dot(table_y[...], field[...])
-    modes_from(first_pass, wide_modes, modes_out)
+def paired_of(point_weights):
+    channels = point_weights.shape[0]
+    wide = jnp.concatenate([point_weights[...].astype(jnp.float32)] * 4, 1)
+    tall = jnp.concatenate([wide] * 4, 0)
+    row = lax.broadcasted_iota(jnp.int32, tall.shape, 0)
+    return jnp.where(row // channels == lanes_of(tall.shape) // channels, tall, 0.0).astype(jnp.bfloat16)
+
+
+def forward_yz_kernel(
+    table_in, field_in, modes_hbm, table_y, field, modes_out, first_pass, wide_modes, semaphores
+):
+    table_fetch = Fetched(table_in, table_y, semaphores, 0)
+    field_fetch = Fetched(field_in, field, semaphores, 1, PIECES, 1)
+    store = Fetched(modes_out, modes_hbm, semaphores, 1 + PIECES, PIECES)
+    table_fetch.start()
+    field_fetch.start()
+    table_fetch.wait()
+    width = field.shape[1] // PIECES
+    for column in range(PIECES):
+        lanes = pl.ds(column * width, width)
+        field_fetch.wait(column)
+        first_pass[:, lanes] = dot(table_y[...], field[:, lanes])
+    modes_from(first_pass, wide_modes, modes_out, store)
+    store.wait()
 
 
 def middle_kernel(
-    norm_scale, planes, inverse_y, table_y, paired, field, cotangent,
-    modes_out, field_out, out_grad, stacked, first_pass, wide_modes,
+    norm_scale,
+    planes_in, inverse_in, table_in, point_in, field_in, cotangent_in,
+    modes_hbm, field_out_hbm, out_grad_hbm,
+    planes, inverse_y, table_y, point_weights, field, cotangent, modes_out, field_out, out_grad,
+    stacked, first_pass, wide_modes, semaphores,
 ):
+    small = [
+        Fetched(source, target, semaphores, at)
+        for at, (source, target) in enumerate(
+            ((planes_in, planes), (inverse_in, inverse_y), (point_in, point_weights), (table_in, table_y))
+        )
+    ]
+    field_fetch = Fetched(field_in, field, semaphores, 4, PIECES, 1)
+    cotangent_fetch = Fetched(cotangent_in, cotangent, semaphores, 4 + PIECES, PIECES, 1)
+    modes_store = Fetched(modes_out, modes_hbm, semaphores, 4 + 2 * PIECES, PIECES)
+    out_store = Fetched(field_out, field_out_hbm, semaphores, 4 + 3 * PIECES, PIECES, 1)
+    grad_store = Fetched(out_grad, out_grad_hbm, semaphores, 4 + 4 * PIECES, PIECES, 1)
+    for fetch in small:
+        fetch.start()
+    for at in range(PIECES):
+        field_fetch.start(at)
+        cotangent_fetch.start(at)
+    small[2].wait()
+    paired = paired_of(point_weights)
+    small[0].wait()
     stacked_from(planes, wide_modes, stacked, norm_scale)
+    small[1].wait()
+    small[3].wait()
     root_const = math.sqrt(2.0 / math.pi)
-    width = paired.shape[0]
+    width = field.shape[1] // PIECES
     rows_per = 64
-    for column in range(field.shape[1] // width):
+    for column in range(PIECES):
         lanes = pl.ds(column * width, width)
         terms = three_terms(stacked, lanes)
+        field_fetch.wait(column)
+        cotangent_fetch.wait(column)
         for start in range(0, field.shape[0], rows_per):
             rows = pl.ds(start, rows_per)
-            pre_act = dot(inverse_y[rows, :], terms) + dot(field[rows, lanes], paired[...])
+            pre_act = dot(inverse_y[rows, :], terms) + dot(field[rows, lanes], paired)
             square = pre_act * pre_act
             tangent = jnp.tanh(pre_act * (root_const + root_const * GELU_COEF * square))
             half = 0.5 + 0.5 * tangent
@@ -148,11 +219,17 @@
             slope = half + activated * (1.0 - tangent) * (root_const + 3.0 * root_const * GELU_COEF * square)
             field_out[rows, lanes] = activated.astype(field_out.dtype)
             out_grad[rows, lanes] = (cotangent[rows, lanes].astype(jnp.float32) * slope).astype(out_grad.dtype)
+        grad_store.start(column)
+        out_store.start(column)
         first_pass[:, lanes] = dot(table_y[...], out_grad[:, lanes])
-    modes_from(first_pass, wide_modes, modes_out)
-
-
-def last_kernel(norm_scale, planes, inverse_y, paired, out_grad, field_grad, stacked, wide_modes):
+    modes_from(first_pass, wide_modes, modes_out, modes_store)
+    grad_store.wait()
+    out_store.wait()
+    modes_store.wait()
+
+
+def last_kernel(norm_scale, planes, inverse_y, point_weights, out_grad, field_grad, stacked, wide_modes):
+    paired = paired_of(point_weights)
     stacked_from(planes, wide_modes, stacked, norm_scale)
     width = paired.shape[0]
     rows_per = 128
@@ -161,8 +238,10 @@
         terms = three_terms(stacked, lanes)
         for start in range(0, out_grad.shape[0], rows_per):
             rows = pl.ds(start, rows_per)
-            grad = dot(inverse_y[rows, :], terms) + dot(out_grad[rows, lanes], paired[...])
-            field_grad[rows, lanes] = grad.astype(field_grad.dtype)
+            mixed = lax.dot_general(
+                out_grad[rows, lanes], paired, (((1,), (1,)), ((), ())), preferred_element_type=jnp.float32
+            )
+            field_grad[rows, lanes] = (dot(inverse_y[rows, :], terms) + mixed).astype(field_grad.dtype)
 
 
 def coeffs_of(along_x, mode_data, norm_scale):
@@ -171,14 +250,18 @@
     return ((both[:count] + quarter_turn(both[count:], -1)) * norm_scale).astype(jnp.bfloat16)
 
 
-def planes_of(along_x, mixed):
-    turned = quarter_turn(mixed.astype(jnp.float32), 1).astype(jnp.bfloat16)
-    return lax.dot_general(
-        along_x[...],
-        jnp.concatenate([mixed, turned], 0),
-        (((0,), (0,)), ((), ())),
-        preferred_element_type=jnp.float32,
-    ).astype(jnp.bfloat16)
+def store_planes(along_x, mixed, planes_out, store):
+    mixed = mixed[...]
+    turned = quarter_turn(mixed.astype(jnp.bfloat16).astype(jnp.float32), 1).astype(jnp.bfloat16)
+    terms = jnp.concatenate([mixed.astype(jnp.bfloat16), turned], 0)
+    size = planes_out.shape[0] // PIECES
+    for piece in range(PIECES):
+        rows = pl.ds(piece * size, size)
+        planes_out[rows, :] = lax.dot_general(
+            along_x[:, rows], terms, (((0,), (0,)), ((), ())), preferred_element_type=jnp.float32
+        ).astype(jnp.bfloat16)
+        store.start(piece)
+    store.wait()
 
 
 def own_block(shape, channels):
@@ -186,12 +269,14 @@
     return lanes_of(shape) // channels == row % 8
 
 
-def mixed_forward(coeffs, weights, mixed):
+def mixed_forward(coeffs, weights, weights_fetch, mixed):
     count, width = coeffs.shape
     channels = width // 2
     mine = own_block((8, 8 * channels), channels)
     low = lanes_of((8, width)) < channels
     for start in range(0, count, 8):
+        if start % (count // PIECES) == 0:
+            weights_fetch.wait(start // (count // PIECES))
         pair = coeffs[start : start + 8].astype(jnp.float32)
         swapped = halves_swapped(pair)
         real = jnp.where(low, pair, swapped)
@@ -203,12 +288,14 @@
         mixed[pl.ds(start, 8), :] = both[:8] + quarter_turn(both[8:], 1)
 
 
-def mixed_backward(coeffs, weights, mixed):
+def mixed_backward(coeffs, weights, weights_fetch, mixed):
     count, width = coeffs.shape
     channels = width // 2
     mine = own_block((8, 8 * channels), channels)
     low = lanes_of((8, width)) < channels
     for start in range(0, count, 8):
+        if start % (count // PIECES) == 0:
+            weights_fetch.wait(start // (count // PIECES))
         pair = coeffs[start : start + 8].astype(jnp.float32)
         sides = jnp.concatenate([pair, quarter_turn(pair, -1)], 0).astype(jnp.bfloat16)
         every = lax.dot_general(
@@ -225,36 +312,108 @@
         mixed[pl.ds(start, 8), :] = jnp.where(low, folded[0], folded[1])
 
 
-def mix_forward_kernel(norm_scale, mode_data, along_x, weights, coeffs_out, planes_out, mixed):
+def mix_forward_kernel(
+    norm_scale,
+    mode_in, along_in, weights_in,
+    coeffs_hbm, planes_hbm,
+    mode_data, along_x, weights, coeffs_out, planes_out, mixed, semaphores,
+):
+    mode_fetch = Fetched(mode_in, mode_data, semaphores, 0)
+    along_fetch = Fetched(along_in, along_x, semaphores, 1)
+    coeffs_store = Fetched(coeffs_out, coeffs_hbm, semaphores, 2)
+    weights_fetch = Fetched(weights_in, weights, semaphores, 3, PIECES)
+    store = Fetched(planes_out, planes_hbm, semaphores, 3 + PIECES, PIECES)
+    mode_fetch.start()
+    along_fetch.start()
+    weights_fetch.start()
+    mode_fetch.wait()
+    along_fetch.wait()
     coeffs = coeffs_of(along_x, mode_data, norm_scale)
     coeffs_out[...] = coeffs
-    mixed_forward(coeffs, weights, mixed)
-    planes_out[...] = planes_of(along_x, mixed[...].astype(jnp.bfloat16))
-
-
-def forward_x_kernel(norm_scale, mode_data, along_x, coeffs_out):
-    coeffs_out[...] = coeffs_of(along_x, mode_data, norm_scale)
-
-
-def mix_backward_kernel(coeffs_in, along_x, weights, planes_out, mixed):
-    mixed_backward(coeffs_in[...], weights, mixed)
-    planes_out[...] = planes_of(along_x, mixed[...].astype(jnp.bfloat16))
+    coeffs_store.start()
+    mixed_forward(coeffs, weights, weights_fetch, mixed)
+    store_planes(along_x, mixed, planes_out, store)
+    coeffs_store.wait()
+
+
+def mix_backward_kernel(
+    norm_scale, samples,
+    core, mode_in, along_in, weights_in, coeffs_in_hbm,
+    kept, given, planes_hbm,
+    mode_data, along_x, weights, coeffs_in, planes_out, mixed, semaphores,
+):
+    mode_fetch = Fetched(mode_in, mode_data, semaphores, 0)
+    along_fetch = Fetched(along_in, along_x, semaphores, 1)
+    coeffs_fetch = Fetched(coeffs_in_hbm, coeffs_in, semaphores, 2)
+    weights_fetch = Fetched(weights_in, weights, semaphores, 3, PIECES)
+    store = Fetched(planes_out, planes_hbm, semaphores, 3 + PIECES, PIECES)
+    mode_fetch.start()
+    along_fetch.start()
+    coeffs_fetch.start()
+    weights_fetch.start()
+    mode_fetch.wait()
+    along_fetch.wait()
+    coeffs = coeffs_of(along_x, mode_data, norm_scale)
+    coeffs_fetch.wait()
+    first_core = core[0] == 0
+    size = coeffs.shape[0] // samples
+    for side, values in enumerate((coeffs_in[...], coeffs)):
+        for place in range(samples // 2):
+            even = values[2 * place * size : (2 * place + 1) * size].astype(jnp.float32)
+            odd = values[(2 * place + 1) * size : (2 * place + 2) * size].astype(jnp.float32)
+            rows = pl.ds((side * (samples // 2) + place) * size, size)
+            kept[rows, :] = jnp.where(first_core, even, odd).astype(jnp.bfloat16)
+            given[rows, :] = jnp.where(first_core, odd, even).astype(jnp.bfloat16)
+    mixed_backward(coeffs, weights, weights_fetch, mixed)
+    store_planes(along_x, mixed, planes_out, store)
 
 
 def call(kernel, operands, outs, scratch, name):
-    single = isinstance(outs, tuple)
-    flat = [outs] if single else list(outs)
-    whole = pl.BlockSpec(memory_space=pltpu.VMEM)
-    result = pl.pallas_call(
+    copied = [pltpu.VMEM(array.shape, array.dtype) for array in operands] + [
+        pltpu.VMEM(shape, jnp.bfloat16) for shape in outs
+    ]
+    return pl.pallas_call(
         kernel,
         name=name,
-        out_shape=[jax.ShapeDtypeStruct(shape, jnp.bfloat16) for shape in flat],
+        out_shape=[jax.ShapeDtypeStruct(shape, jnp.bfloat16) for shape in outs],
+        in_specs=[pl.BlockSpec(memory_space=pl.ANY)] * len(operands),
+        out_specs=[pl.BlockSpec(memory_space=pl.ANY)] * len(outs),
+        scratch_shapes=copied
+        + [pltpu.VMEM(shape, jnp.float32) for shape in scratch]
+        + [pltpu.SemaphoreType.DMA((4 + 5 * PIECES,))],
+        compiler_params=pltpu.CompilerParams(vmem_limit_bytes=LARGE_BYTES),
+    )(*operands)
+
+
+def call_mix_backward(norm_scale, samples, core, operands, rows):
+    whole = pl.BlockSpec(memory_space=pltpu.VMEM)
+    width = operands[0].shape[1]
+    count = operands[3].shape[0]
+    outs = [(count, width), (count, width), operands[0].shape]
+    return pl.pallas_call(
+        lambda *refs: mix_backward_kernel(norm_scale, samples, *refs),
+        name="mix_backward",
+        out_shape=[jax.ShapeDtypeStruct(shape, jnp.bfloat16) for shape in outs],
+        in_specs=[pl.BlockSpec(memory_space=pltpu.SMEM)] + [pl.BlockSpec(memory_space=pl.ANY)] * len(operands),
+        out_specs=[whole, whole, pl.BlockSpec(memory_space=pl.ANY)],
+        scratch_shapes=[pltpu.VMEM(array.shape, array.dtype) for array in operands]
+        + [pltpu.VMEM(outs[2], jnp.bfloat16), pltpu.VMEM(rows, jnp.float32)]
+        + [pltpu.SemaphoreType.DMA((4 + 5 * PIECES,))],
+        compiler_params=pltpu.CompilerParams(vmem_limit_bytes=LARGE_BYTES),
+    )(core, *operands)
+
+
+def call_last(norm_scale, operands, shape, scratch):
+    whole = pl.BlockSpec(memory_space=pltpu.VMEM)
+    return pl.pallas_call(
+        lambda *refs: last_kernel(norm_scale, *refs),
+        name="last",
+        out_shape=jax.ShapeDtypeStruct(shape, jnp.bfloat16),
         in_specs=[whole] * len(operands),
-        out_specs=[whole] * len(flat),
+        out_specs=whole,
         scratch_shapes=[pltpu.VMEM(shape, jnp.float32) for shape in scratch],
-        compiler_params=pltpu.CompilerParams(vmem_limit_bytes=VMEM_BYTES),
+        compiler_params=pltpu.CompilerParams(vmem_limit_bytes=SMALL_BYTES),
     )(*operands)
-    return result[0] if single else result
 
 
 def exchange(rows):
@@ -263,16 +422,12 @@
     return lax.all_to_all(slots, "gx", split_axis=0, concat_axis=0, tiled=True).reshape(rows.shape)
 
 
-def swap_samples(both):
+def swap_samples(kept, given, mine):
     count = lax.axis_size("sa")
-    mine = lax.axis_index("sa")
-    core = jnp.bitwise_and(mine, 1)
+    width = kept.shape[1]
+    taken = lax.ppermute(given, "sa", [(i, i ^ 1) for i in range(count)])
+    pair = jnp.stack([kept, taken], 0).reshape(2, 2, count // 2, -1, width)
     place = jnp.right_shift(mine, 1)
-    blocks = both.reshape((2, count // 2, 2, both.shape[1] // count) + both.shape[2:])
-    kept = lax.dynamic_index_in_dim(blocks, core, 2, keepdims=False)
-    given = lax.dynamic_index_in_dim(blocks, 1 - core, 2, keepdims=False)
-    taken = lax.ppermute(given, "sa", [(i, i ^ 1) for i in range(count)])
-    pair = jnp.stack([kept, taken], 0)
     arrived = [lax.dynamic_index_in_dim(pair, place, 2, keepdims=False)]
     for step in range(1, count // 2):
         block = lax.dynamic_index_in_dim(pair, jnp.bitwise_xor(place, step), 2, keepdims=False)
@@ -306,15 +461,14 @@
     along_x = table_x(kx_count, x_length, mode_block)
     table_y, inverse_y, along_x = map(jnp.asarray, (table_y, inverse_y, along_x))
     weights = mode_weights.reshape(-1, width)
-    four = jnp.eye(4, dtype=point_weights.dtype)
-    paired = jnp.kron(four, point_weights)
-    paired_back = jnp.kron(four, point_weights.T)
     scaled = lambda kernel: lambda *refs: kernel(norm_scale, *refs)
     rows = kx_count * mode_block
     planar = (mode_total, width)
     stacked = (2 * KY, last_width)
-
-    modes = call(forward_yz_kernel, (table_y, field), planar, [stacked, planar], "forward_yz")
+    mine = lax.axis_index("sa")
+    core, field = lax.optimization_barrier((jnp.bitwise_and(mine, 1).reshape(1), field))
+
+    (modes,) = call(forward_yz_kernel, (table_y, field), [planar], [stacked, planar], "forward_yz")
     coeffs_in, planes = call(
         scaled(mix_forward_kernel),
         (exchange(modes), along_x, weights),
@@ -324,25 +478,23 @@
     )
     modes, field_out, out_grad = call(
         scaled(middle_kernel),
-        (exchange(planes), inverse_y, table_y, paired, field, cotangent_rows),
+        (exchange(planes), inverse_y, table_y, point_weights, field, cotangent_rows),
         [planar, field.shape, field.shape],
         [stacked, stacked, planar],
         "middle",
     )
-    coeffs_grad = call(
-        scaled(forward_x_kernel), (exchange(modes), along_x), (rows, width), [], "forward_x"
-    )
-    planes = call(
-        mix_backward_kernel, (coeffs_grad, along_x, weights), planar, [(rows, width)], "mix_backward"
-    )
-    both = jnp.stack([coeffs_in, coeffs_grad], 0).reshape(2, kx_count, mode_block, width)
-    shared = swap_samples(both)
-    field_grad = call(
-        scaled(last_kernel),
-        (exchange(planes), inverse_y, paired_back, out_grad),
-        field.shape,
-        [stacked, planar],
-        "last",
+    kept, given, planes = call_mix_backward(
+        norm_scale,
+        samples,
+        core,
+        (exchange(modes), along_x, weights, coeffs_in),
+        (rows, width),
+    )
+    shared = swap_samples(kept, given, mine).reshape(
+        samples, 2, kx_count // samples, mode_block, width
+    )
+    field_grad = call_last(
+        norm_scale, (exchange(planes), inverse_y, point_weights, out_grad), field.shape, [stacked, planar]
     )
     shared, field_grad = lax.optimization_barrier((shared, field_grad))
     weight_grad = sample_sum(shared[:, 0], shared[:, 1])

time: 122 us -> 123 us (level)
  blocking collectives: 28.8 us -> 65.6 us
  waiting for transfers between devices: 21.6 us -> 2.5 us
  starting transfers between devices: 47.3 us -> 33.6 us
  local copies, waits for them, and re-layouts: 10.4 us -> 0.17 us
  Pallas kernels: 8.99 us -> 17.1 us
    all_to_all x1 -> x3, blocking collectives: 28.8 us -> 65.6 us  [exchange(): lax.all_to_all(slots, 'gx', split_axis=0, concat_axis=0, tiled=True)]
    all_to_all x3 -> x1, waiting for transfers between devices: 19.3 us -> 0.01 us  [exchange(): lax.all_to_all(slots, 'gx', split_axis=0, concat_axis=0, tiled=True)]
    all_to_all x3 -> x1, starting transfers between devices: 19.8 us -> 6.18 us  [exchange(): lax.all_to_all(slots, 'gx', split_axis=0, concat_axis=0, tiled=True)]
    unnamed x36 -> x6, local copies, waits for them, and re-layouts: 8.72 us -> 0.01 us
    pallas_call x0 -> x2, Pallas kernels: none -> 6.16 us  [the longest x1 4.45 us: call_mix_backward(): pl.pallas_call(lambda *refs: mix_backward_kernel(norm_scale, samples, *re...]
    pallas_call x6 -> x3, Pallas kernels: 8.99 us -> 10.9 us  [call(): pl.pallas_call(kernel, name=name, out_shape=[jax.ShapeDtypeStruct(shape,...]
    mul x2 -> x0, local copies, waits for them, and re-layouts: 1.39 us -> none  [the longest x1 1.18 us: on_device(): paired = jnp.kron(four, point_weights)]
    ppermute x3, starting transfers between devices: 20.2 us -> 19 us  [swap_samples(): lax.ppermute(block, 'sa', [(i, i ^ 2 * step) for i in range(count)])]
  transfers between devices with their start and end apart: 7 -> 5, of which waited for: 3 -> 1; matrix products, arithmetic and copies ran while one was open for 2% -> 1% of each run, Pallas kernels for 1% -> 0%
where the time goes in v4:
time: 123 us; the launch traced here: 122 us
  blocking collectives  65.6 us (53%)
  starting transfers between devices  33.6 us (27%)
  Pallas kernels  17.1 us (14%)
  waiting for transfers between devices  2.5 us (2%)
    all_to_all x3, blocking collectives, exchange(): lax.all_to_all(slots, 'gx', split_axis=0, concat_axis=0, tiled=True)  65.6 us
    ppermute x3, starting transfers between devices, swap_samples(): lax.ppermute(block, 'sa', [(i, i ^ 2 * step) for i in range(count)])  19 us
    pallas_call x3, Pallas kernels, call(): pl.pallas_call(kernel, name=name, out_shape=[jax.ShapeDtypeStruct(shape,...  10.9 us
    ppermute x1, starting transfers between devices, swap_samples(): taken = lax.ppermute(given, 'sa', [(i, i ^ 1) for i in range(count)])  8.46 us
    all_to_all x1, starting transfers between devices, exchange(): lax.all_to_all(slots, 'gx', split_axis=0, concat_axis=0, tiled=True)  6.18 us
    pallas_call x1, Pallas kernels, call_mix_backward(): pl.pallas_call(lambda *refs: mix_backward_kernel(norm_scale, samples, *re...  4.45 us
    ppermute x3, waiting for transfers between devices, swap_samples(): lax.ppermute(block, 'sa', [(i, i ^ 2 * step) for i in range(count)])  2.49 us
  transfers between devices with their start and end apart: 5, of which 1 were waited for; matrix products, arithmetic and copies ran while one was open for 1% of the time, Pallas kernels for 0%

profile of v4, /device:TPU:1, one launch (start us, length us, event | category | flops | bytes accessed | tf_op | source)
XLA Modules:
  0.0 122.0 jit_solution(16078811913696329812)
XLA Ops:
  0.6 2.8 %forward_yz.1 = bf16[512,128]{1,0:T(8,128)(2,1)} custom-call(bf16[64,256]{1,0:T(8,128)(2,1)} %constant.28.clone.table_in.refs_2_, bf16[256,1024]{1,0:T(8,128)(2,1)} %bitcast.52), custom_call_target="tpu_custom_call" | custom-call | tf_op jit(solution)/shard_map/forward_yz/pallas_call | solution.py:375
  3.4 29.2 %all_to_all.20 = bf16[128,4,128]{2,1,0:T(4,128)(2,1)} all-to-all(bf16[128,4,128]{2,1,0:T(4,128)(2,1)} %bitcast.56), channel_id=1, replica_groups=mesh['gx'=128,'sa'=8] {'gx'}, dimensions={0} | all-to-all | bytes 262144 | tf_op jit(solution)/shard_map/all_to_all | solution.py:422
  32.6 3.6 %mix_forward.1 = (bf16[128,128]{1,0:T(8,128)(2,1)}, bf16[512,128]{1,0:T(8,128)(2,1)}) custom-call(bf16[512,128]{1,0:T(8,128)(2,1)} %bitcast.55, bf16[256,512]{1,0:T(8,128)(2,1)} %constant.30.clone.refs_1_.refs_2_, bf16[8192,128]{1,0:T(8,128)(2,1)} %bitcast.50), custom_call_target="tpu_custom_call" | custom-call | tf_op jit(solution)/shard_map/mix_forward/pallas_call | solution.py:375
  36.3 18.2 %all_to_all.21 = bf16[128,4,128]{2,1,0:T(4,128)(2,1)} all-to-all(bf16[128,4,128]{2,1,0:T(4,128)(2,1)} %bitcast.62), channel_id=1, replica_groups=mesh['gx'=128,'sa'=8] {'gx'}, dimensions={0} | all-to-all | bytes 262144 | tf_op jit(solution)/shard_map/all_to_all | solution.py:422
  54.4 0.0 copy-start.1
  54.4 0.0 copy-start.2
  54.4 4.5 %middle.1 = (bf16[512,128]{1,0:T(8,128)(2,1)}, bf16[256,1024]{1,0:T(8,128)(2,1)}, bf16[256,1024]{1,0:T(8,128)(2,1)}) custom-call(bf16[512,128]{1,0:T(8,128)(2,1)} %bitcast.59, bf16[256,192]{1,0:T(8,128)(2,1)} %constant.29.clone.refs_1_, bf16[64,256]{1,0:T(8,128)(2,1)} %constant.28.clone.table_in.refs_2_, bf16[64,64]{1,0:T(8,128)(2,1)} %refs_2_.3, ...), custom_call_target="tpu_custom_call" | custom-call | tf_op jit(solution)/shard_map/middle/pallas_call | solution.py:375
  58.9 0.0 copy-start
  59.0 18.3 %all_to_all.22 = bf16[128,4,128]{2,1,0:T(4,128)(2,1)} all-to-all(bf16[128,4,128]{2,1,0:T(4,128)(2,1)} %bitcast.61), channel_id=1, replica_groups=mesh['gx'=128,'sa'=8] {'gx'}, dimensions={0} | all-to-all | bytes 262144 | tf_op jit(solution)/shard_map/all_to_all | solution.py:422
  77.2 4.5 %mix_backward.1 = (bf16[128,128]{1,0:T(8,128)(2,1)}, bf16[128,128]{1,0:T(8,128)(2,1)}, bf16[512,128]{1,0:T(8,128)(2,1)}) custom-call(s32[1]{0:T(128)} %bitcast.refs_0_, bf16[512,128]{1,0:T(8,128)(2,1)} %bitcast.54, bf16[256,512]{1,0:T(8,128)(2,1)} %constant.30.clone.refs_1_.refs_2_, bf16[8192,128]{1,0:T(8,128)(2,1)} %bitcast.51, ...), custom_call_target="tpu_custom_call" | custom-call | tf_op jit(solution)/shard_map/mix_backward/pallas_call | solution.py:393
  81.7 8.5 %collective-permute-start = (bf16[128,128]{1,0:T(8,128)(2,1)}, bf16[128,128]{1,0:T(8,128)(2,1)S(1)}, u32[]{:S(2)}, u32[]{:S(2)}) collective-permute-start(bf16[128,128]{1,0:T(8,128)(2,1)} %get-tuple-element.22), channel_id=1, source_target_pairs={{0,1},{1,0},{2,3},{3,2},{4,5},{5,4},{6,7},{7,6},{8,9},{9,8},{10,11... | collective-permute-start | bytes 98312 | tf_op jit(solution)/shard_map/ppermute | solution.py:428
  90.2 6.2 %all-to-all-start.3 = ((bf16[128,4,128]{2,1,0:T(4,128)(2,1)}), bf16[128,4,128]{2,1,0:T(4,128)(2,1)S(1)}, u32[]{:S(2)}, u32[]{:S(2)}) async-start(bf16[128,4,128]{2,1,0:T(4,128)(2,1)} %bitcast.60), calls=%async_computation.3 | async-start | bytes 262144 | tf_op jit(solution)/shard_map/all_to_all | solution.py:422
  96.4 0.0 collective-permute-done
  96.4 0.8 fusion.7
  97.2 13.1 %collective-permute-start.3 = (bf16[2,2,16,128]{3,2,1,0:T(8,128)(2,1)S(1)}, bf16[2,2,16,128]{3,2,1,0:T(8,128)(2,1)S(1)}, u32[]{:S(2)}, u32[]{:S(2)}) collective-permute-start(bf16[2,2,16,128]{3,2,1,0:T(8,128)(2,1)S(1)} %get-tuple-element.33), channel_id=1, source_target_pairs={{0,6},{1,7},{2,4},{3,5},{4,2},{5,3},{6,0},{7,1},{8,14},{9,15},{10,... | collective-permute-start | bytes 49160 | tf_op jit(solution)/shard_map/ppermute | solution.py:434
  110.2 1.9 %collective-permute-start.2 = (bf16[2,2,16,128]{3,2,1,0:T(8,128)(2,1)S(1)}, bf16[2,2,16,128]{3,2,1,0:T(8,128)(2,1)S(1)}, u32[]{:S(2)}, u32[]{:S(2)}) collective-permute-start(bf16[2,2,16,128]{3,2,1,0:T(8,128)(2,1)S(1)} %get-tuple-element.32), channel_id=1, source_target_pairs={{0,4},{1,5},{2,6},{3,7},{4,0},{5,1},{6,2},{7,3},{8,12},{9,13},{10,... | collective-permute-start | bytes 49160 | tf_op jit(solution)/shard_map/ppermute | solution.py:434
  112.2 4.0 %collective-permute-start.1 = (bf16[2,2,16,128]{3,2,1,0:T(8,128)(2,1)S(1)}, bf16[2,2,16,128]{3,2,1,0:T(8,128)(2,1)S(1)}, u32[]{:S(2)}, u32[]{:S(2)}) collective-permute-start(bf16[2,2,16,128]{3,2,1,0:T(8,128)(2,1)S(1)} %get-tuple-element.31), channel_id=1, source_target_pairs={{0,2},{1,3},{2,0},{3,1},{4,6},{5,7},{6,4},{7,5},{8,10},{9,11},{10,... | collective-permute-start | bytes 49160 | tf_op jit(solution)/shard_map/ppermute | solution.py:434
  116.2 0.0 collective-permute-done.3
  116.2 2.5 %collective-permute-done.2 = bf16[2,2,16,128]{3,2,1,0:T(8,128)(2,1)S(1)} collective-permute-done((bf16[2,2,16,128]{3,2,1,0:T(8,128)(2,1)S(1)}, bf16[2,2,16,128]{3,2,1,0:T(8,128)(2,1)S(1)}, u32[]{:S(2)}, u32[]{:S(2)}) %collective-permute-start.2) | collective-permute-done | bytes 16416 | tf_op jit(solution)/shard_map/ppermute | solution.py:434
  118.7 0.0 collective-permute-done.1
  118.8 0.1 pad_maximum_fusion
  118.9 0.0 all-to-all-done.3
  118.9 0.0 copy-done.1
  118.9 0.0 copy-done.2
  118.9 0.0 copy-done
  118.9 1.7 %last.1 = bf16[256,1024]{1,0:T(8,128)(2,1)} custom-call(bf16[512,128]{1,0:T(8,128)(2,1)S(1)} %bitcast.49, bf16[256,192]{1,0:T(8,128)(2,1)S(1)} %copy-done.1, bf16[64,64]{1,0:T(8,128)(2,1)S(1)} %copy-done.2, bf16[256,1024]{1,0:T(8,128)(2,1)S(1)} %copy-done), custom_call_target="tpu_custom_call" | custom-call | tf_op jit(solution)/shard_map/last/pallas_call | solution.py:408
  120.6 0.1 fusion.14
  120.7 0.1 reshape_squeeze.3
  120.8 0.1 maximum_bitcast_fusion
  120.9 1.1 convolution_bitcast_fusion
  (5 shorter events, 0.1 us)
Async XLA Ops:
  54.4 64.4 %copy-start.1 = (bf16[256,192]{1,0:T(8,128)(2,1)S(1)}, bf16[256,192]{1,0:T(8,128)(2,1)}, u32[]{:S(2)}) copy-start(bf16[256,192]{1,0:T(8,128)(2,1)} %constant.29.clone.refs_1_) | copy-start | bytes 294916
  54.4 64.4 %copy-start.2 = (bf16[64,64]{1,0:T(8,128)(2,1)S(1)}, bf16[64,64]{1,0:T(8,128)(2,1)}, u32[]{:S(2)}) copy-start(bf16[64,64]{1,0:T(8,128)(2,1)} %refs_2_.3) | copy-start | bytes 24580
  58.9 59.9 %copy-start = (bf16[256,1024]{1,0:T(8,128)(2,1)S(1)}, bf16[256,1024]{1,0:T(8,128)(2,1)}, u32[]{:S(2)}) copy-start(bf16[256,1024]{1,0:T(8,128)(2,1)} %get-tuple-element.24.refs_3_) | copy-start | bytes 1572868
  81.7 14.7 %collective-permute-start = (bf16[128,128]{1,0:T(8,128)(2,1)}, bf16[128,128]{1,0:T(8,128)(2,1)S(1)}, u32[]{:S(2)}, u32[]{:S(2)}) collective-permute-start(bf16[128,128]{1,0:T(8,128)(2,1)} %get-tuple-element.22), channel_id=1, source_target_pairs={{0,1},{1,0},{2,3},{3,2},{4,5},{5,4},{6,7},{7,6},{8,9},{9,8},{10,11... | collective-permute-start | bytes 98312 | tf_op jit(solution)/shard_map/ppermute | solution.py:428
  90.2 28.7 %all-to-all-start.3 = ((bf16[128,4,128]{2,1,0:T(4,128)(2,1)}), bf16[128,4,128]{2,1,0:T(4,128)(2,1)S(1)}, u32[]{:S(2)}, u32[]{:S(2)}) async-start(bf16[128,4,128]{2,1,0:T(4,128)(2,1)} %bitcast.60), calls=%async_computation.3 | async-start | bytes 262144 | tf_op jit(solution)/shard_map/all_to_all | solution.py:422
  97.2 19.0 %collective-permute-start.3 = (bf16[2,2,16,128]{3,2,1,0:T(8,128)(2,1)S(1)}, bf16[2,2,16,128]{3,2,1,0:T(8,128)(2,1)S(1)}, u32[]{:S(2)}, u32[]{:S(2)}) collective-permute-start(bf16[2,2,16,128]{3,2,1,0:T(8,128)(2,1)S(1)} %get-tuple-element.33), channel_id=1, source_target_pairs={{0,6},{1,7},{2,4},{3,5},{4,2},{5,3},{6,0},{7,1},{8,14},{9,15},{10,... | collective-permute-start | bytes 49160 | tf_op jit(solution)/shard_map/ppermute | solution.py:434
  110.2 8.5 %collective-permute-start.2 = (bf16[2,2,16,128]{3,2,1,0:T(8,128)(2,1)S(1)}, bf16[2,2,16,128]{3,2,1,0:T(8,128)(2,1)S(1)}, u32[]{:S(2)}, u32[]{:S(2)}) collective-permute-start(bf16[2,2,16,128]{3,2,1,0:T(8,128)(2,1)S(1)} %get-tuple-element.32), channel_id=1, source_target_pairs={{0,4},{1,5},{2,6},{3,7},{4,0},{5,1},{6,2},{7,3},{8,12},{9,13},{10,... | collective-permute-start | bytes 49160 | tf_op jit(solution)/shard_map/ppermute | solution.py:434
  112.2 6.6 %collective-permute-start.1 = (bf16[2,2,16,128]{3,2,1,0:T(8,128)(2,1)S(1)}, bf16[2,2,16,128]{3,2,1,0:T(8,128)(2,1)S(1)}, u32[]{:S(2)}, u32[]{:S(2)}) collective-permute-start(bf16[2,2,16,128]{3,2,1,0:T(8,128)(2,1)S(1)} %get-tuple-element.31), channel_id=1, source_target_pairs={{0,2},{1,3},{2,0},{3,1},{4,6},{5,7},{6,4},{7,5},{8,10},{9,11},{10,... | collective-permute-start | bytes 49160 | tf_op jit(solution)/shard_map/ppermute | solution.py:434

commit v5 on v3

--- a/solution.py
+++ b/solution.py
@@ -11,7 +11,9 @@
 KY = 32
 KZ = 16
 GELU_COEF = 0.044715
-VMEM_BYTES = 40 << 20
+FIRST_BYTES = 16 << 20
+SMALL_BYTES = 16 << 20
+PIECES = 4
 
 
 def angles(freq_count, grid_count):
@@ -81,6 +83,26 @@
     return lower + upper
 
 
+class Fetched:
+    def __init__(self, source, target, semaphores, first, pieces=1, axis=0):
+        size = source.shape[axis] // pieces
+        self.copies = []
+        for at in range(pieces):
+            part = pl.ds(at * size, size)
+            index = (part,) if axis == 0 else (slice(None), part)
+            self.copies.append(
+                pltpu.make_async_copy(source.at[index], target.at[index], semaphores.at[first + at])
+            )
+
+    def start(self, at=None):
+        for copy in self.copies if at is None else self.copies[at : at + 1]:
+            copy.start()
+
+    def wait(self, at=None):
+        for copy in self.copies if at is None else self.copies[at : at + 1]:
+            copy.wait()
+
+
 def modes_from(first_pass, wide_modes, modes_out):
     width = modes_out.shape[1]
     low = lanes_of((8, width)) < width // 2
@@ -95,7 +117,8 @@
         spectrum = fourier(parts, -1)
         for kz in range(KZ):
             wide_modes[pl.ds(block * 8 * KZ + kz, 8, stride=KZ), :] = spectrum[(kz + KZ // 2) % KZ]
-    modes_out[...] = wide_modes[...].astype(modes_out.dtype)
+        rows = pl.ds(block * 8 * KZ, 8 * KZ)
+        modes_out[rows, :] = wide_modes[rows, :].astype(modes_out.dtype)
 
 
 def stacked_from(planes, wide_modes, stacked, norm_scale):
@@ -122,25 +145,55 @@
     return jnp.concatenate([high, low, high], 0)
 
 
-def forward_yz_kernel(table_y, field, modes_out, first_pass, wide_modes):
-    first_pass[...] = dot(table_y[...], field[...])
+def paired_of(point_weights):
+    channels = point_weights.shape[0]
+    wide = jnp.concatenate([point_weights[...].astype(jnp.float32)] * 4, 1)
+    tall = jnp.concatenate([wide] * 4, 0)
+    row = lax.broadcasted_iota(jnp.int32, tall.shape, 0)
+    return jnp.where(row // channels == lanes_of(tall.shape) // channels, tall, 0.0).astype(jnp.bfloat16)
+
+
+def forward_yz_kernel(*refs):
+    count = (len(refs) - 4) // 2
+    sources, (modes_out, *targets) = refs[:count], refs[count : 2 * count + 1]
+    first_pass, wide_modes, semaphores = refs[2 * count + 1 :]
+    fetches = [
+        Fetched(source, target, semaphores, at, PIECES if at == 0 else 1, 1)
+        if at == 0
+        else Fetched(source, target, semaphores, PIECES + at)
+        for at, (source, target) in enumerate(zip(sources, targets))
+    ]
+    fetches[1].start()
+    fetches[0].start()
+    for fetch in fetches[2:]:
+        fetch.start()
+    field, table_y = targets[:2]
+    fetches[1].wait()
+    width = field.shape[1] // PIECES
+    for column in range(PIECES):
+        lanes = pl.ds(column * width, width)
+        fetches[0].wait(column)
+        first_pass[:, lanes] = dot(table_y[...], field[:, lanes])
     modes_from(first_pass, wide_modes, modes_out)
+    for fetch in fetches[2:]:
+        fetch.wait()
 
 
 def middle_kernel(
-    norm_scale, planes, inverse_y, table_y, paired, field, cotangent,
+    norm_scale, planes, inverse_y, table_y, point_weights, field, cotangent,
     modes_out, field_out, out_grad, stacked, first_pass, wide_modes,
 ):
+    paired = paired_of(point_weights)
     stacked_from(planes, wide_modes, stacked, norm_scale)
     root_const = math.sqrt(2.0 / math.pi)
-    width = paired.shape[0]
+    width = field.shape[1] // PIECES
     rows_per = 64
-    for column in range(field.shape[1] // width):
+    for column in range(PIECES):
         lanes = pl.ds(column * width, width)
         terms = three_terms(stacked, lanes)
         for start in range(0, field.shape[0], rows_per):
             rows = pl.ds(start, rows_per)
-            pre_act = dot(inverse_y[rows, :], terms) + dot(field[rows, lanes], paired[...])
+            pre_act = dot(inverse_y[rows, :], terms) + dot(field[rows, lanes], paired)
             square = pre_act * pre_act
             tangent = jnp.tanh(pre_act * (root_const + root_const * GELU_COEF * square))
             half = 0.5 + 0.5 * tangent
@@ -152,7 +205,8 @@
     modes_from(first_pass, wide_modes, modes_out)
 
 
-def last_kernel(norm_scale, planes, inverse_y, paired, out_grad, field_grad, stacked, wide_modes):
+def last_kernel(norm_scale, planes, inverse_y, point_weights, out_grad, field_grad, stacked, wide_modes):
+    paired = paired_of(point_weights)
     stacked_from(planes, wide_modes, stacked, norm_scale)
     width = paired.shape[0]
     rows_per = 128
@@ -161,8 +215,10 @@
         terms = three_terms(stacked, lanes)
         for start in range(0, out_grad.shape[0], rows_per):
             rows = pl.ds(start, rows_per)
-            grad = dot(inverse_y[rows, :], terms) + dot(out_grad[rows, lanes], paired[...])
-            field_grad[rows, lanes] = grad.astype(field_grad.dtype)
+            mixed = lax.dot_general(
+                out_grad[rows, lanes], paired, (((1,), (1,)), ((), ())), preferred_element_type=jnp.float32
+            )
+            field_grad[rows, lanes] = (dot(inverse_y[rows, :], terms) + mixed).astype(field_grad.dtype)
 
 
 def coeffs_of(along_x, mode_data, norm_scale):
@@ -171,14 +227,16 @@
     return ((both[:count] + quarter_turn(both[count:], -1)) * norm_scale).astype(jnp.bfloat16)
 
 
-def planes_of(along_x, mixed):
-    turned = quarter_turn(mixed.astype(jnp.float32), 1).astype(jnp.bfloat16)
-    return lax.dot_general(
-        along_x[...],
-        jnp.concatenate([mixed, turned], 0),
-        (((0,), (0,)), ((), ())),
-        preferred_element_type=jnp.float32,
-    ).astype(jnp.bfloat16)
+def store_planes(along_x, mixed, planes_out):
+    mixed = mixed[...]
+    turned = quarter_turn(mixed.astype(jnp.bfloat16).astype(jnp.float32), 1).astype(jnp.bfloat16)
+    terms = jnp.concatenate([mixed.astype(jnp.bfloat16), turned], 0)
+    size = planes_out.shape[0] // PIECES
+    for piece in range(PIECES):
+        rows = pl.ds(piece * size, size)
+        planes_out[rows, :] = lax.dot_general(
+            along_x[:, rows], terms, (((0,), (0,)), ((), ())), preferred_element_type=jnp.float32
+        ).astype(jnp.bfloat16)
 
 
 def own_block(shape, channels):
@@ -229,32 +287,53 @@
     coeffs = coeffs_of(along_x, mode_data, norm_scale)
     coeffs_out[...] = coeffs
     mixed_forward(coeffs, weights, mixed)
-    planes_out[...] = planes_of(along_x, mixed[...].astype(jnp.bfloat16))
-
-
-def forward_x_kernel(norm_scale, mode_data, along_x, coeffs_out):
-    coeffs_out[...] = coeffs_of(along_x, mode_data, norm_scale)
-
-
-def mix_backward_kernel(coeffs_in, along_x, weights, planes_out, mixed):
-    mixed_backward(coeffs_in[...], weights, mixed)
-    planes_out[...] = planes_of(along_x, mixed[...].astype(jnp.bfloat16))
-
-
-def call(kernel, operands, outs, scratch, name):
-    single = isinstance(outs, tuple)
-    flat = [outs] if single else list(outs)
+    store_planes(along_x, mixed, planes_out)
+
+
+def mix_backward_kernel(
+    norm_scale, samples, core, mode_data, along_x, weights, coeffs_in, kept, given, planes_out, mixed
+):
+    coeffs = coeffs_of(along_x, mode_data, norm_scale)
+    first_core = core[0] == 0
+    size = coeffs.shape[0] // samples
+    for side, values in enumerate((coeffs_in[...], coeffs)):
+        for place in range(samples // 2):
+            even = values[2 * place * size : (2 * place + 1) * size].astype(jnp.float32)
+            odd = values[(2 * place + 1) * size : (2 * place + 2) * size].astype(jnp.float32)
+            rows = pl.ds((side * (samples // 2) + place) * size, size)
+            kept[rows, :] = jnp.where(first_core, even, odd).astype(jnp.bfloat16)
+            given[rows, :] = jnp.where(first_core, odd, even).astype(jnp.bfloat16)
+    mixed_backward(coeffs, weights, mixed)
+    store_planes(along_x, mixed, planes_out)
+
+
+def call_first(operands, modes_shape, scratch):
+    outs = [jax.ShapeDtypeStruct(modes_shape, jnp.bfloat16)] + [
+        jax.ShapeDtypeStruct(array.shape, array.dtype) for array in operands
+    ]
+    return pl.pallas_call(
+        forward_yz_kernel,
+        name="forward_yz",
+        out_shape=outs,
+        in_specs=[pl.BlockSpec(memory_space=pltpu.HBM)] * len(operands),
+        out_specs=[pl.BlockSpec(memory_space=pltpu.VMEM)] * len(outs),
+        scratch_shapes=[pltpu.VMEM(shape, jnp.float32) for shape in scratch]
+        + [pltpu.SemaphoreType.DMA((PIECES + len(operands),))],
+        compiler_params=pltpu.CompilerParams(vmem_limit_bytes=FIRST_BYTES),
+    )(*(pltpu.with_memory_space_constraint(array, pltpu.HBM) for array in operands))
+
+
+def call(kernel, operands, outs, scratch, name, scalars=()):
     whole = pl.BlockSpec(memory_space=pltpu.VMEM)
-    result = pl.pallas_call(
+    return pl.pallas_call(
         kernel,
         name=name,
-        out_shape=[jax.ShapeDtypeStruct(shape, jnp.bfloat16) for shape in flat],
-        in_specs=[whole] * len(operands),
-        out_specs=[whole] * len(flat),
+        out_shape=[jax.ShapeDtypeStruct(shape, jnp.bfloat16) for shape in outs],
+        in_specs=[pl.BlockSpec(memory_space=pltpu.SMEM)] * len(scalars) + [whole] * len(operands),
+        out_specs=[whole] * len(outs),
         scratch_shapes=[pltpu.VMEM(shape, jnp.float32) for shape in scratch],
-        compiler_params=pltpu.CompilerParams(vmem_limit_bytes=VMEM_BYTES),
-    )(*operands)
-    return result[0] if single else result
+        compiler_params=pltpu.CompilerParams(vmem_limit_bytes=SMALL_BYTES),
+    )(*scalars, *operands)
 
 
 def exchange(rows):
@@ -263,16 +342,12 @@
     return lax.all_to_all(slots, "gx", split_axis=0, concat_axis=0, tiled=True).reshape(rows.shape)
 
 
-def swap_samples(both):
+def swap_samples(kept, given, mine):
     count = lax.axis_size("sa")
-    mine = lax.axis_index("sa")
-    core = jnp.bitwise_and(mine, 1)
+    width = kept.shape[1]
+    taken = lax.ppermute(given, "sa", [(i, i ^ 1) for i in range(count)])
+    pair = jnp.stack([kept, taken], 0).reshape(2, 2, count // 2, -1, width)
     place = jnp.right_shift(mine, 1)
-    blocks = both.reshape((2, count // 2, 2, both.shape[1] // count) + both.shape[2:])
-    kept = lax.dynamic_index_in_dim(blocks, core, 2, keepdims=False)
-    given = lax.dynamic_index_in_dim(blocks, 1 - core, 2, keepdims=False)
-    taken = lax.ppermute(given, "sa", [(i, i ^ 1) for i in range(count)])
-    pair = jnp.stack([kept, taken], 0)
     arrived = [lax.dynamic_index_in_dim(pair, place, 2, keepdims=False)]
     for step in range(1, count // 2):
         block = lax.dynamic_index_in_dim(pair, jnp.bitwise_xor(place, step), 2, keepdims=False)
@@ -306,15 +381,16 @@
     along_x = table_x(kx_count, x_length, mode_block)
     table_y, inverse_y, along_x = map(jnp.asarray, (table_y, inverse_y, along_x))
     weights = mode_weights.reshape(-1, width)
-    four = jnp.eye(4, dtype=point_weights.dtype)
-    paired = jnp.kron(four, point_weights)
-    paired_back = jnp.kron(four, point_weights.T)
     scaled = lambda kernel: lambda *refs: kernel(norm_scale, *refs)
     rows = kx_count * mode_block
     planar = (mode_total, width)
     stacked = (2 * KY, last_width)
-
-    modes = call(forward_yz_kernel, (table_y, field), planar, [stacked, planar], "forward_yz")
+    mine = lax.axis_index("sa")
+    core, field = lax.optimization_barrier((jnp.bitwise_and(mine, 1).reshape(1), field))
+
+    modes, field, table_y, weights, along_x, inverse_y, point_weights, cotangent_rows = call_first(
+        (field, table_y, weights, along_x, inverse_y, point_weights, cotangent_rows), planar, [stacked, planar]
+    )
     coeffs_in, planes = call(
         scaled(mix_forward_kernel),
         (exchange(modes), along_x, weights),
@@ -324,23 +400,26 @@
     )
     modes, field_out, out_grad = call(
         scaled(middle_kernel),
-        (exchange(planes), inverse_y, table_y, paired, field, cotangent_rows),
+        (exchange(planes), inverse_y, table_y, point_weights, field, cotangent_rows),
         [planar, field.shape, field.shape],
         [stacked, stacked, planar],
         "middle",
     )
-    coeffs_grad = call(
-        scaled(forward_x_kernel), (exchange(modes), along_x), (rows, width), [], "forward_x"
-    )
-    planes = call(
-        mix_backward_kernel, (coeffs_grad, along_x, weights), planar, [(rows, width)], "mix_backward"
-    )
-    both = jnp.stack([coeffs_in, coeffs_grad], 0).reshape(2, kx_count, mode_block, width)
-    shared = swap_samples(both)
-    field_grad = call(
+    kept, given, planes = call(
+        lambda *refs: mix_backward_kernel(norm_scale, samples, *refs),
+        (exchange(modes), along_x, weights, coeffs_in),
+        [(rows, width), (rows, width), planar],
+        [(rows, width)],
+        "mix_backward",
+        (core,),
+    )
+    shared = swap_samples(kept, given, mine).reshape(
+        samples, 2, kx_count // samples, mode_block, width
+    )
+    (field_grad,) = call(
         scaled(last_kernel),
-        (exchange(planes), inverse_y, paired_back, out_grad),
-        field.shape,
+        (exchange(planes), inverse_y, point_weights, out_grad),
+        [field.shape],
         [stacked, planar],
         "last",
     )

time: 122 us -> 113 us (0.926)
  blocking collectives: 28.8 us -> 62 us
  waiting for transfers between devices: 21.6 us -> 4.59 us
  starting transfers between devices: 47.3 us -> 33.7 us
  local copies, waits for them, and re-layouts: 10.4 us -> 0.15 us
  other arithmetic: 2.17 us -> 0.27 us
    all_to_all x1 -> x3, blocking collectives: 28.8 us -> 62 us  [exchange(): lax.all_to_all(slots, 'gx', split_axis=0, concat_axis=0, tiled=True)]
    all_to_all x3 -> x1, waiting for transfers between devices: 19.3 us -> 0.01 us  [exchange(): lax.all_to_all(slots, 'gx', split_axis=0, concat_axis=0, tiled=True)]
    all_to_all x3 -> x1, starting transfers between devices: 19.8 us -> 6.19 us  [exchange(): lax.all_to_all(slots, 'gx', split_axis=0, concat_axis=0, tiled=True)]
    unnamed x36 -> x0, local copies, waits for them, and re-layouts: 8.72 us -> none
    ppermute x3, waiting for transfers between devices: 2.3 us -> 4.58 us  [swap_samples(): lax.ppermute(block, 'sa', [(i, i ^ 2 * step) for i in range(count)])]
    pallas_call x0 -> x1, Pallas kernels: none -> 2.18 us  [call_first(): pl.pallas_call(forward_yz_kernel, name='forward_yz', out_shape=outs, in_s...]
    pallas_call x6 -> x4, Pallas kernels: 8.99 us -> 7.52 us  [call(): pl.pallas_call(kernel, name=name, out_shape=[jax.ShapeDtypeStruct(shape,...]
    mul x2 -> x0, local copies, waits for them, and re-layouts: 1.39 us -> none  [the longest x1 1.18 us: on_device(): paired = jnp.kron(four, point_weights)]
  transfers between devices with their start and end apart: 7 -> 5, of which waited for: 3 -> 1; matrix products, arithmetic and copies ran while one was open for 2% -> 0% of each run, Pallas kernels for 1% -> 0%
where the time goes in v5:
time: 113 us; the launch traced here: 112 us
  blocking collectives  62 us (55%)
  starting transfers between devices  33.7 us (30%)
  Pallas kernels  9.71 us (9%)
  waiting for transfers between devices  4.59 us (4%)
    all_to_all x3, blocking collectives, exchange(): lax.all_to_all(slots, 'gx', split_axis=0, concat_axis=0, tiled=True)  62 us
    ppermute x3, starting transfers between devices, swap_samples(): lax.ppermute(block, 'sa', [(i, i ^ 2 * step) for i in range(count)])  20.2 us
    pallas_call x4, Pallas kernels, call(): pl.pallas_call(kernel, name=name, out_shape=[jax.ShapeDtypeStruct(shape,...  7.52 us
    ppermute x1, starting transfers between devices, swap_samples(): taken = lax.ppermute(given, 'sa', [(i, i ^ 1) for i in range(count)])  7.23 us
    all_to_all x1, starting transfers between devices, exchange(): lax.all_to_all(slots, 'gx', split_axis=0, concat_axis=0, tiled=True)  6.19 us
    ppermute x3, waiting for transfers between devices, swap_samples(): lax.ppermute(block, 'sa', [(i, i ^ 2 * step) for i in range(count)])  4.58 us
  transfers between devices with their start and end apart: 5, of which 1 were waited for; matrix products, arithmetic and copies ran while one was open for 0% of the time, Pallas kernels for 0%

profile of v5, /device:TPU:1, one launch (start us, length us, event | category | flops | bytes accessed | tf_op | source)
XLA Modules:
  0.0 112.2 jit_solution(10281118973109741684)
XLA Ops:
  0.6 2.2 %forward_yz.1 = (bf16[512,128]{1,0:T(8,128)(2,1)S(1)}, bf16[256,1024]{1,0:T(8,128)(2,1)S(1)}, bf16[64,256]{1,0:T(8,128)(2,1)S(1)}, bf16[8192,128]{1,0:T(8,128)(2...) custom-call(bf16[256,1024]{1,0:T(8,128)(2,1)} %bitcast.58, ...), custom_call_target="tpu_custom_call" | custom-call | tf_op jit(solution)/shard_map/forward_yz/pallas_call | solution.py:314
  2.8 28.8 %all_to_all.20 = bf16[128,4,128]{2,1,0:T(4,128)(2,1)S(1)} all-to-all(bf16[128,4,128]{2,1,0:T(4,128)(2,1)S(1)} %bitcast.53), channel_id=1, replica_groups=mesh['gx'=128,'sa'=8] {'gx'}, dimensions={0} | all-to-all | bytes 262144 | tf_op jit(solution)/shard_map/all_to_all | solution.py:342
  31.7 1.1 mix_forward.1
  32.7 16.6 %all_to_all.21 = bf16[128,4,128]{2,1,0:T(4,128)(2,1)S(1)} all-to-all(bf16[128,4,128]{2,1,0:T(4,128)(2,1)S(1)} %bitcast.55), channel_id=1, replica_groups=mesh['gx'=128,'sa'=8] {'gx'}, dimensions={0} | all-to-all | bytes 262144 | tf_op jit(solution)/shard_map/all_to_all | solution.py:342
  49.3 2.7 %middle.1 = (bf16[512,128]{1,0:T(8,128)(2,1)S(1)}, bf16[256,1024]{1,0:T(8,128)(2,1)}, bf16[256,1024]{1,0:T(8,128)(2,1)S(1)}) custom-call(bf16[512,128]{1,0:T(8,128)(2,1)S(1)} %bitcast.52, bf16[256,192]{1,0:T(8,128)(2,1)S(1)} %get-tuple-element.28.refs_1_, bf16[64,256]{1,0:T(8,128)(2,1)S(1)} %get-tuple-element.29.refs_2_, ...), custom_call_target="tpu_custom_call" | custom-call | tf_op jit(solution)/shard_map/middle/pallas_call | solution.py:328
  52.0 16.6 %all_to_all.22 = bf16[128,4,128]{2,1,0:T(4,128)(2,1)S(1)} all-to-all(bf16[128,4,128]{2,1,0:T(4,128)(2,1)S(1)} %bitcast.54), channel_id=1, replica_groups=mesh['gx'=128,'sa'=8] {'gx'}, dimensions={0} | all-to-all | bytes 262144 | tf_op jit(solution)/shard_map/all_to_all | solution.py:342
  68.6 2.0 %mix_backward.1 = (bf16[128,128]{1,0:T(8,128)(2,1)S(1)}, bf16[128,128]{1,0:T(8,128)(2,1)S(1)}, bf16[512,128]{1,0:T(8,128)(2,1)}) custom-call(s32[1]{0:T(128)} %bitcast.refs_0_, bf16[512,128]{1,0:T(8,128)(2,1)S(1)} %bitcast.49, bf16[256,512]{1,0:T(8,128)(2,1)S(1)} %get-tuple-element.25.refs_1_.refs_2_, ...), custom_call_target="tpu_custom_call" | custom-call | tf_op jit(solution)/shard_map/mix_backward/pallas_call | solution.py:328
  70.6 7.2 %collective-permute-start = (bf16[128,128]{1,0:T(8,128)(2,1)S(1)}, bf16[128,128]{1,0:T(8,128)(2,1)S(1)}, u32[]{:S(2)}, u32[]{:S(2)}) collective-permute-start(bf16[128,128]{1,0:T(8,128)(2,1)S(1)} %get-tuple-element.38), channel_id=1, source_target_pairs={{0,1},{1,0},{2,3},{3,2},{4,5},{5,4},{6,7},{7,6},{8,9},{9,8},{10,11... | collective-permute-start | bytes 98312 | tf_op jit(solution)/shard_map/ppermute | solution.py:348
  77.9 6.2 %all-to-all-start.3 = ((bf16[128,4,128]{2,1,0:T(4,128)(2,1)}), bf16[128,4,128]{2,1,0:T(4,128)(2,1)S(1)}, u32[]{:S(2)}, u32[]{:S(2)}) async-start(bf16[128,4,128]{2,1,0:T(4,128)(2,1)} %bitcast.20), calls=%async_computation.3 | async-start | bytes 262144 | tf_op jit(solution)/shard_map/all_to_all | solution.py:342
  84.1 0.0 collective-permute-done
  84.1 6.7 %collective-permute-start.1 = (bf16[2,2,16,128]{3,2,1,0:T(8,128)(2,1)S(1)}, bf16[2,2,16,128]{3,2,1,0:T(8,128)(2,1)S(1)}, u32[]{:S(2)}, u32[]{:S(2)}) collective-permute-start(bf16[2,2,16,128]{3,2,1,0:T(8,128)(2,1)S(1)} %get-tuple-element.47), channel_id=1, source_target_pairs={{0,2},{1,3},{2,0},{3,1},{4,6},{5,7},{6,4},{7,5},{8,10},{9,11},{10,... | collective-permute-start | bytes 49160 | tf_op jit(solution)/shard_map/ppermute | solution.py:354
  90.9 11.6 %collective-permute-start.2 = (bf16[2,2,16,128]{3,2,1,0:T(8,128)(2,1)S(1)}, bf16[2,2,16,128]{3,2,1,0:T(8,128)(2,1)S(1)}, u32[]{:S(2)}, u32[]{:S(2)}) collective-permute-start(bf16[2,2,16,128]{3,2,1,0:T(8,128)(2,1)S(1)} %get-tuple-element.48), channel_id=1, source_target_pairs={{0,4},{1,5},{2,6},{3,7},{4,0},{5,1},{6,2},{7,3},{8,12},{9,13},{10,... | collective-permute-start | bytes 49160 | tf_op jit(solution)/shard_map/ppermute | solution.py:354
  102.5 1.9 %collective-permute-start.3 = (bf16[2,2,16,128]{3,2,1,0:T(8,128)(2,1)S(1)}, bf16[2,2,16,128]{3,2,1,0:T(8,128)(2,1)S(1)}, u32[]{:S(2)}, u32[]{:S(2)}) collective-permute-start(bf16[2,2,16,128]{3,2,1,0:T(8,128)(2,1)S(1)} %get-tuple-element.49), channel_id=1, source_target_pairs={{0,6},{1,7},{2,4},{3,5},{4,2},{5,3},{6,0},{7,1},{8,14},{9,15},{10,... | collective-permute-start | bytes 49160 | tf_op jit(solution)/shard_map/ppermute | solution.py:354
  104.4 0.0 collective-permute-done.1
  104.5 0.0 collective-permute-done.2
  104.5 4.6 %collective-permute-done.3 = bf16[2,2,16,128]{3,2,1,0:T(8,128)(2,1)S(1)} collective-permute-done((bf16[2,2,16,128]{3,2,1,0:T(8,128)(2,1)S(1)}, bf16[2,2,16,128]{3,2,1,0:T(8,128)(2,1)S(1)}, u32[]{:S(2)}, u32[]{:S(2)}) %collective-permute-start.3) | collective-permute-done | bytes 16416 | tf_op jit(solution)/shard_map/ppermute | solution.py:354
  109.1 0.1 pad_maximum_fusion
  109.2 0.0 all-to-all-done.3
  109.2 1.7 %last.1 = bf16[256,1024]{1,0:T(8,128)(2,1)} custom-call(bf16[512,128]{1,0:T(8,128)(2,1)S(1)} %bitcast.51, bf16[256,192]{1,0:T(8,128)(2,1)S(1)} %get-tuple-element.28.refs_1_, bf16[64,64]{1,0:T(8,128)(2,1)S(1)} %get-tuple-element.30.refs_3_.refs_2_, bf16[256,1024]{1,0:T(8,128)(2,1)S(1)} %get-tuple-element.40.refs_3_), custom_call_target="tpu_custom_call" | custom-call | tf_op jit(solution)/shard_map/last/pallas_call | solution.py:328
  110.9 0.1 fusion.14
  111.0 0.1 reshape_squeeze.3
  111.1 0.1 maximum_bitcast_fusion
  111.2 1.1 convolution_bitcast_fusion
  (6 shorter events, 0.1 us)
Async XLA Ops:
  70.6 13.4 %collective-permute-start = (bf16[128,128]{1,0:T(8,128)(2,1)S(1)}, bf16[128,128]{1,0:T(8,128)(2,1)S(1)}, u32[]{:S(2)}, u32[]{:S(2)}) collective-permute-start(bf16[128,128]{1,0:T(8,128)(2,1)S(1)} %get-tuple-element.38), channel_id=1, source_target_pairs={{0,1},{1,0},{2,3},{3,2},{4,5},{5,4},{6,7},{7,6},{8,9},{9,8},{10,11... | collective-permute-start | bytes 98312 | tf_op jit(solution)/shard_map/ppermute | solution.py:348
  77.9 31.3 %all-to-all-start.3 = ((bf16[128,4,128]{2,1,0:T(4,128)(2,1)}), bf16[128,4,128]{2,1,0:T(4,128)(2,1)S(1)}, u32[]{:S(2)}, u32[]{:S(2)}) async-start(bf16[128,4,128]{2,1,0:T(4,128)(2,1)} %bitcast.20), calls=%async_computation.3 | async-start | bytes 262144 | tf_op jit(solution)/shard_map/all_to_all | solution.py:342
  84.1 20.3 %collective-permute-start.1 = (bf16[2,2,16,128]{3,2,1,0:T(8,128)(2,1)S(1)}, bf16[2,2,16,128]{3,2,1,0:T(8,128)(2,1)S(1)}, u32[]{:S(2)}, u32[]{:S(2)}) collective-permute-start(bf16[2,2,16,128]{3,2,1,0:T(8,128)(2,1)S(1)} %get-tuple-element.47), channel_id=1, source_target_pairs={{0,2},{1,3},{2,0},{3,1},{4,6},{5,7},{6,4},{7,5},{8,10},{9,11},{10,... | collective-permute-start | bytes 49160 | tf_op jit(solution)/shard_map/ppermute | solution.py:354
  90.9 13.6 %collective-permute-start.2 = (bf16[2,2,16,128]{3,2,1,0:T(8,128)(2,1)S(1)}, bf16[2,2,16,128]{3,2,1,0:T(8,128)(2,1)S(1)}, u32[]{:S(2)}, u32[]{:S(2)}) collective-permute-start(bf16[2,2,16,128]{3,2,1,0:T(8,128)(2,1)S(1)} %get-tuple-element.48), channel_id=1, source_target_pairs={{0,4},{1,5},{2,6},{3,7},{4,0},{5,1},{6,2},{7,3},{8,12},{9,13},{10,... | collective-permute-start | bytes 49160 | tf_op jit(solution)/shard_map/ppermute | solution.py:354
  102.5 6.6 %collective-permute-start.3 = (bf16[2,2,16,128]{3,2,1,0:T(8,128)(2,1)S(1)}, bf16[2,2,16,128]{3,2,1,0:T(8,128)(2,1)S(1)}, u32[]{:S(2)}, u32[]{:S(2)}) collective-permute-start(bf16[2,2,16,128]{3,2,1,0:T(8,128)(2,1)S(1)} %get-tuple-element.49), channel_id=1, source_target_pairs={{0,6},{1,7},{2,4},{3,5},{4,2},{5,3},{6,0},{7,1},{8,14},{9,15},{10,... | collective-permute-start | bytes 49160 | tf_op jit(solution)/shard_map/ppermute | solution.py:354

commit v6 on v5

--- a/solution.py
+++ b/solution.py
@@ -14,6 +14,7 @@
 FIRST_BYTES = 16 << 20
 SMALL_BYTES = 16 << 20
 PIECES = 4
+SORT_HINT = 40_000_000_000
 
 
 def angles(freq_count, grid_count):
@@ -181,8 +182,9 @@
 
 def middle_kernel(
     norm_scale, planes, inverse_y, table_y, point_weights, field, cotangent,
-    modes_out, field_out, out_grad, stacked, first_pass, wide_modes,
+    modes_out, field_out_hbm, out_grad, stacked, first_pass, wide_modes, field_out, semaphores,
 ):
+    store = Fetched(field_out, field_out_hbm, semaphores, 0, PIECES, 1)
     paired = paired_of(point_weights)
     stacked_from(planes, wide_modes, stacked, norm_scale)
     root_const = math.sqrt(2.0 / math.pi)
@@ -201,16 +203,22 @@
             slope = half + activated * (1.0 - tangent) * (root_const + 3.0 * root_const * GELU_COEF * square)
             field_out[rows, lanes] = activated.astype(field_out.dtype)
             out_grad[rows, lanes] = (cotangent[rows, lanes].astype(jnp.float32) * slope).astype(out_grad.dtype)
+        store.start(column)
         first_pass[:, lanes] = dot(table_y[...], out_grad[:, lanes])
     modes_from(first_pass, wide_modes, modes_out)
-
-
-def last_kernel(norm_scale, planes, inverse_y, point_weights, out_grad, field_grad, stacked, wide_modes):
+    store.wait()
+
+
+def last_kernel(
+    norm_scale, planes, inverse_y, point_weights, out_grad,
+    field_grad_hbm, stacked, wide_modes, field_grad, semaphores,
+):
+    store = Fetched(field_grad, field_grad_hbm, semaphores, 0, PIECES, 1)
     paired = paired_of(point_weights)
     stacked_from(planes, wide_modes, stacked, norm_scale)
     width = paired.shape[0]
     rows_per = 128
-    for column in range(out_grad.shape[1] // width):
+    for column in range(PIECES):
         lanes = pl.ds(column * width, width)
         terms = three_terms(stacked, lanes)
         for start in range(0, out_grad.shape[0], rows_per):
@@ -219,6 +227,8 @@
                 out_grad[rows, lanes], paired, (((1,), (1,)), ((), ())), preferred_element_type=jnp.float32
             )
             field_grad[rows, lanes] = (dot(inverse_y[rows, :], terms) + mixed).astype(field_grad.dtype)
+        store.start(column)
+    store.wait()
 
 
 def coeffs_of(along_x, mode_data, norm_scale):
@@ -323,15 +333,21 @@
     )(*(pltpu.with_memory_space_constraint(array, pltpu.HBM) for array in operands))
 
 
-def call(kernel, operands, outs, scratch, name, scalars=()):
+def call(kernel, operands, outs, scratch, name, scalars=(), estimate=None, stored=None):
     whole = pl.BlockSpec(memory_space=pltpu.VMEM)
+    out_specs = [whole] * len(outs)
+    scratch_shapes = [pltpu.VMEM(shape, jnp.float32) for shape in scratch]
+    if stored is not None:
+        out_specs[stored] = pl.BlockSpec(memory_space=pl.ANY)
+        scratch_shapes += [pltpu.VMEM(outs[stored], jnp.bfloat16), pltpu.SemaphoreType.DMA((PIECES,))]
     return pl.pallas_call(
         kernel,
         name=name,
+        cost_estimate=estimate,
         out_shape=[jax.ShapeDtypeStruct(shape, jnp.bfloat16) for shape in outs],
         in_specs=[pl.BlockSpec(memory_space=pltpu.SMEM)] * len(scalars) + [whole] * len(operands),
-        out_specs=[whole] * len(outs),
-        scratch_shapes=[pltpu.VMEM(shape, jnp.float32) for shape in scratch],
+        out_specs=out_specs,
+        scratch_shapes=scratch_shapes,
         compiler_params=pltpu.CompilerParams(vmem_limit_bytes=SMALL_BYTES),
     )(*scalars, *operands)
 
@@ -342,17 +358,33 @@
     return lax.all_to_all(slots, "gx", split_axis=0, concat_axis=0, tiled=True).reshape(rows.shape)
 
 
-def swap_samples(kept, given, mine):
+def sort_kernel(place, kept, taken, *blocks):
+    size = kept.shape[0] // (2 * len(blocks))
+    for step, block in enumerate(blocks):
+        wanted = jnp.bitwise_xor(place[0], step)
+        for core, source in enumerate((kept, taken)):
+            for side in range(2):
+                start = pl.multiple_of((side * len(blocks) + wanted) * size, size)
+                block[pl.ds((2 * core + side) * size, size), :] = source[pl.ds(start, size), :]
+
+
+def swap_samples(kept, given, place):
     count = lax.axis_size("sa")
-    width = kept.shape[1]
     taken = lax.ppermute(given, "sa", [(i, i ^ 1) for i in range(count)])
-    pair = jnp.stack([kept, taken], 0).reshape(2, 2, count // 2, -1, width)
-    place = jnp.right_shift(mine, 1)
-    arrived = [lax.dynamic_index_in_dim(pair, place, 2, keepdims=False)]
-    for step in range(1, count // 2):
-        block = lax.dynamic_index_in_dim(pair, jnp.bitwise_xor(place, step), 2, keepdims=False)
-        arrived.append(lax.ppermute(block, "sa", [(i, i ^ 2 * step) for i in range(count)]))
-    return jnp.concatenate(arrived, 0)
+    rows, width = kept.shape
+    blocks = call(
+        sort_kernel,
+        (kept, taken),
+        [(4 * rows // count, width)] * (count // 2),
+        [],
+        "sort",
+        (place,),
+        pl.CostEstimate(flops=SORT_HINT, bytes_accessed=4 * rows * width, transcendentals=0),
+    )
+    return [blocks[0]] + [
+        lax.ppermute(blocks[step], "sa", [(i, i ^ 2 * step) for i in range(count)])
+        for step in range(1, count // 2)
+    ]
 
 
 def sample_sum(left_side, right_side):
@@ -386,7 +418,9 @@
     planar = (mode_total, width)
     stacked = (2 * KY, last_width)
     mine = lax.axis_index("sa")
-    core, field = lax.optimization_barrier((jnp.bitwise_and(mine, 1).reshape(1), field))
+    core, place, field = lax.optimization_barrier(
+        (jnp.bitwise_and(mine, 1).reshape(1), jnp.right_shift(mine, 1).reshape(1), field)
+    )
 
     modes, field, table_y, weights, along_x, inverse_y, point_weights, cotangent_rows = call_first(
         (field, table_y, weights, along_x, inverse_y, point_weights, cotangent_rows), planar, [stacked, planar]
@@ -404,6 +438,7 @@
         [planar, field.shape, field.shape],
         [stacked, stacked, planar],
         "middle",
+        stored=1,
     )
     kept, given, planes = call(
         lambda *refs: mix_backward_kernel(norm_scale, samples, *refs),
@@ -413,17 +448,17 @@
         "mix_backward",
         (core,),
     )
-    shared = swap_samples(kept, given, mine).reshape(
-        samples, 2, kx_count // samples, mode_block, width
-    )
+    arrived = swap_samples(kept, given, place)
     (field_grad,) = call(
         scaled(last_kernel),
         (exchange(planes), inverse_y, point_weights, out_grad),
         [field.shape],
         [stacked, planar],
         "last",
-    )
-    shared, field_grad = lax.optimization_barrier((shared, field_grad))
+        stored=0,
+    )
+    arrived, field_grad = lax.optimization_barrier((arrived, field_grad))
+    shared = jnp.concatenate(arrived, 0).reshape(samples, 2, kx_count // samples, mode_block, width)
     weight_grad = sample_sum(shared[:, 0], shared[:, 1])
     return (
         field_out.reshape(field_in.shape),

time: 113 us -> 110 us (0.973)
  waiting for transfers between devices: 4.59 us -> 3.03 us
    ppermute x3, waiting for transfers between devices: 4.58 us -> 3.02 us  [swap_samples(): lax.ppermute(blocks[step], 'sa', [(i, i ^ 2 * step) for i in range(count)])]
    pallas_call x4 -> x5, Pallas kernels: 7.52 us -> 6.97 us  [call(): pl.pallas_call(kernel, name=name, cost_estimate=estimate, out_shape=[jax....]
  transfers between devices with their start and end apart: 5 -> 5, of which waited for: 1 -> 1; matrix products, arithmetic and copies ran while one was open for 0% -> 0% of each run, Pallas kernels for 0% -> 1%
where the time goes in v6:
time: 110 us
  blocking collectives  62 us (56%)
  starting transfers between devices  33.7 us (31%)
  Pallas kernels  9.15 us (8%)
  waiting for transfers between devices  3.03 us (3%)
    all_to_all x3, blocking collectives, exchange(): lax.all_to_all(slots, 'gx', split_axis=0, concat_axis=0, tiled=True)  62 us
    ppermute x3, starting transfers between devices, swap_samples(): lax.ppermute(blocks[step], 'sa', [(i, i ^ 2 * step) for i in range(count)])  20.3 us
    ppermute x1, starting transfers between devices, swap_samples(): taken = lax.ppermute(given, 'sa', [(i, i ^ 1) for i in range(count)])  7.22 us
    pallas_call x5, Pallas kernels, call(): pl.pallas_call(kernel, name=name, cost_estimate=estimate, out_shape=[jax....  6.97 us
    all_to_all x1, starting transfers between devices, exchange(): lax.all_to_all(slots, 'gx', split_axis=0, concat_axis=0, tiled=True)  6.19 us
    ppermute x3, waiting for transfers between devices, swap_samples(): lax.ppermute(blocks[step], 'sa', [(i, i ^ 2 * step) for i in range(count)])  3.02 us
  transfers between devices with their start and end apart: 5, of which 1 were waited for; matrix products, arithmetic and copies ran while one was open for 0% of the time, Pallas kernels for 1%

profile of v6, /device:TPU:1, one launch (start us, length us, event | category | flops | bytes accessed | tf_op | source)
XLA Modules:
  0.0 110.0 jit_solution(16776841676004850807)
XLA Ops:
  0.6 2.2 %forward_yz.1 = (bf16[512,128]{1,0:T(8,128)(2,1)S(1)}, bf16[256,1024]{1,0:T(8,128)(2,1)S(1)}, bf16[64,256]{1,0:T(8,128)(2,1)S(1)}, bf16[8192,128]{1,0:T(8,128)(2...) custom-call(bf16[256,1024]{1,0:T(8,128)(2,1)} %bitcast.36, ...), custom_call_target="tpu_custom_call" | custom-call | tf_op jit(solution)/shard_map/forward_yz/pallas_call | solution.py:324
  2.8 28.8 %all_to_all.20 = bf16[128,4,128]{2,1,0:T(4,128)(2,1)S(1)} all-to-all(bf16[128,4,128]{2,1,0:T(4,128)(2,1)S(1)} %bitcast.32), channel_id=1, replica_groups=mesh['gx'=128,'sa'=8] {'gx'}, dimensions={0} | all-to-all | bytes 262144 | tf_op jit(solution)/shard_map/all_to_all | solution.py:358
  31.7 1.1 mix_forward.1
  32.7 16.6 %all_to_all.21 = bf16[128,4,128]{2,1,0:T(4,128)(2,1)S(1)} all-to-all(bf16[128,4,128]{2,1,0:T(4,128)(2,1)S(1)} %bitcast.34), channel_id=1, replica_groups=mesh['gx'=128,'sa'=8] {'gx'}, dimensions={0} | all-to-all | bytes 262144 | tf_op jit(solution)/shard_map/all_to_all | solution.py:358
  49.3 2.2 %middle.1 = (bf16[512,128]{1,0:T(8,128)(2,1)S(1)}, bf16[256,1024]{1,0:T(8,128)(2,1)}, bf16[256,1024]{1,0:T(8,128)(2,1)S(1)}) custom-call(bf16[512,128]{1,0:T(8,128)(2,1)S(1)} %bitcast.31, bf16[256,192]{1,0:T(8,128)(2,1)S(1)} %get-tuple-element.36.refs_1_, bf16[64,256]{1,0:T(8,128)(2,1)S(1)} %get-tuple-element.37.refs_2_, ...), custom_call_target="tpu_custom_call" | custom-call | tf_op jit(solution)/shard_map/middle/pallas_call | solution.py:343
  51.6 16.6 %all_to_all.22 = bf16[128,4,128]{2,1,0:T(4,128)(2,1)S(1)} all-to-all(bf16[128,4,128]{2,1,0:T(4,128)(2,1)S(1)} %bitcast.33), channel_id=1, replica_groups=mesh['gx'=128,'sa'=8] {'gx'}, dimensions={0} | all-to-all | bytes 262144 | tf_op jit(solution)/shard_map/all_to_all | solution.py:358
  68.2 2.0 %mix_backward.1 = (bf16[128,128]{1,0:T(8,128)(2,1)S(1)}, bf16[128,128]{1,0:T(8,128)(2,1)S(1)}, bf16[512,128]{1,0:T(8,128)(2,1)}) custom-call(s32[1]{0:T(128)} %bitcast.refs_0_, bf16[512,128]{1,0:T(8,128)(2,1)S(1)} %bitcast.28, bf16[256,512]{1,0:T(8,128)(2,1)S(1)} %get-tuple-element.33.refs_1_.refs_2_, ...), custom_call_target="tpu_custom_call" | custom-call | tf_op jit(solution)/shard_map/mix_backward/pallas_call | solution.py:343
  70.2 7.2 %collective-permute-start = (bf16[128,128]{1,0:T(8,128)(2,1)S(1)}, bf16[128,128]{1,0:T(8,128)(2,1)S(1)}, u32[]{:S(2)}, u32[]{:S(2)}) collective-permute-start(bf16[128,128]{1,0:T(8,128)(2,1)S(1)} %get-tuple-element.47), channel_id=1, source_target_pairs={{0,1},{1,0},{2,3},{3,2},{4,5},{5,4},{6,7},{7,6},{8,9},{9,8},{10,11... | collective-permute-start | bytes 98312 | tf_op jit(solution)/shard_map/ppermute | solution.py:373
  77.4 6.2 %all-to-all-start.3 = ((bf16[128,4,128]{2,1,0:T(4,128)(2,1)}), bf16[128,4,128]{2,1,0:T(4,128)(2,1)S(1)}, u32[]{:S(2)}, u32[]{:S(2)}) async-start(bf16[128,4,128]{2,1,0:T(4,128)(2,1)} %bitcast.12), calls=%async_computation.3 | async-start | bytes 262144 | tf_op jit(solution)/shard_map/all_to_all | solution.py:358
  83.6 0.0 collective-permute-done.taken
  83.6 6.8 %collective-permute-start.1 = (bf16[64,128]{1,0:T(8,128)(2,1)S(1)}, bf16[64,128]{1,0:T(8,128)(2,1)S(1)}, u32[]{:S(2)}, u32[]{:S(2)}) collective-permute-start(bf16[64,128]{1,0:T(8,128)(2,1)S(1)} %get-tuple-element.49), channel_id=1, source_target_pairs={{0,2},{1,3},{2,0},{3,1},{4,6},{5,7},{6,4},{7,5},{8,10},{9,11},{10,... | collective-permute-start | bytes 49160 | tf_op jit(solution)/shard_map/ppermute | solution.py:385
  90.4 11.6 %collective-permute-start.2 = (bf16[64,128]{1,0:T(8,128)(2,1)S(1)}, bf16[64,128]{1,0:T(8,128)(2,1)S(1)}, u32[]{:S(2)}, u32[]{:S(2)}) collective-permute-start(bf16[64,128]{1,0:T(8,128)(2,1)S(1)} %get-tuple-element.50), channel_id=1, source_target_pairs={{0,4},{1,5},{2,6},{3,7},{4,0},{5,1},{6,2},{7,3},{8,12},{9,13},{10,... | collective-permute-start | bytes 49160 | tf_op jit(solution)/shard_map/ppermute | solution.py:385
  102.0 1.9 %collective-permute-start.3 = (bf16[64,128]{1,0:T(8,128)(2,1)S(1)}, bf16[64,128]{1,0:T(8,128)(2,1)S(1)}, u32[]{:S(2)}, u32[]{:S(2)}) collective-permute-start(bf16[64,128]{1,0:T(8,128)(2,1)S(1)} %get-tuple-element.51), channel_id=1, source_target_pairs={{0,6},{1,7},{2,4},{3,5},{4,2},{5,3},{6,0},{7,1},{8,14},{9,15},{10,... | collective-permute-start | bytes 49160 | tf_op jit(solution)/shard_map/ppermute | solution.py:385
  103.9 0.0 all-to-all-done.3
  103.9 1.6 %last.1 = bf16[256,1024]{1,0:T(8,128)(2,1)} custom-call(bf16[512,128]{1,0:T(8,128)(2,1)S(1)} %bitcast.30, bf16[256,192]{1,0:T(8,128)(2,1)S(1)} %get-tuple-element.36.refs_1_, bf16[64,64]{1,0:T(8,128)(2,1)S(1)} %get-tuple-element.38.refs_3_.refs_2_, bf16[256,1024]{1,0:T(8,128)(2,1)S(1)} %get-tuple-element.53.refs_3_), custom_call_target="tpu_custom_call" | custom-call | tf_op jit(solution)/shard_map/last/pallas_call | solution.py:343
  105.5 0.0 collective-permute-done.1
  105.6 0.0 collective-permute-done.2
  105.6 3.0 %collective-permute-done.3 = bf16[64,128]{1,0:T(8,128)(2,1)S(1)} collective-permute-done((bf16[64,128]{1,0:T(8,128)(2,1)S(1)}, bf16[64,128]{1,0:T(8,128)(2,1)S(1)}, u32[]{:S(2)}, u32[]{:S(2)}) %collective-permute-start.3) | collective-permute-done | bytes 16416 | tf_op jit(solution)/shard_map/ppermute | solution.py:385
  108.6 0.1 reshape.71
  108.7 0.1 fusion.6
  108.8 0.1 maximum_bitcast_fusion
  108.9 1.1 convolution_bitcast_fusion
  (4 shorter events, 0.1 us)
Async XLA Ops:
  70.2 13.4 %collective-permute-start = (bf16[128,128]{1,0:T(8,128)(2,1)S(1)}, bf16[128,128]{1,0:T(8,128)(2,1)S(1)}, u32[]{:S(2)}, u32[]{:S(2)}) collective-permute-start(bf16[128,128]{1,0:T(8,128)(2,1)S(1)} %get-tuple-element.47), channel_id=1, source_target_pairs={{0,1},{1,0},{2,3},{3,2},{4,5},{5,4},{6,7},{7,6},{8,9},{9,8},{10,11... | collective-permute-start | bytes 98312 | tf_op jit(solution)/shard_map/ppermute | solution.py:373
  77.4 26.5 %all-to-all-start.3 = ((bf16[128,4,128]{2,1,0:T(4,128)(2,1)}), bf16[128,4,128]{2,1,0:T(4,128)(2,1)S(1)}, u32[]{:S(2)}, u32[]{:S(2)}) async-start(bf16[128,4,128]{2,1,0:T(4,128)(2,1)} %bitcast.12), calls=%async_computation.3 | async-start | bytes 262144 | tf_op jit(solution)/shard_map/all_to_all | solution.py:358
  83.6 21.9 %collective-permute-start.1 = (bf16[64,128]{1,0:T(8,128)(2,1)S(1)}, bf16[64,128]{1,0:T(8,128)(2,1)S(1)}, u32[]{:S(2)}, u32[]{:S(2)}) collective-permute-start(bf16[64,128]{1,0:T(8,128)(2,1)S(1)} %get-tuple-element.49), channel_id=1, source_target_pairs={{0,2},{1,3},{2,0},{3,1},{4,6},{5,7},{6,4},{7,5},{8,10},{9,11},{10,... | collective-permute-start | bytes 49160 | tf_op jit(solution)/shard_map/ppermute | solution.py:385
  90.4 15.2 %collective-permute-start.2 = (bf16[64,128]{1,0:T(8,128)(2,1)S(1)}, bf16[64,128]{1,0:T(8,128)(2,1)S(1)}, u32[]{:S(2)}, u32[]{:S(2)}) collective-permute-start(bf16[64,128]{1,0:T(8,128)(2,1)S(1)} %get-tuple-element.50), channel_id=1, source_target_pairs={{0,4},{1,5},{2,6},{3,7},{4,0},{5,1},{6,2},{7,3},{8,12},{9,13},{10,... | collective-permute-start | bytes 49160 | tf_op jit(solution)/shard_map/ppermute | solution.py:385
  102.0 6.6 %collective-permute-start.3 = (bf16[64,128]{1,0:T(8,128)(2,1)S(1)}, bf16[64,128]{1,0:T(8,128)(2,1)S(1)}, u32[]{:S(2)}, u32[]{:S(2)}) collective-permute-start(bf16[64,128]{1,0:T(8,128)(2,1)S(1)} %get-tuple-element.51), channel_id=1, source_target_pairs={{0,6},{1,7},{2,4},{3,5},{4,2},{5,3},{6,0},{7,1},{8,14},{9,15},{10,... | collective-permute-start | bytes 49160 | tf_op jit(solution)/shard_map/ppermute | solution.py:385

commit v7 on v6

--- a/solution.py
+++ b/solution.py
@@ -237,7 +237,7 @@
     return ((both[:count] + quarter_turn(both[count:], -1)) * norm_scale).astype(jnp.bfloat16)
 
 
-def store_planes(along_x, mixed, planes_out):
+def store_planes(along_x, mixed, planes_out, store=None):
     mixed = mixed[...]
     turned = quarter_turn(mixed.astype(jnp.bfloat16).astype(jnp.float32), 1).astype(jnp.bfloat16)
     terms = jnp.concatenate([mixed.astype(jnp.bfloat16), turned], 0)
@@ -247,6 +247,10 @@
         planes_out[rows, :] = lax.dot_general(
             along_x[:, rows], terms, (((0,), (0,)), ((), ())), preferred_element_type=jnp.float32
         ).astype(jnp.bfloat16)
+        if store is not None:
+            store.start(piece)
+    if store is not None:
+        store.wait()
 
 
 def own_block(shape, channels):
@@ -293,16 +297,23 @@
         mixed[pl.ds(start, 8), :] = jnp.where(low, folded[0], folded[1])
 
 
-def mix_forward_kernel(norm_scale, mode_data, along_x, weights, coeffs_out, planes_out, mixed):
+def mix_forward_kernel(
+    norm_scale, mode_data, along_x, weights, later_hbm, coeffs_out, planes_out, later, mixed, semaphores
+):
+    fetch = Fetched(later_hbm, later, semaphores, 0)
+    fetch.start()
     coeffs = coeffs_of(along_x, mode_data, norm_scale)
     coeffs_out[...] = coeffs
     mixed_forward(coeffs, weights, mixed)
     store_planes(along_x, mixed, planes_out)
+    fetch.wait()
 
 
 def mix_backward_kernel(
-    norm_scale, samples, core, mode_data, along_x, weights, coeffs_in, kept, given, planes_out, mixed
+    norm_scale, samples, core, mode_data, along_x, weights, coeffs_in,
+    kept, given, planes_hbm, mixed, planes_out, semaphores,
 ):
+    store = Fetched(planes_out, planes_hbm, semaphores, 0, PIECES)
     coeffs = coeffs_of(along_x, mode_data, norm_scale)
     first_core = core[0] == 0
     size = coeffs.shape[0] // samples
@@ -314,7 +325,7 @@
             kept[rows, :] = jnp.where(first_core, even, odd).astype(jnp.bfloat16)
             given[rows, :] = jnp.where(first_core, odd, even).astype(jnp.bfloat16)
     mixed_backward(coeffs, weights, mixed)
-    store_planes(along_x, mixed, planes_out)
+    store_planes(along_x, mixed, planes_out, store)
 
 
 def call_first(operands, modes_shape, scratch):
@@ -333,19 +344,26 @@
     )(*(pltpu.with_memory_space_constraint(array, pltpu.HBM) for array in operands))
 
 
-def call(kernel, operands, outs, scratch, name, scalars=(), estimate=None, stored=None):
+def call(kernel, operands, outs, scratch, name, scalars=(), estimate=None, stored=None, brought=None):
     whole = pl.BlockSpec(memory_space=pltpu.VMEM)
     out_specs = [whole] * len(outs)
     scratch_shapes = [pltpu.VMEM(shape, jnp.float32) for shape in scratch]
     if stored is not None:
         out_specs[stored] = pl.BlockSpec(memory_space=pl.ANY)
         scratch_shapes += [pltpu.VMEM(outs[stored], jnp.bfloat16), pltpu.SemaphoreType.DMA((PIECES,))]
+    in_specs = [pl.BlockSpec(memory_space=pltpu.SMEM)] * len(scalars) + [whole] * len(operands)
+    if brought is not None:
+        operands = (*operands, pltpu.with_memory_space_constraint(brought, pltpu.HBM))
+        in_specs.append(pl.BlockSpec(memory_space=pltpu.HBM))
+        outs = [*outs, brought.shape]
+        out_specs.append(whole)
+        scratch_shapes.append(pltpu.SemaphoreType.DMA((1,)))
     return pl.pallas_call(
         kernel,
         name=name,
         cost_estimate=estimate,
         out_shape=[jax.ShapeDtypeStruct(shape, jnp.bfloat16) for shape in outs],
-        in_specs=[pl.BlockSpec(memory_space=pltpu.SMEM)] * len(scalars) + [whole] * len(operands),
+        in_specs=in_specs,
         out_specs=out_specs,
         scratch_shapes=scratch_shapes,
         compiler_params=pltpu.CompilerParams(vmem_limit_bytes=SMALL_BYTES),
@@ -422,15 +440,16 @@
         (jnp.bitwise_and(mine, 1).reshape(1), jnp.right_shift(mine, 1).reshape(1), field)
     )
 
-    modes, field, table_y, weights, along_x, inverse_y, point_weights, cotangent_rows = call_first(
-        (field, table_y, weights, along_x, inverse_y, point_weights, cotangent_rows), planar, [stacked, planar]
-    )
-    coeffs_in, planes = call(
+    modes, field, table_y, weights, along_x, inverse_y, point_weights = call_first(
+        (field, table_y, weights, along_x, inverse_y, point_weights), planar, [stacked, planar]
+    )
+    coeffs_in, planes, cotangent_rows = call(
         scaled(mix_forward_kernel),
         (exchange(modes), along_x, weights),
         [(rows, width), planar],
         [(rows, width)],
         "mix_forward",
+        brought=cotangent_rows,
     )
     modes, field_out, out_grad = call(
         scaled(middle_kernel),
@@ -447,6 +466,7 @@
         [(rows, width)],
         "mix_backward",
         (core,),
+        stored=2,
     )
     arrived = swap_samples(kept, given, place)
     (field_grad,) = call(

time: 110 us -> 110 us (level)
  no operation moved by 1% of the time
where the time goes in v7:
time: 110 us
  blocking collectives  62 us (56%)
  starting transfers between devices  33.7 us (31%)
  Pallas kernels  9.02 us (8%)
  waiting for transfers between devices  3.02 us (3%)
    all_to_all x3, blocking collectives, exchange(): lax.all_to_all(slots, 'gx', split_axis=0, concat_axis=0, tiled=True)  62 us
    ppermute x3, starting transfers between devices, swap_samples(): lax.ppermute(blocks[step], 'sa', [(i, i ^ 2 * step) for i in range(count)])  20.3 us
    ppermute x1, starting transfers between devices, swap_samples(): taken = lax.ppermute(given, 'sa', [(i, i ^ 1) for i in range(count)])  7.24 us
    pallas_call x5, Pallas kernels, call(): pl.pallas_call(kernel, name=name, cost_estimate=estimate, out_shape=[jax....  6.99 us
    all_to_all x1, starting transfers between devices, exchange(): lax.all_to_all(slots, 'gx', split_axis=0, concat_axis=0, tiled=True)  6.19 us
    ppermute x3, waiting for transfers between devices, swap_samples(): lax.ppermute(blocks[step], 'sa', [(i, i ^ 2 * step) for i in range(count)])  3.02 us
  transfers between devices with their start and end apart: 5, of which 1 were waited for; matrix products, arithmetic and copies ran while one was open for 0% of the time, Pallas kernels for 1%

profile of v7, /device:TPU:1, one launch (start us, length us, event | category | flops | bytes accessed | tf_op | source)
XLA Modules:
  0.0 109.9 jit_solution(6654238627579270081)
XLA Ops:
  0.6 2.0 %forward_yz.1 = (bf16[512,128]{1,0:T(8,128)(2,1)S(1)}, bf16[256,1024]{1,0:T(8,128)(2,1)S(1)}, bf16[64,256]{1,0:T(8,128)(2,1)S(1)}, bf16[8192,128]{1,0:T(8,128)(2...) custom-call(bf16[256,1024]{1,0:T(8,128)(2,1)} %bitcast.38, ...), custom_call_target="tpu_custom_call" | custom-call | tf_op jit(solution)/shard_map/forward_yz/pallas_call | solution.py:335
  2.7 28.8 %all_to_all.20 = bf16[128,4,128]{2,1,0:T(4,128)(2,1)S(1)} all-to-all(bf16[128,4,128]{2,1,0:T(4,128)(2,1)S(1)} %bitcast.32), channel_id=1, replica_groups=mesh['gx'=128,'sa'=8] {'gx'}, dimensions={0} | all-to-all | bytes 262144 | tf_op jit(solution)/shard_map/all_to_all | solution.py:376
  31.5 1.1 mix_forward.1
  32.6 16.6 %all_to_all.21 = bf16[128,4,128]{2,1,0:T(4,128)(2,1)S(1)} all-to-all(bf16[128,4,128]{2,1,0:T(4,128)(2,1)S(1)} %bitcast.34), channel_id=1, replica_groups=mesh['gx'=128,'sa'=8] {'gx'}, dimensions={0} | all-to-all | bytes 262144 | tf_op jit(solution)/shard_map/all_to_all | solution.py:376
  49.2 2.3 %middle.1 = (bf16[512,128]{1,0:T(8,128)(2,1)S(1)}, bf16[256,1024]{1,0:T(8,128)(2,1)}, bf16[256,1024]{1,0:T(8,128)(2,1)S(1)}) custom-call(bf16[512,128]{1,0:T(8,128)(2,1)S(1)} %bitcast.31, bf16[256,192]{1,0:T(8,128)(2,1)S(1)} %get-tuple-element.36.refs_1_, bf16[64,256]{1,0:T(8,128)(2,1)S(1)} %get-tuple-element.37.refs_2_, ...), custom_call_target="tpu_custom_call" | custom-call | tf_op jit(solution)/shard_map/middle/pallas_call | solution.py:361
  51.4 16.6 %all_to_all.22 = bf16[128,4,128]{2,1,0:T(4,128)(2,1)S(1)} all-to-all(bf16[128,4,128]{2,1,0:T(4,128)(2,1)S(1)} %bitcast.33), channel_id=1, replica_groups=mesh['gx'=128,'sa'=8] {'gx'}, dimensions={0} | all-to-all | bytes 262144 | tf_op jit(solution)/shard_map/all_to_all | solution.py:376
  68.0 2.0 %mix_backward.1 = (bf16[128,128]{1,0:T(8,128)(2,1)S(1)}, bf16[128,128]{1,0:T(8,128)(2,1)S(1)}, bf16[512,128]{1,0:T(8,128)(2,1)}) custom-call(s32[1]{0:T(128)} %bitcast.refs_0_, bf16[512,128]{1,0:T(8,128)(2,1)S(1)} %bitcast.28, bf16[256,512]{1,0:T(8,128)(2,1)S(1)} %get-tuple-element.33.refs_1_.refs_2_, ...), custom_call_target="tpu_custom_call" | custom-call | tf_op jit(solution)/shard_map/mix_backward/pallas_call | solution.py:361
  70.0 7.2 %collective-permute-start = (bf16[128,128]{1,0:T(8,128)(2,1)S(1)}, bf16[128,128]{1,0:T(8,128)(2,1)S(1)}, u32[]{:S(2)}, u32[]{:S(2)}) collective-permute-start(bf16[128,128]{1,0:T(8,128)(2,1)S(1)} %get-tuple-element.47), channel_id=1, source_target_pairs={{0,1},{1,0},{2,3},{3,2},{4,5},{5,4},{6,7},{7,6},{8,9},{9,8},{10,11... | collective-permute-start | bytes 98312 | tf_op jit(solution)/shard_map/ppermute | solution.py:391
  77.3 6.2 %all-to-all-start.3 = ((bf16[128,4,128]{2,1,0:T(4,128)(2,1)}), bf16[128,4,128]{2,1,0:T(4,128)(2,1)S(1)}, u32[]{:S(2)}, u32[]{:S(2)}) async-start(bf16[128,4,128]{2,1,0:T(4,128)(2,1)} %bitcast.12), calls=%async_computation.3 | async-start | bytes 262144 | tf_op jit(solution)/shard_map/all_to_all | solution.py:376
  83.5 0.0 collective-permute-done.taken
  83.5 6.7 %collective-permute-start.1 = (bf16[64,128]{1,0:T(8,128)(2,1)S(1)}, bf16[64,128]{1,0:T(8,128)(2,1)S(1)}, u32[]{:S(2)}, u32[]{:S(2)}) collective-permute-start(bf16[64,128]{1,0:T(8,128)(2,1)S(1)} %get-tuple-element.49), channel_id=1, source_target_pairs={{0,2},{1,3},{2,0},{3,1},{4,6},{5,7},{6,4},{7,5},{8,10},{9,11},{10,... | collective-permute-start | bytes 49160 | tf_op jit(solution)/shard_map/ppermute | solution.py:403
  90.3 11.6 %collective-permute-start.2 = (bf16[64,128]{1,0:T(8,128)(2,1)S(1)}, bf16[64,128]{1,0:T(8,128)(2,1)S(1)}, u32[]{:S(2)}, u32[]{:S(2)}) collective-permute-start(bf16[64,128]{1,0:T(8,128)(2,1)S(1)} %get-tuple-element.50), channel_id=1, source_target_pairs={{0,4},{1,5},{2,6},{3,7},{4,0},{5,1},{6,2},{7,3},{8,12},{9,13},{10,... | collective-permute-start | bytes 49160 | tf_op jit(solution)/shard_map/ppermute | solution.py:403
  101.9 1.9 %collective-permute-start.3 = (bf16[64,128]{1,0:T(8,128)(2,1)S(1)}, bf16[64,128]{1,0:T(8,128)(2,1)S(1)}, u32[]{:S(2)}, u32[]{:S(2)}) collective-permute-start(bf16[64,128]{1,0:T(8,128)(2,1)S(1)} %get-tuple-element.51), channel_id=1, source_target_pairs={{0,6},{1,7},{2,4},{3,5},{4,2},{5,3},{6,0},{7,1},{8,14},{9,15},{10,... | collective-permute-start | bytes 49160 | tf_op jit(solution)/shard_map/ppermute | solution.py:403
  103.8 0.0 all-to-all-done.3
  103.8 1.6 %last.1 = bf16[256,1024]{1,0:T(8,128)(2,1)} custom-call(bf16[512,128]{1,0:T(8,128)(2,1)S(1)} %bitcast.30, bf16[256,192]{1,0:T(8,128)(2,1)S(1)} %get-tuple-element.36.refs_1_, bf16[64,64]{1,0:T(8,128)(2,1)S(1)} %get-tuple-element.38.refs_3_.refs_2_, bf16[256,1024]{1,0:T(8,128)(2,1)S(1)} %get-tuple-element.53.refs_3_), custom_call_target="tpu_custom_call" | custom-call | tf_op jit(solution)/shard_map/last/pallas_call | solution.py:361
  105.4 0.0 collective-permute-done.1
  105.4 0.0 collective-permute-done.2
  105.5 3.0 %collective-permute-done.3 = bf16[64,128]{1,0:T(8,128)(2,1)S(1)} collective-permute-done((bf16[64,128]{1,0:T(8,128)(2,1)S(1)}, bf16[64,128]{1,0:T(8,128)(2,1)S(1)}, u32[]{:S(2)}, u32[]{:S(2)}) %collective-permute-start.3) | collective-permute-done | bytes 16416 | tf_op jit(solution)/shard_map/ppermute | solution.py:403
  108.5 0.1 reshape.71
  108.6 0.1 fusion.6
  108.7 0.1 maximum_bitcast_fusion
  108.8 1.1 convolution_bitcast_fusion
  (4 shorter events, 0.1 us)
Async XLA Ops:
  70.0 13.4 %collective-permute-start = (bf16[128,128]{1,0:T(8,128)(2,1)S(1)}, bf16[128,128]{1,0:T(8,128)(2,1)S(1)}, u32[]{:S(2)}, u32[]{:S(2)}) collective-permute-start(bf16[128,128]{1,0:T(8,128)(2,1)S(1)} %get-tuple-element.47), channel_id=1, source_target_pairs={{0,1},{1,0},{2,3},{3,2},{4,5},{5,4},{6,7},{7,6},{8,9},{9,8},{10,11... | collective-permute-start | bytes 98312 | tf_op jit(solution)/shard_map/ppermute | solution.py:391
  77.3 26.5 %all-to-all-start.3 = ((bf16[128,4,128]{2,1,0:T(4,128)(2,1)}), bf16[128,4,128]{2,1,0:T(4,128)(2,1)S(1)}, u32[]{:S(2)}, u32[]{:S(2)}) async-start(bf16[128,4,128]{2,1,0:T(4,128)(2,1)} %bitcast.12), calls=%async_computation.3 | async-start | bytes 262144 | tf_op jit(solution)/shard_map/all_to_all | solution.py:376
  83.5 21.9 %collective-permute-start.1 = (bf16[64,128]{1,0:T(8,128)(2,1)S(1)}, bf16[64,128]{1,0:T(8,128)(2,1)S(1)}, u32[]{:S(2)}, u32[]{:S(2)}) collective-permute-start(bf16[64,128]{1,0:T(8,128)(2,1)S(1)} %get-tuple-element.49), channel_id=1, source_target_pairs={{0,2},{1,3},{2,0},{3,1},{4,6},{5,7},{6,4},{7,5},{8,10},{9,11},{10,... | collective-permute-start | bytes 49160 | tf_op jit(solution)/shard_map/ppermute | solution.py:403
  90.3 15.2 %collective-permute-start.2 = (bf16[64,128]{1,0:T(8,128)(2,1)S(1)}, bf16[64,128]{1,0:T(8,128)(2,1)S(1)}, u32[]{:S(2)}, u32[]{:S(2)}) collective-permute-start(bf16[64,128]{1,0:T(8,128)(2,1)S(1)} %get-tuple-element.50), channel_id=1, source_target_pairs={{0,4},{1,5},{2,6},{3,7},{4,0},{5,1},{6,2},{7,3},{8,12},{9,13},{10,... | collective-permute-start | bytes 49160 | tf_op jit(solution)/shard_map/ppermute | solution.py:403
  101.9 6.6 %collective-permute-start.3 = (bf16[64,128]{1,0:T(8,128)(2,1)S(1)}, bf16[64,128]{1,0:T(8,128)(2,1)S(1)}, u32[]{:S(2)}, u32[]{:S(2)}) collective-permute-start(bf16[64,128]{1,0:T(8,128)(2,1)S(1)} %get-tuple-element.51), channel_id=1, source_target_pairs={{0,6},{1,7},{2,4},{3,5},{4,2},{5,3},{6,0},{7,1},{8,14},{9,15},{10,... | collective-permute-start | bytes 49160 | tf_op jit(solution)/shard_map/ppermute | solution.py:403

commit v8 on v7

--- a/solution.py
+++ b/solution.py
@@ -161,7 +161,7 @@
     fetches = [
         Fetched(source, target, semaphores, at, PIECES if at == 0 else 1, 1)
         if at == 0
-        else Fetched(source, target, semaphores, PIECES + at)
+        else Fetched(source, target, semaphores, PIECES * (1 + at), PIECES if source.shape[0] >= 256 else 1)
         for at, (source, target) in enumerate(zip(sources, targets))
     ]
     fetches[1].start()
@@ -339,7 +339,7 @@
         in_specs=[pl.BlockSpec(memory_space=pltpu.HBM)] * len(operands),
         out_specs=[pl.BlockSpec(memory_space=pltpu.VMEM)] * len(outs),
         scratch_shapes=[pltpu.VMEM(shape, jnp.float32) for shape in scratch]
-        + [pltpu.SemaphoreType.DMA((PIECES + len(operands),))],
+        + [pltpu.SemaphoreType.DMA((PIECES * (1 + len(operands)),))],
         compiler_params=pltpu.CompilerParams(vmem_limit_bytes=FIRST_BYTES),
     )(*(pltpu.with_memory_space_constraint(array, pltpu.HBM) for array in operands))
 

time: 110 us -> 110 us (level)
  no operation moved by 1% of the time
where the time goes in v8:
time: 110 us
  blocking collectives  62 us (56%)
  starting transfers between devices  33.7 us (31%)
  Pallas kernels  9.19 us (8%)
  waiting for transfers between devices  3.03 us (3%)
    all_to_all x3, blocking collectives, exchange(): lax.all_to_all(slots, 'gx', split_axis=0, concat_axis=0, tiled=True)  62 us
    ppermute x3, starting transfers between devices, swap_samples(): lax.ppermute(blocks[step], 'sa', [(i, i ^ 2 * step) for i in range(count)])  20.2 us
    ppermute x1, starting transfers between devices, swap_samples(): taken = lax.ppermute(given, 'sa', [(i, i ^ 1) for i in range(count)])  7.26 us
    pallas_call x5, Pallas kernels, call(): pl.pallas_call(kernel, name=name, cost_estimate=estimate, out_shape=[jax....  6.98 us
    all_to_all x1, starting transfers between devices, exchange(): lax.all_to_all(slots, 'gx', split_axis=0, concat_axis=0, tiled=True)  6.19 us
    ppermute x3, waiting for transfers between devices, swap_samples(): lax.ppermute(blocks[step], 'sa', [(i, i ^ 2 * step) for i in range(count)])  3.02 us
    pallas_call x1, Pallas kernels, call_first(): pl.pallas_call(forward_yz_kernel, name='forward_yz', out_shape=outs, in_s...  2.21 us
  transfers between devices with their start and end apart: 5, of which 1 were waited for; matrix products, arithmetic and copies ran while one was open for 0% of the time, Pallas kernels for 1%

profile of v8, /device:TPU:1, one launch (start us, length us, event | category | flops | bytes accessed | tf_op | source)
XLA Modules:
  0.0 110.0 jit_solution(18241339387371356458)
XLA Ops:
  0.6 2.2 %forward_yz.1 = (bf16[512,128]{1,0:T(8,128)(2,1)S(1)}, bf16[256,1024]{1,0:T(8,128)(2,1)S(1)}, bf16[64,256]{1,0:T(8,128)(2,1)S(1)}, bf16[8192,128]{1,0:T(8,128)(2...) custom-call(bf16[256,1024]{1,0:T(8,128)(2,1)} %bitcast.38, ...), custom_call_target="tpu_custom_call" | custom-call | tf_op jit(solution)/shard_map/forward_yz/pallas_call | solution.py:335
  2.9 28.8 %all_to_all.20 = bf16[128,4,128]{2,1,0:T(4,128)(2,1)S(1)} all-to-all(bf16[128,4,128]{2,1,0:T(4,128)(2,1)S(1)} %bitcast.32), channel_id=1, replica_groups=mesh['gx'=128,'sa'=8] {'gx'}, dimensions={0} | all-to-all | bytes 262144 | tf_op jit(solution)/shard_map/all_to_all | solution.py:376
  31.7 1.1 mix_forward.1
  32.8 16.6 %all_to_all.21 = bf16[128,4,128]{2,1,0:T(4,128)(2,1)S(1)} all-to-all(bf16[128,4,128]{2,1,0:T(4,128)(2,1)S(1)} %bitcast.34), channel_id=1, replica_groups=mesh['gx'=128,'sa'=8] {'gx'}, dimensions={0} | all-to-all | bytes 262144 | tf_op jit(solution)/shard_map/all_to_all | solution.py:376
  49.3 2.3 %middle.1 = (bf16[512,128]{1,0:T(8,128)(2,1)S(1)}, bf16[256,1024]{1,0:T(8,128)(2,1)}, bf16[256,1024]{1,0:T(8,128)(2,1)S(1)}) custom-call(bf16[512,128]{1,0:T(8,128)(2,1)S(1)} %bitcast.31, bf16[256,192]{1,0:T(8,128)(2,1)S(1)} %get-tuple-element.36.refs_1_, bf16[64,256]{1,0:T(8,128)(2,1)S(1)} %get-tuple-element.37.refs_2_, ...), custom_call_target="tpu_custom_call" | custom-call | tf_op jit(solution)/shard_map/middle/pallas_call | solution.py:361
  51.6 16.6 %all_to_all.22 = bf16[128,4,128]{2,1,0:T(4,128)(2,1)S(1)} all-to-all(bf16[128,4,128]{2,1,0:T(4,128)(2,1)S(1)} %bitcast.33), channel_id=1, replica_groups=mesh['gx'=128,'sa'=8] {'gx'}, dimensions={0} | all-to-all | bytes 262144 | tf_op jit(solution)/shard_map/all_to_all | solution.py:376
  68.2 2.0 %mix_backward.1 = (bf16[128,128]{1,0:T(8,128)(2,1)S(1)}, bf16[128,128]{1,0:T(8,128)(2,1)S(1)}, bf16[512,128]{1,0:T(8,128)(2,1)}) custom-call(s32[1]{0:T(128)} %bitcast.refs_0_, bf16[512,128]{1,0:T(8,128)(2,1)S(1)} %bitcast.28, bf16[256,512]{1,0:T(8,128)(2,1)S(1)} %get-tuple-element.33.refs_1_.refs_2_, ...), custom_call_target="tpu_custom_call" | custom-call | tf_op jit(solution)/shard_map/mix_backward/pallas_call | solution.py:361
  70.2 7.3 %collective-permute-start = (bf16[128,128]{1,0:T(8,128)(2,1)S(1)}, bf16[128,128]{1,0:T(8,128)(2,1)S(1)}, u32[]{:S(2)}, u32[]{:S(2)}) collective-permute-start(bf16[128,128]{1,0:T(8,128)(2,1)S(1)} %get-tuple-element.47), channel_id=1, source_target_pairs={{0,1},{1,0},{2,3},{3,2},{4,5},{5,4},{6,7},{7,6},{8,9},{9,8},{10,11... | collective-permute-start | bytes 98312 | tf_op jit(solution)/shard_map/ppermute | solution.py:391
  77.5 6.2 %all-to-all-start.3 = ((bf16[128,4,128]{2,1,0:T(4,128)(2,1)}), bf16[128,4,128]{2,1,0:T(4,128)(2,1)S(1)}, u32[]{:S(2)}, u32[]{:S(2)}) async-start(bf16[128,4,128]{2,1,0:T(4,128)(2,1)} %bitcast.12), calls=%async_computation.3 | async-start | bytes 262144 | tf_op jit(solution)/shard_map/all_to_all | solution.py:376
  83.7 0.0 collective-permute-done.taken
  83.7 6.8 %collective-permute-start.1 = (bf16[64,128]{1,0:T(8,128)(2,1)S(1)}, bf16[64,128]{1,0:T(8,128)(2,1)S(1)}, u32[]{:S(2)}, u32[]{:S(2)}) collective-permute-start(bf16[64,128]{1,0:T(8,128)(2,1)S(1)} %get-tuple-element.49), channel_id=1, source_target_pairs={{0,2},{1,3},{2,0},{3,1},{4,6},{5,7},{6,4},{7,5},{8,10},{9,11},{10,... | collective-permute-start | bytes 49160 | tf_op jit(solution)/shard_map/ppermute | solution.py:403
  90.5 11.6 %collective-permute-start.2 = (bf16[64,128]{1,0:T(8,128)(2,1)S(1)}, bf16[64,128]{1,0:T(8,128)(2,1)S(1)}, u32[]{:S(2)}, u32[]{:S(2)}) collective-permute-start(bf16[64,128]{1,0:T(8,128)(2,1)S(1)} %get-tuple-element.50), channel_id=1, source_target_pairs={{0,4},{1,5},{2,6},{3,7},{4,0},{5,1},{6,2},{7,3},{8,12},{9,13},{10,... | collective-permute-start | bytes 49160 | tf_op jit(solution)/shard_map/ppermute | solution.py:403
  102.0 1.9 %collective-permute-start.3 = (bf16[64,128]{1,0:T(8,128)(2,1)S(1)}, bf16[64,128]{1,0:T(8,128)(2,1)S(1)}, u32[]{:S(2)}, u32[]{:S(2)}) collective-permute-start(bf16[64,128]{1,0:T(8,128)(2,1)S(1)} %get-tuple-element.51), channel_id=1, source_target_pairs={{0,6},{1,7},{2,4},{3,5},{4,2},{5,3},{6,0},{7,1},{8,14},{9,15},{10,... | collective-permute-start | bytes 49160 | tf_op jit(solution)/shard_map/ppermute | solution.py:403
  104.0 0.0 all-to-all-done.3
  104.0 1.6 %last.1 = bf16[256,1024]{1,0:T(8,128)(2,1)} custom-call(bf16[512,128]{1,0:T(8,128)(2,1)S(1)} %bitcast.30, bf16[256,192]{1,0:T(8,128)(2,1)S(1)} %get-tuple-element.36.refs_1_, bf16[64,64]{1,0:T(8,128)(2,1)S(1)} %get-tuple-element.38.refs_3_.refs_2_, bf16[256,1024]{1,0:T(8,128)(2,1)S(1)} %get-tuple-element.53.refs_3_), custom_call_target="tpu_custom_call" | custom-call | tf_op jit(solution)/shard_map/last/pallas_call | solution.py:361
  105.6 0.0 collective-permute-done.1
  105.6 0.0 collective-permute-done.2
  105.6 3.0 %collective-permute-done.3 = bf16[64,128]{1,0:T(8,128)(2,1)S(1)} collective-permute-done((bf16[64,128]{1,0:T(8,128)(2,1)S(1)}, bf16[64,128]{1,0:T(8,128)(2,1)S(1)}, u32[]{:S(2)}, u32[]{:S(2)}) %collective-permute-start.3) | collective-permute-done | bytes 16416 | tf_op jit(solution)/shard_map/ppermute | solution.py:403
  108.7 0.1 reshape.71
  108.8 0.1 fusion.6
  108.9 0.1 maximum_bitcast_fusion
  109.0 1.1 convolution_bitcast_fusion
  (4 shorter events, 0.1 us)
Async XLA Ops:
  70.2 13.5 %collective-permute-start = (bf16[128,128]{1,0:T(8,128)(2,1)S(1)}, bf16[128,128]{1,0:T(8,128)(2,1)S(1)}, u32[]{:S(2)}, u32[]{:S(2)}) collective-permute-start(bf16[128,128]{1,0:T(8,128)(2,1)S(1)} %get-tuple-element.47), channel_id=1, source_target_pairs={{0,1},{1,0},{2,3},{3,2},{4,5},{5,4},{6,7},{7,6},{8,9},{9,8},{10,11... | collective-permute-start | bytes 98312 | tf_op jit(solution)/shard_map/ppermute | solution.py:391
  77.5 26.5 %all-to-all-start.3 = ((bf16[128,4,128]{2,1,0:T(4,128)(2,1)}), bf16[128,4,128]{2,1,0:T(4,128)(2,1)S(1)}, u32[]{:S(2)}, u32[]{:S(2)}) async-start(bf16[128,4,128]{2,1,0:T(4,128)(2,1)} %bitcast.12), calls=%async_computation.3 | async-start | bytes 262144 | tf_op jit(solution)/shard_map/all_to_all | solution.py:376
  83.7 21.9 %collective-permute-start.1 = (bf16[64,128]{1,0:T(8,128)(2,1)S(1)}, bf16[64,128]{1,0:T(8,128)(2,1)S(1)}, u32[]{:S(2)}, u32[]{:S(2)}) collective-permute-start(bf16[64,128]{1,0:T(8,128)(2,1)S(1)} %get-tuple-element.49), channel_id=1, source_target_pairs={{0,2},{1,3},{2,0},{3,1},{4,6},{5,7},{6,4},{7,5},{8,10},{9,11},{10,... | collective-permute-start | bytes 49160 | tf_op jit(solution)/shard_map/ppermute | solution.py:403
  90.5 15.1 %collective-permute-start.2 = (bf16[64,128]{1,0:T(8,128)(2,1)S(1)}, bf16[64,128]{1,0:T(8,128)(2,1)S(1)}, u32[]{:S(2)}, u32[]{:S(2)}) collective-permute-start(bf16[64,128]{1,0:T(8,128)(2,1)S(1)} %get-tuple-element.50), channel_id=1, source_target_pairs={{0,4},{1,5},{2,6},{3,7},{4,0},{5,1},{6,2},{7,3},{8,12},{9,13},{10,... | collective-permute-start | bytes 49160 | tf_op jit(solution)/shard_map/ppermute | solution.py:403
  102.0 6.6 %collective-permute-start.3 = (bf16[64,128]{1,0:T(8,128)(2,1)S(1)}, bf16[64,128]{1,0:T(8,128)(2,1)S(1)}, u32[]{:S(2)}, u32[]{:S(2)}) collective-permute-start(bf16[64,128]{1,0:T(8,128)(2,1)S(1)} %get-tuple-element.51), channel_id=1, source_target_pairs={{0,6},{1,7},{2,4},{3,5},{4,2},{5,3},{6,0},{7,1},{8,14},{9,15},{10,... | collective-permute-start | bytes 49160 | tf_op jit(solution)/shard_map/ppermute | solution.py:403
